TPU v7x, 512 devices: a whole 4x8x8 slice. The times are simulated.
512 devices in a mesh: depth: 16 (over x, z_hi), plane: 32 (over z_lo, y, core).
Axes of the slice: x: 4, y: 8, z: 8 (z_hi: 4, z_lo: 2; z = z_hi * 2 + z_lo), core: 2. Of those that a mesh axis runs over, the one named last changes fastest.
Arguments:
- volume: bfloat16 [64, 128, 128], P('depth', 'plane'), may hold values from -6 to 6
- cotangent: float32 [64, 128, 128], P('depth', 'plane'), may hold values from -6 to 6
- kernel_in: bfloat16 [27, 32], replicated, may hold values from -1.25 to 1.25
- kernel_mid: bfloat16 [27, 32, 32], replicated, may hold values from -0.21875 to 0.21875
- kernel_out: bfloat16 [27, 32], replicated, may hold values from -0.21875 to 0.21875
- measured: float32 [64, 32, 1024], P('depth'), may hold values from -24 to 24
- angle_ids: int32 [8], replicated, may hold values from 0 to 31, as said below
- ray_bins: int32 [8, 128, 128], P(None, 'plane'), may hold values from 0 to 1023, as said below
Outputs:
- grad_volume: float32 [64, 128, 128], P('depth', 'plane')
- grad_kernel_in: float32 [27, 32], replicated
- grad_kernel_mid: float32 [27, 32, 32], replicated
- grad_kernel_out: float32 [27, 32], replicated
Inputs may be any that keep to these rules, and one draw needn't show every extreme that they name: `angle_ids`: each entry names a measured view; the entries are distinct. `ray_bins`: for each view a, the bins follow parallel-beam geometry: a cell's bin is the detector position of its centre projected along the direction of view angle_ids[a], clipped at the detector's ends.
All inputs are finite; a program needn't handle non-finite values.
Results may differ from a plain program's by a relative error of at most 0.0051.
Values may be sent and summed in bfloat16 or wider, within the bound.
No kernel may reach another device: no remote copies, remote signals or barrier semaphores. Data moves between devices by JAX's collectives and lax.ppermute only.
A program may use at most 64 MiB of HBM per device.

v0:
```python
import jax
import jax.numpy as jnp
from jax import lax
from jax.sharding import PartitionSpec as P

BINS = 1024
ANG = 8


delta_scale = 6.0


def extended(cells, sides, width):
    for axis, dim in sides:
        count = lax.axis_size(axis)
        ends = count - 1
        head = lax.slice_in_dim(cells, 0, width, axis=dim)
        tail = lax.slice_in_dim(cells, cells.shape[dim] - width, cells.shape[dim], axis=dim)
        cells = jnp.concatenate(
            [
                lax.ppermute(tail, axis, [(i, (i + 1) % count) for i in range(ends)]),
                cells,
                lax.ppermute(head, axis, [((i + 1) % count, i) for i in range(ends)]),
            ],
            axis=dim,
        )
    return cells


def shifts():
    return [
        (step_z, step_y, step_x)
        for step_z in (-1, 0, 1)
        for step_y in (-1, 0, 1)
        for step_x in (-1, 0, 1)
    ]


def pad_row(field):
    return jnp.pad(field, ((0, 0), (0, 0), (0, 0), (1, 1)))


def extend(field):
    padded = extended(field, (("depth", 1), ("plane", 2)), 1)
    return pad_row(padded)


def window_at(padded, start_z, start_y, start_x, extent):
    return lax.slice(
        padded,
        (0, start_z, start_y, start_x),
        (padded.shape[0], start_z + extent[0], start_y + extent[1], start_x + extent[2]),
    )


def forward_conv(padded, kernel, extent, base):
    summed = jnp.zeros((kernel.shape[1],) + tuple(extent), jnp.float32)
    for position, (step_z, step_y, step_x) in enumerate(shifts()):
        window = window_at(padded, base[0] + step_z, base[1] + step_y, base[2] + step_x, extent)
        summed = summed + jnp.einsum(
            "oc,czhw->ozhw", kernel[position], window, preferred_element_type=jnp.float32
        )
    return summed


def adjoint_conv(padded, kernel, extent, base):
    summed = jnp.zeros((kernel.shape[2],) + tuple(extent), jnp.float32)
    for position, (step_z, step_y, step_x) in enumerate(shifts()):
        window = window_at(padded, base[0] - step_z, base[1] - step_y, base[2] - step_x, extent)
        summed = summed + jnp.einsum(
            "oc,ozhw->czhw", kernel[position], window, preferred_element_type=jnp.float32
        )
    return summed


def kernel_grad(grad_out, padded_in, extent, base):
    pieces = []
    for position, (step_z, step_y, step_x) in enumerate(shifts()):
        window = window_at(padded_in, base[0] + step_z, base[1] + step_y, base[2] + step_x, extent)
        pieces.append(
            jnp.einsum("ozhw,czhw->oc", grad_out, window, preferred_element_type=jnp.float32)
        )
    return jnp.stack(pieces)


def silu_slope(value):
    sigma = jax.nn.sigmoid(value)
    return sigma * (1.0 + value * (1.0 - sigma))


def project_pair(first, second, ray_bins):
    slices = first.shape[0]
    flattened = jnp.concatenate((first.reshape(slices, -1), second.reshape(slices, -1)), axis=0).T

    def one_view(bins_view):
        return jax.ops.segment_sum(flattened, bins_view.reshape(-1), num_segments=BINS)

    per_view = lax.map(one_view, ray_bins)
    stacked = jnp.transpose(per_view, (2, 0, 1))
    return (stacked[:slices], stacked[slices:])


def back_project(rays, ray_bins):

    def accumulate(summed, view_pair):
        rays_view, bins_view = view_pair
        return (summed + jnp.take(rays_view, bins_view.reshape(-1), axis=1), None)

    initial = jnp.zeros((rays.shape[0], ray_bins.shape[1] * ray_bins.shape[2]), rays.dtype)
    summed = lax.scan(accumulate, initial, (jnp.transpose(rays, (1, 0, 2)), ray_bins))[0]
    return summed.reshape(rays.shape[0], ray_bins.shape[1], ray_bins.shape[2])


def curvature(residual):
    ratio = residual / delta_scale
    inner = 1.0 + ratio * ratio
    return 1.0 / (inner * jnp.sqrt(inner))


def per_device(volume, cotangent, kernel_in, kernel_mid, kernel_out, measured, angle_ids, ray_bins):
    extent = volume.shape
    depth_rows, plane_rows, cells = extent
    first_in = kernel_in[:, :, None]
    last_out = kernel_out[:, None, :]
    source_pad = extend(volume[None])
    first_raw = forward_conv(source_pad, first_in, extent, (1, 1, 1))
    act_first = jax.nn.silu(first_raw).astype(jnp.bfloat16)
    slope_first = silu_slope(first_raw)
    first_pad = extend(act_first)
    second_raw = forward_conv(first_pad, kernel_mid, extent, (1, 1, 1))
    act_second = jax.nn.silu(second_raw).astype(jnp.bfloat16)
    slope_second = silu_slope(second_raw)
    second_pad = extend(act_second)
    residue = forward_conv(second_pad, last_out, extent, (1, 1, 1))[0]
    source_margin, first_margin, second_margin = (1, 1, 1)
    mid_margin, low_margin = (0, 0)
    denoised = volume.astype(jnp.float32) - residue
    chosen = jnp.take(measured, angle_ids, axis=1)
    local_rays, local_cot = project_pair(denoised, cotangent, ray_bins)
    forward_rays, cot_rays = lax.psum((local_rays, local_cot), "plane")
    weighted = curvature(forward_rays - chosen) * cot_rays
    grad_denoised = cotangent - 0.25 / ANG * back_project(weighted, ray_bins)
    cell_count = depth_rows * lax.axis_size("depth") * plane_rows * lax.axis_size("plane") * cells
    grad_scale = float(cell_count) ** (-0.5)
    grad_last = (-grad_denoised).astype(jnp.bfloat16)
    last_pad = extend(grad_last[None])
    mid_extent = (depth_rows + 2 * mid_margin, plane_rows + 2 * mid_margin, cells)
    low_extent = (depth_rows + 2 * low_margin, plane_rows + 2 * low_margin, cells)
    term_out = kernel_grad(grad_last[None], second_pad, extent, (second_margin, second_margin, 1))[
        :, 0, :
    ]
    grad_second = adjoint_conv(last_pad, last_out, mid_extent, (1, 1, 1))
    grad_mid = (grad_second * slope_second).astype(jnp.bfloat16)
    term_mid = kernel_grad(grad_mid, first_pad, extent, (first_margin, first_margin, 1))
    mid_pad = extend(grad_mid)
    grad_first = adjoint_conv(mid_pad, kernel_mid, low_extent, (1, 1, 1))
    grad_low = (grad_first * slope_first).astype(jnp.bfloat16)
    term_in = kernel_grad(grad_low, source_pad, extent, (source_margin, source_margin, 1))[:, :, 0]
    term_in, term_mid, term_out = lax.psum((term_in, term_mid, term_out), ("depth", "plane"))
    low_pad = extend(grad_low)
    grad_volume = grad_denoised + adjoint_conv(low_pad, first_in, extent, (1, 1, 1))[0]
    return (grad_volume, term_in * grad_scale, term_mid * grad_scale, term_out * grad_scale)


def solution(mesh):
    placed = (
        P("depth", "plane", None),
        P("depth", "plane", None),
        P(),
        P(),
        P(),
        P("depth", None, None),
        P(),
        P(None, "plane", None),
    )
    return jax.shard_map(
        per_device,
        mesh=mesh,
        in_specs=placed,
        out_specs=(P("depth", "plane", None), P(), P(), P()),
        check_vma=False,
    )
```

profile of v0, /device:TPU:1, one launch (start us, length us, event | category | flops | bytes accessed | tf_op | source)
XLA Modules:
  0.0 825.1 jit_solution(6284097332181020481)
XLA Ops:
  8.0 6.6 collective-permute-start
  14.6 1.3 collective-permute-start.1
  17.8 1.6 bitcast_convert_fusion.52
  19.5 1.5 bitcast_convert_fusion.51
  24.3 4.0 collective-permute-start.2
  28.3 1.9 collective-permute-start.3
  30.3 1.4 fusion.427
  31.6 1.6 collective-permute-done.3
  36.9 7.6 collective-permute-start.4
  46.7 4.9 collective-permute-done.5
  51.6 3.2 collective-permute-start.6
  54.8 2.1 collective-permute-start.7
  56.9 3.4 collective-permute-done.7
  62.9 1.8 fusion.700
  69.6 5.8 collective-permute-start.8
  75.4 1.3 collective-permute-start.9
  76.8 4.1 collective-permute-done.9
  81.0 3.3 collective-permute-start.10
  84.3 1.9 collective-permute-start.11
  87.2 2.5 collective-permute-done.11
  94.1 1.8 fusion.701
  96.8 36.2 %while.21 = (s32[]{:T(128)}, f32[8,1024,8]{1,0,2:T(8,128)S(1)}, s32[8,4,128]{2,1,0:T(4,128)}, f32[512,8]{1,0:T(8,128)}, s32[]{:T(128)}, /*index=5*/f32[]{:T(128)}, s32[]{:T(128)}) while((s32[]{:T(128)}, f32[8,1024,8]{1,0,2:T(8,128)S(1)}, s32[8,4,128]{2,1,0:T(4,128)}, f32[512,8]{1,0:T(8,128)}, s32[]{:T(128)}, /*index=5*/f32[]{:T(128)}, ...), condition=%wide.region_2.3_spmd, body=%wide.region_0.2_spmd.sunk | while | flops 4098 | bytes 168533 | solution.py:98
  97.5 3.3 scatter_custom_fusion.5
  101.8 3.5 scatter_custom_fusion.5
  106.4 3.2 scatter_custom_fusion.5
  110.5 4.1 scatter_custom_fusion.5
  115.7 3.6 scatter_custom_fusion.5
  120.3 3.3 scatter_custom_fusion.5
  124.7 3.5 scatter_custom_fusion.5
  129.3 3.4 scatter_custom_fusion.5
  135.3 224.8 %all-reduce.13.cloned.1.call-done = (f32[4,8,1024]{2,1,0:T(8,128)}, f32[4,8,1024]{2,1,0:T(8,128)}) async-done(((f32[4,8,1024]{2,1,0:T(8,128)}, f32[4,8,1024]{2,1,0:T(8,128)}), (f32[4,8,1024]{2,1,0:T(8,128)}, f32[4,8,1024]{2,1,0:T(8,128)})) %all-reduce.13.cloned.1.call-update) | async-done | bytes 262160 | tf_op jit(solution)/shard_map/psum | solution.py:140
  361.2 17.5 %while.22 = (s32[]{:T(128)}, f32[4,512]{0,1:T(8,128)S(1)}, s32[8,4,128]{2,1,0:T(4,128)}, f32[8,4,1024]{2,0,1:T(8,128)S(1)}, s32[]{:T(128)}, /*index=5*/s32[]{:T(128)}) while((s32[]{:T(128)}, f32[4,512]{0,1:T(8,128)S(1)}, s32[8,4,128]{2,1,0:T(4,128)}, f32[8,4,1024]{2,0,1:T(8,128)S(1)}, s32[]{:T(128)}, /*index=5*/s32[]{:T(128)}) %tuple.247), condition=%wide.region_6.7_spmd.clone, body=%wide.region_5.6_spmd.clone.sunk | while | flops 11779 | bytes 123991 | solution.py:110
  379.0 4.5 collective-permute-start.12
  383.5 1.5 collective-permute-start.13
  389.7 1.9 collective-permute-start.14
  391.6 3.0 collective-permute-start.15
  394.6 1.9 collective-permute-done.15
  404.1 5.5 collective-permute-start.16
  412.5 3.9 collective-permute-done.17
  416.4 2.2 collective-permute-start.19
  418.6 3.4 collective-permute-start.18
  422.2 265.8 %all-reduce.11.cloned.1.call-done = f32[27,32,32]{2,1,0:T(8,128)} async-done(((f32[27,32,32]{2,1,0:T(8,128)}), f32[27,32,32]{2,1,0:T(8,128)}) %all-reduce.11.cloned.1.call-update) | async-done | bytes 110608 | tf_op jit(solution)/shard_map/psum | solution.py:159
  688.0 1.8 broadcast_multiply_fusion
  701.2 94.7 %all-reduce.6 = (f32[27,32]{1,0:T(8,128)S(1)}, f32[27,32]{1,0:T(8,128)S(1)}) all-reduce(f32[27,32]{1,0:T(8,128)S(1)} %bitcast.2037, f32[27,32]{1,0:T(8,128)S(1)} %bitcast.2036), channel_id=1, replica_groups=mesh['depth'=16,'plane'=32] {'depth','plane'}, use_global_device_ids=true, to_apply=%region_7.8 | all-reduce | flops 1728 | bytes 13824 | tf_op jit(solution)/shard_map/psum | solution.py:159
  796.5 4.0 collective-permute-start.20
  802.4 3.7 collective-permute-done.21
  806.1 4.0 collective-permute-start.23
  810.1 2.0 collective-permute-start.22
  (550 shorter events, 88.4 us)
Async XLA Ops:
  7.2 38.8 %copy-start = (f32[4,32,1024]{2,1,0:T(8,128)S(1)}, f32[4,32,1024]{2,1,0:T(8,128)}, u32[]{:S(2)}) copy-start(f32[4,32,1024]{2,1,0:T(8,128)} %param.17) | copy-start | bytes 1572868
  7.2 352.9 %all-reduce.13.cloned.1.call-start = ((), (), s32[]{:S(2)}) async-start(), calls=%async_computation.1 | async-start | bytes 524288 | tf_op jit(solution)/shard_map/psum | solution.py:140
  8.0 15.6 %collective-permute-start = (bf16[1,1,4,128]{3,2,1,0:T(4,128)(2,1)S(1)}, bf16[1,1,4,128]{3,2,1,0:T(4,128)(2,1)S(1)}, u32[]{:S(2)}, u32[]{:S(2)}) collective-permute-start(bf16[1,1,4,128]{3,2,1,0:T(4,128)(2,1)S(1)} %get-tuple-element.323), channel_id=1, source_target_pairs={{0,32},{32,64},{64,96},{96,128},{128,160},{160,192},{192,224},{224... | collective-permute-start | bytes 3080 | tf_op jit(solution)/shard_map/ppermute | solution.py:21
  14.6 9.0 %collective-permute-start.1 = (bf16[1,1,4,128]{3,2,1,0:T(4,128)(2,1)S(1)}, bf16[1,1,4,128]{3,2,1,0:T(4,128)(2,1)S(1)}, u32[]{:S(2)}, u32[]{:S(2)}) collective-permute-start(bf16[1,1,4,128]{3,2,1,0:T(4,128)(2,1)S(1)} %get-tuple-element.324), channel_id=1, source_target_pairs={{32,0},{64,32},{96,64},{128,96},{160,128},{192,160},{224,192},{256... | collective-permute-start | bytes 3080 | tf_op jit(solution)/shard_map/ppermute | solution.py:23
  24.3 7.4 collective-permute-start.2
  28.3 4.9 collective-permute-start.3
  34.7 11.2 %copy-start.52 = (f32[4,4,128]{2,1,0:T(4,128)S(1)}, f32[4,4,128]{2,1,0:T(4,128)}, u32[]{:S(2)}) copy-start(f32[4,4,128]{2,1,0:T(4,128)} %param.13) | copy-start | bytes 24580
  36.9 9.8 %collective-permute-start.4 = (bf16[32,1,4,128]{3,0,2,1:T(8,128)(2,1)S(1)}, bf16[32,1,4,128]{3,0,2,1:T(8,128)(2,1)S(1)}, u32[]{:S(2)}, u32[]{:S(2)}) collective-permute-start(bf16[32,1,4,128]{3,0,2,1:T(8,128)(2,1)S(1)} %get-tuple-element.175), channel_id=1, source_target_pairs={{0,32},{32,64},{64,96},{96,128},{128,160},{160,192},{192,224},{224... | collective-permute-start | bytes 98312 | tf_op jit(solution)/shard_map/ppermute | solution.py:21
  44.6 7.1 collective-permute-start.5
  51.6 5.3 collective-permute-start.6
  54.8 5.5 collective-permute-start.7
  69.6 7.2 collective-permute-start.8
  75.4 5.6 collective-permute-start.9
  81.0 6.3 collective-permute-start.10
  84.3 5.4 collective-permute-start.11
  133.8 554.2 %all-reduce.11.cloned.1.call-start = ((), (), s32[]{:S(2)}) async-start(), calls=%async_computation | async-start | bytes 884736 | tf_op jit(solution)/shard_map/psum | solution.py:159
  134.5 225.6 %copy-start.96 = (pred[8]{0:T(512)(128)(4,1)S(1)}, pred[8]{0:T(512)(128)(4,1)}, u32[]{:S(2)}) copy-start(pred[8]{0:T(512)(128)(4,1)} %compare_and_fusion.1) | copy-start | bytes 28
  379.0 10.6 %collective-permute-start.12 = (bf16[1,1,4,128]{3,2,1,0:T(4,128)(2,1)S(1)}, bf16[1,1,4,128]{3,2,1,0:T(4,128)(2,1)S(1)}, u32[]{:S(2)}, u32[]{:S(2)}) collective-permute-start(bf16[1,1,4,128]{3,2,1,0:T(4,128)(2,1)S(1)} %get-tuple-element.321), channel_id=1, source_target_pairs={{0,32},{32,64},{64,96},{96,128},{128,160},{160,192},{192,224},{224... | collective-permute-start | bytes 3080 | tf_op jit(solution)/shard_map/ppermute | solution.py:21
  383.5 6.1 collective-permute-start.13
  388.6 8.2 copy-start.71
  388.6 8.2 copy-start.72
  388.7 8.2 copy-start.73
  388.7 8.2 copy-start.74
  388.7 8.2 copy-start.75
  388.7 8.2 copy-start.76
  388.7 8.2 copy-start.77
  388.7 8.2 copy-start.78
  388.7 8.2 copy-start.79
  388.7 8.2 copy-start.80
  388.7 8.2 copy-start.81
  388.7 8.2 copy-start.82
  388.8 8.2 copy-start.83
  388.8 8.2 copy-start.84
  388.8 8.2 copy-start.85
  388.8 8.2 copy-start.86
  388.8 8.2 copy-start.87
  388.8 8.2 copy-start.88
  388.8 8.2 copy-start.89
  389.7 4.9 collective-permute-start.14
  391.6 4.9 collective-permute-start.15
  404.1 8.3 %collective-permute-start.16 = (bf16[32,1,4,128]{3,0,2,1:T(8,128)(2,1)S(1)}, bf16[32,1,4,128]{3,0,2,1:T(8,128)(2,1)S(1)}, u32[]{:S(2)}, u32[]{:S(2)}) collective-permute-start(bf16[32,1,4,128]{3,0,2,1:T(8,128)(2,1)S(1)} %get-tuple-element.169), channel_id=1, source_target_pairs={{0,32},{32,64},{64,96},{96,128},{128,160},{160,192},{192,224},{224... | collective-permute-start | bytes 98312 | tf_op jit(solution)/shard_map/ppermute | solution.py:21
  409.7 6.7 collective-permute-start.17
  416.4 273.4 %collective-permute-start.19 = (bf16[32,6,1,128]{3,0,2,1:T(8,128)(2,1)S(1)}, bf16[32,6,1,128]{3,0,2,1:T(8,128)(2,1)S(1)}, u32[]{:S(2)}, u32[]{:S(2)}) collective-permute-start(bf16[32,6,1,128]{3,0,2,1:T(8,128)(2,1)S(1)} %get-tuple-element.156), channel_id=1, source_target_pairs={{1,0},{2,1},{3,2},{4,3},{5,4},{6,5},{7,6},{8,7},{9,8},{10,9},{11,1... | collective-permute-start | bytes 147464 | tf_op jit(solution)/shard_map/ppermute | solution.py:23
  418.6 271.2 %collective-permute-start.18 = (bf16[32,6,1,128]{3,0,2,1:T(8,128)(2,1)S(1)}, bf16[32,6,1,128]{3,0,2,1:T(8,128)(2,1)S(1)}, u32[]{:S(2)}, u32[]{:S(2)}) collective-permute-start(bf16[32,6,1,128]{3,0,2,1:T(8,128)(2,1)S(1)} %get-tuple-element.155), channel_id=1, source_target_pairs={{0,1},{1,2},{2,3},{3,4},{4,5},{5,6},{6,7},{7,8},{8,9},{9,10},{10,1... | collective-permute-start | bytes 147464 | tf_op jit(solution)/shard_map/ppermute | solution.py:21
  796.5 5.9 collective-permute-start.20
  800.5 5.6 collective-permute-start.21
  806.1 6.2 collective-permute-start.23
  810.1 3.2 collective-permute-start.22
  (75 other events, 204.6 us)
Sparse Core Ops, SparseCore 0:
  133.9 226.1 all-reduce.12
  412.6 275.3 all-reduce.10
where the time goes:
time: 829 us; the launch traced here: 825 us
  waiting for transfers between devices  518 us (62%)
  blocking collectives  94.7 us (11%)
  starting transfers between devices  74.9 us (9%)
  other arithmetic  56.2 us (7%)
  matrix products  32.7 us (4%)
  local copies, waits for them, and re-layouts  32.5 us (4%)
  between operations  15.8 us (2%)
    psum x1, waiting for transfers between devices, per_device(): lax.psum((term_in, term_mid, term_out), ('depth', 'plane'))  266 us
    psum x1, waiting for transfers between devices, per_device(): forward_rays, cot_rays = lax.psum((local_rays, local_cot), 'plane')  225 us
    psum x1, blocking collectives, per_device(): lax.psum((term_in, term_mid, term_out), ('depth', 'plane'))  94.7 us
    ppermute x12, starting transfers between devices, extended(): lax.ppermute(tail, axis, [(i, (i + 1) % count) for i in range(ends)])  51.8 us
    scatter-add x8, other arithmetic, one_view(): jax.ops.segment_sum(flattened, bins_view.reshape(-1), num_segments=BINS)  27.9 us
    ppermute x12, waiting for transfers between devices, extended(): lax.ppermute(head, axis, [((i + 1) % count, i) for i in range(ends)])  26.1 us
    ppermute x12, starting transfers between devices, extended(): lax.ppermute(head, axis, [((i + 1) % count, i) for i in range(ends)])  22.9 us
  transfers between devices with their start and end apart: 26, of which 11 were waited for; matrix products, arithmetic and copies ran while one was open for 2% of the time, Pallas kernels for 0%

commit v1 on v0

v1 whole, which is shorter than its diff:
```python
import functools

import jax
import jax.numpy as jnp
from jax import lax
from jax.experimental import pallas as pl
from jax.experimental.pallas import tpu as pltpu
from jax.sharding import PartitionSpec as P

BINS = 1024
ANG = 8
C = 32
W = 128
Z = 4
H = 4
HI = BINS // 128
TILES = ANG * Z

delta_scale = 6.0
F32 = jnp.float32
BF16 = jnp.bfloat16


def lanes_of(shape):
    return lax.broadcasted_iota(jnp.int32, shape, len(shape) - 1)


def from_left(x):
    lane = lanes_of(x.shape)
    return jnp.where(lane > 0, pltpu.roll(x, 1, x.ndim - 1), 0.0)


def from_right(x):
    lane = lanes_of(x.shape)
    return jnp.where(lane < W - 1, pltpu.roll(x, W - 1, x.ndim - 1), 0.0)


def dot(a, b):
    return jnp.dot(a, b, preferred_element_type=F32)


def dot_nt(a, b):
    return lax.dot_general(a, b, (((1,), (1,)), ((), ())), preferred_element_type=F32)


def row_ok(rows, first, count):
    at = lax.broadcasted_iota(jnp.int32, (rows, W), 0) // C + first
    return (at >= 0) & (at < count)


def banded(base, height, shift):
    rows = [pltpu.roll(base, h + shift, 1) if h + shift else base for h in range(height)]
    return jnp.concatenate(rows, axis=0)[:, :144].astype(BF16)


def triple(ref, z, start, size):
    return jnp.concatenate([ref[z + oz, start : start + size, :] for oz in range(3)], axis=0)


def three_shifts(ref, flat, count):
    shape = (count, 16, W)
    ref[:, 0:16, :] = from_left(flat).reshape(shape).astype(BF16)
    ref[:, 16:32, :] = flat.reshape(shape).astype(BF16)
    ref[:, 32:48, :] = from_right(flat).reshape(shape).astype(BF16)


def low_match(low_row):
    n = low_row.shape[1]
    at = lax.broadcasted_iota(jnp.int32, (128, n), 0)
    return jnp.where(low_row == at, 1.0, 0.0).astype(BF16)


def conv_mid(ref, weights, z, row):
    x = triple(ref, z, row * C, 3 * C)
    y = dot(weights, x)
    return y[C : 2 * C] + from_left(y[0:C]) + from_right(y[2 * C :])


def conv_last(ref, weights, z, row):
    y = dot(weights, triple(ref, z, row * C, 3 * C))
    return y[1:2] + from_left(y[0:1]) + from_right(y[2:3])


def project(field, bins_ref, a):
    parts, lows = [], []
    at = lax.broadcasted_iota(jnp.int32, (HI, W), 0)
    for h in range(H):
        bins = bins_ref[a, h : h + 1, :]
        match = (bins >> 7) == at
        rows = [jnp.where(match, field[h][r : r + 1, :], 0.0) for r in range(field[h].shape[0])]
        parts.append(jnp.concatenate(rows, axis=0))
        lows.append(low_match(bins & 127))
    part = jnp.concatenate(parts, axis=1)
    low = jnp.concatenate(lows, axis=1)
    head = part.astype(BF16)
    rest = (part - head.astype(F32)).astype(BF16)
    n = part.shape[0]
    both = dot_nt(jnp.concatenate([head, rest], axis=0), low)
    return both[:n] + both[n:]


def forward_kernel(depth_count, plane_count, pos, lo, mid, hi, first, second, third, cot, bins,
                   vc_out, act1_out, slope1_out, act2_out, slope2_out, rays_out,
                   vs, v3, vcs, a1, a2):
    depth_at = pos[0] * Z
    plane_at = pos[1] * H
    nz, nh = depth_count * Z, plane_count * H
    vs[...] = jnp.zeros_like(vs)
    vs[:, 0:4, :] = lo[...].astype(F32)
    vs[:, 4:8, :] = mid[...].astype(F32)
    vs[:, 8:12, :] = hi[...].astype(F32)
    three_shifts(v3, vs[...].reshape(12 * 16, W), 12)
    vcs[...] = jnp.zeros_like(vcs)
    for z in range(Z):
        for h in range(H):
            for oz in range(3):
                vcs[z * H + h, oz * 3 : oz * 3 + 3, :] = vs[z + 3 + oz, h + 3 : h + 6, :]
    vc_out[...] = vcs[...].astype(BF16)
    weights = banded(first[...], 10, 0)
    ok_rows = row_ok(10 * C, plane_at - 3, nh)
    for z in range(10):
        p = dot(weights, v3[z : z + 3].reshape(144, W))
        sigma = jax.nn.sigmoid(p)
        at = depth_at + (z - 3)
        ok = ok_rows & (at >= 0) & (at < nz)
        act = jnp.where(ok, p * sigma, 0.0).astype(BF16)
        a1[z] = act
        if 2 <= z < 8:
            act1_out[z - 2] = act[2 * C : 8 * C]
            slope1_out[z - 2] = (sigma * (1.0 + p * (1.0 - sigma)))[2 * C : 8 * C]
    wide = second[...]
    ok_rows = row_ok(8 * C, plane_at - 2, nh)
    for z in range(8):
        p = jnp.concatenate([conv_mid(a1, wide, z, h) for h in range(8)], axis=0)
        sigma = jax.nn.sigmoid(p)
        at = depth_at + (z - 2)
        ok = ok_rows & (at >= 0) & (at < nz)
        act = jnp.where(ok, p * sigma, 0.0).astype(BF16)
        slope2_out[z] = sigma * (1.0 + p * (1.0 - sigma))
        if 1 <= z < 7:
            a2[z - 1] = act[C : 7 * C]
            act2_out[z - 1] = act[C : 7 * C]
    last = third[...]
    field = []
    for h in range(H):
        rows = []
        for z in range(Z):
            rows.append(vs[z + 4, h + 4 : h + 5, :] - conv_last(a2, last, z, h))
        for z in range(Z):
            rows.append(cot[z, h : h + 1, :])
        field.append(jnp.concatenate(rows, axis=0))
    for a in range(ANG):
        tile = project(field, bins, a).reshape(2, Z, HI, 128)
        rays_out[a * Z : (a + 1) * Z, 0:HI, :] = tile[0]
        rays_out[a * Z : (a + 1) * Z, HI : 2 * HI, :] = tile[1]


def weigh_kernel(planes, rays, chosen, out):
    each = TILES // planes
    total = jnp.sum(rays[...], axis=0)
    for t in range(each):
        forward = total[t * 2 * HI : t * 2 * HI + HI]
        turned = total[t * 2 * HI + HI : (t + 1) * 2 * HI]
        ratio = (forward - chosen[t]) / delta_scale
        inner = 1.0 + ratio * ratio
        weighted = turned / (inner * jnp.sqrt(inner))
        out[:, t * HI : (t + 1) * HI, :] = jnp.broadcast_to(weighted[None], (planes, HI, 128))


def back_kernel(plane_count, pos, rays, bins_lo, bins_mid, bins_hi, cot_lo, cot_mid, cot_hi,
                slab_out, own_out, slab):
    plane_at = pos[1] * H
    nh = plane_count * H
    pieces = (bins_lo, bins_mid, bins_hi)
    cots = (cot_lo, cot_mid, cot_hi)
    at = lax.broadcasted_iota(jnp.int32, (HI, W), 0)
    spans = range(1, 11)
    total = [None] * len(spans)
    for a in range(ANG):
        rows = rays[a * Z : (a + 1) * Z].reshape(Z * HI, 128)
        head = rows.astype(BF16)
        rest = (rows - head.astype(F32)).astype(BF16)
        both = jnp.concatenate([head, rest], axis=0)
        bins = [pieces[h // H][a, h % H : h % H + 1, :] for h in spans]
        low = jnp.concatenate([low_match(b & 127) for b in bins], axis=1)
        spread = dot(both, low)
        spread = spread[: Z * HI] + spread[Z * HI :]
        for i, b in enumerate(bins):
            match = (b >> 7) == at
            match = jnp.concatenate([match] * Z, axis=0)
            term = jnp.where(match, spread[:, i * W : (i + 1) * W], 0.0)
            total[i] = term if total[i] is None else total[i] + term
    slab[...] = jnp.zeros_like(slab)
    for i, h in enumerate(spans):
        summed = jnp.sum(total[i].reshape(Z, HI, W), axis=1)
        field = cots[h // H][:, h % H, :] - (0.25 / ANG) * summed
        row = plane_at + h - H
        slab[h] = jnp.where((row >= 0) & (row < nh), -field, 0.0)
        if H <= h < 2 * H:
            own_out[h - H] = field
    slab_out[...] = slab[...].astype(BF16)


def backward_kernel(depth_count, plane_count, pos, lo, mid, hi, own, first, second, third,
                    vc, act1, slope1, act2, slope2,
                    volume_out, mid_out, out_out, in_out,
                    gs, v3, gx, gm, gm3, low, low3):
    depth_at = pos[0] * Z
    plane_at = pos[1] * H
    nz, nh = depth_count * Z, plane_count * H
    gs[...] = jnp.zeros_like(gs)
    for h in range(12):
        gs[0:3, h, :] = lo[h].astype(F32)[1:4]
        gs[3:7, h, :] = mid[h].astype(F32)
        gs[7:10, h, :] = hi[h].astype(F32)[0:3]
    three_shifts(v3, gs[...].reshape(160, W), 10)
    gx[...] = jnp.zeros_like(gx)
    rows = gs[3:7, 4:8, :].reshape(16, W)
    gx[:, 0, :] = from_right(rows)
    gx[:, 1, :] = rows
    gx[:, 2, :] = from_left(rows)
    weights = banded(third[...], 8, 1)
    ok_rows = row_ok(8 * C, plane_at - 2, nh)
    for z in range(8):
        y = dot(weights, v3[z : z + 3].reshape(144, W))
        at = depth_at + (z - 2)
        ok = ok_rows & (at >= 0) & (at < nz)
        g = jnp.where(ok, y * slope2[z], 0.0).astype(BF16)
        gm[z] = g
        if 2 <= z < 6:
            inner = g[2 * C : 6 * C].astype(F32)
            gm3[z - 2, 0] = from_right(inner).astype(BF16)
            gm3[z - 2, 1] = g[2 * C : 6 * C]
            gm3[z - 2, 2] = from_left(inner).astype(BF16)

    def shifted(ref):
        return jnp.concatenate(
            [
                jnp.concatenate([ref[z, ox, h * C : (h + 1) * C, :] for ox in range(3)], axis=0)
                for z in range(Z)
                for h in range(H)
            ],
            axis=1,
        )

    def windows(ref):
        return jnp.concatenate(
            [triple(ref, z, h * C, 3 * C) for z in range(Z) for h in range(H)], axis=1
        )

    mid_out[...] = dot_nt(shifted(gm3), windows(act1))
    gx_all = jnp.concatenate([gx[i] for i in range(16)], axis=1).astype(BF16)
    out_out[...] = dot_nt(gx_all, windows(act2))
    wide = second[...]
    ok_rows = row_ok(6 * C, plane_at - 1, nh)
    for z in range(6):
        y = jnp.concatenate([conv_mid(gm, wide, z, h) for h in range(6)], axis=0)
        at = depth_at + (z - 1)
        ok = ok_rows & (at >= 0) & (at < nz)
        g = jnp.where(ok, y * slope1[z], 0.0).astype(BF16)
        low[z] = g
        if 1 <= z < 5:
            inner = g[C : 5 * C].astype(F32)
            low3[z - 1, 0] = from_right(inner).astype(BF16)
            low3[z - 1, 1] = g[C : 5 * C]
            low3[z - 1, 2] = from_left(inner).astype(BF16)
    vc_all = jnp.concatenate([vc[i] for i in range(16)], axis=1)
    in_out[...] = dot_nt(vc_all, shifted(low3))
    last = first[...]
    for z in range(Z):
        for h in range(H):
            volume_out[z, h : h + 1, :] = own[h, z : z + 1, :] + conv_last(low, last, z, h)


def call(kernel, out_shapes, scratch, *args):
    specs = [pl.BlockSpec(memory_space=pltpu.VMEM) for _ in args]
    if args[0].dtype == jnp.int32 and args[0].ndim == 1:
        specs[0] = pl.BlockSpec(memory_space=pltpu.SMEM)
    return pl.pallas_call(
        kernel,
        out_shape=[jax.ShapeDtypeStruct(s, d) for s, d in out_shapes],
        in_specs=specs,
        out_specs=[pl.BlockSpec(memory_space=pltpu.VMEM) for _ in out_shapes],
        scratch_shapes=[pltpu.VMEM(s, d) for s, d in scratch],
        compiler_params=pltpu.CompilerParams(vmem_limit_bytes=40 * 1024 * 1024),
    )(*args)


def beside(cells, axis):
    count = lax.axis_size(axis)
    before = lax.ppermute(cells, axis, [(i, i + 1) for i in range(count - 1)])
    after = lax.ppermute(cells, axis, [(i + 1, i) for i in range(count - 1)])
    return before, after


def scatter_to(cells, axis):
    return lax.all_to_all(cells, axis, 0, 0, tiled=True)


def per_device(volume, cotangent, kernel_in, kernel_mid, kernel_out, measured, angle_ids, ray_bins):
    depths, planes = lax.axis_size("depth"), lax.axis_size("plane")
    depth_at, plane_at = lax.axis_index("depth"), lax.axis_index("plane")
    pos = jnp.stack([depth_at, plane_at]).astype(jnp.int32)

    v_before, v_after = beside(volume, "depth")
    tall = jnp.concatenate([v_before, volume, v_after], axis=0)
    t_before, t_after = beside(tall, "plane")

    in_k = kernel_in.reshape(3, 3, 3, C)
    mid_k = kernel_mid.reshape(3, 3, 3, C, C)
    out_k = kernel_out.reshape(3, 3, 3, C)
    flip = lambda k: k[::-1, ::-1, ::-1]

    def base(k):
        t = jnp.pad(jnp.transpose(k, (3, 0, 2, 1)), ((0, 0), (0, 0), (0, 0), (0, 13)))
        return jnp.pad(t.reshape(C, 144), ((0, 0), (0, 112))).astype(F32)

    def tail(k):
        t = jnp.transpose(k, (2, 0, 1, 3)).reshape(3, 9 * C)
        return jnp.pad(t, ((0, 13), (0, 0)))

    mid_forward = jnp.transpose(mid_k, (2, 3, 0, 1, 4)).reshape(3 * C, 9 * C)
    mid_back = jnp.transpose(flip(mid_k), (2, 4, 0, 1, 3)).reshape(3 * C, 9 * C)

    vc, act1, slope1, act2, slope2, rays = call(
        functools.partial(forward_kernel, depths, planes),
        [
            ((16, 16, W), BF16),
            ((6, 6 * C, W), BF16),
            ((6, 6 * C, W), F32),
            ((6, 6 * C, W), BF16),
            ((8, 8 * C, W), F32),
            ((TILES, 2 * HI, 128), F32),
        ],
        [
            ((12, 16, W), F32),
            ((12, 48, W), BF16),
            ((16, 16, W), F32),
            ((10, 10 * C, W), BF16),
            ((6, 6 * C, W), BF16),
        ],
        pos, t_before, tall, t_after, base(in_k), mid_forward, tail(out_k), cotangent, ray_bins,
    )
    each = TILES // planes
    gathered = scatter_to(rays.reshape(planes, each * 2 * HI, 128), "plane")
    tiles = plane_at * each + jnp.arange(each)
    chosen = jnp.stack(
        [
            lax.dynamic_slice(measured, (tiles[t] % Z, angle_ids[tiles[t] // Z], 0), (1, 1, BINS))
            for t in range(each)
        ]
    ).reshape(each, HI, 128)
    spread = call(
        functools.partial(weigh_kernel, planes),
        [((planes, each * HI, 128), F32)],
        [],
        gathered, chosen,
    )[0]
    weighted = scatter_to(spread, "plane").reshape(TILES, HI, 128)
    c_before, c_after = beside(cotangent, "plane")
    b_before, b_after = beside(ray_bins, "plane")
    slab, own = call(
        functools.partial(back_kernel, planes),
        [((12, Z, W), BF16), ((H, Z, W), F32)],
        [((12, Z, W), F32)],
        pos, weighted, b_before, ray_bins, b_after, c_before, cotangent, c_after,
    )
    s_before, s_after = beside(slab, "depth")
    grad_volume, term_mid, term_out, term_in = call(
        functools.partial(backward_kernel, depths, planes),
        [((Z, H, W), F32), ((3 * C, 9 * C), F32), ((16, 9 * C), F32), ((16, 3 * C), F32)],
        [
            ((10, 16, W), F32),
            ((10, 48, W), BF16),
            ((16, 16, W), F32),
            ((8, 8 * C, W), BF16),
            ((4, 3, 4 * C, W), BF16),
            ((6, 6 * C, W), BF16),
            ((4, 3, 4 * C, W), BF16),
        ],
        pos, s_before, slab, s_after, own, tail(flip(in_k)), mid_back, base(flip(out_k)),
        vc, act1, slope1, act2, slope2,
    )
    flat = jnp.concatenate(
        [term_mid.reshape(-1), term_out[:3].reshape(-1), term_in[:9].reshape(-1)]
    )
    used = flat.shape[0]
    room = 32 * 8 * 128
    sent = jnp.pad(flat, (0, room - used)).reshape(planes, room // planes // 128, 128)
    part = jnp.sum(scatter_to(sent, "plane"), axis=0)
    part = scatter_to(jnp.broadcast_to(part[None], (depths,) + part.shape), "depth")
    part = jnp.sum(part, axis=0)
    full = scatter_to(jnp.broadcast_to(part[None], (planes,) + part.shape), "plane").reshape(-1)
    cell_count = Z * depths * H * planes * W
    full = full * (float(cell_count) ** (-0.5))
    n_mid = 27 * C * C
    got_mid = full[:n_mid].reshape(3, C, 3, 3, C).transpose(2, 3, 0, 1, 4).reshape(27, C, C)
    got_out = full[n_mid : n_mid + 27 * C].reshape(3, 3, 3, C).transpose(1, 2, 0, 3).reshape(27, C)
    got_in = full[n_mid + 27 * C : used].reshape(27, C)
    return (grad_volume, got_in, got_mid, got_out)


def solution(mesh):
    placed = (
        P("depth", "plane", None),
        P("depth", "plane", None),
        P(),
        P(),
        P(),
        P("depth", None, None),
        P(),
        P(None, "plane", None),
    )
    return jax.shard_map(
        per_device,
        mesh=mesh,
        in_specs=placed,
        out_specs=(P("depth", "plane", None), P(), P(), P()),
        check_vma=False,
    )
```

time: 829 us -> 140 us (0.17)
  waiting for transfers between devices: 518 us -> 19.2 us
  other arithmetic: 56.2 us -> 0.18 us
  blocking collectives: 94.7 us -> 50.3 us
  matrix products: 32.7 us -> 0 us
  starting transfers between devices: 74.9 us -> 46.9 us
  local copies, waits for them, and re-layouts: 32.5 us -> 10.3 us
  between operations: 15.8 us -> 2.94 us
  Pallas kernels: 0 us -> 9.77 us
    psum x2 -> x0, waiting for transfers between devices: 491 us -> none  [the longest x1 266 us: per_device(): lax.psum((term_in, term_mid, term_out), ('depth', 'plane'))]
    psum x1 -> x0, blocking collectives: 94.7 us -> none  [per_device(): lax.psum((term_in, term_mid, term_out), ('depth', 'plane'))]
    all_to_all x0 -> x3, blocking collectives: none -> 50.3 us  [scatter_to(): return lax.all_to_all(cells, axis, 0, 0, tiled=True)]
    ppermute x24 -> x10, starting transfers between devices: 74.8 us -> 32.9 us  [the longest x5 24.6 us: beside(): before = lax.ppermute(cells, axis, [(i, i + 1) for i in range(count - 1)])]
    dot_general x189 -> x0, matrix products: 32.7 us -> none  [the longest x81 12.4 us: kernel_grad(): jnp.einsum('ozhw,czhw->oc', grad_out, window, preferred_element_type=jnp....]
    scatter-add x8 -> x0, other arithmetic: 27.9 us -> none  [one_view(): jax.ops.segment_sum(flattened, bins_view.reshape(-1), num_segments=BINS)]
    ppermute x24 -> x10, waiting for transfers between devices: 27 us -> 10.9 us  [the longest x5 10.9 us: beside(): after = lax.ppermute(cells, axis, [(i + 1, i) for i in range(count - 1)])]
    all_to_all x0 -> x2, starting transfers between devices: none -> 13.9 us  [scatter_to(): return lax.all_to_all(cells, axis, 0, 0, tiled=True)]
  transfers between devices with their start and end apart: 26 -> 12, of which waited for: 11 -> 5; matrix products, arithmetic and copies ran while one was open for 2% -> 4% of each run, Pallas kernels for 0% -> 0%
where the time goes in v1:
time: 140 us
  blocking collectives  50.3 us (36%)
  starting transfers between devices  46.9 us (34%)
  waiting for transfers between devices  19.2 us (14%)
  local copies, waits for them, and re-layouts  10.3 us (7%)
  Pallas kernels  9.77 us (7%)
  between operations  2.94 us (2%)
    all_to_all x3, blocking collectives, scatter_to(): return lax.all_to_all(cells, axis, 0, 0, tiled=True)  50.3 us
    ppermute x5, starting transfers between devices, beside(): before = lax.ppermute(cells, axis, [(i, i + 1) for i in range(count - 1)])  24.6 us
    all_to_all x2, starting transfers between devices, scatter_to(): return lax.all_to_all(cells, axis, 0, 0, tiled=True)  13.9 us
    ppermute x5, waiting for transfers between devices, beside(): after = lax.ppermute(cells, axis, [(i + 1, i) for i in range(count - 1)])  10.9 us
    pallas_call x4, Pallas kernels, call(): pl.pallas_call(kernel, out_shape=[jax.ShapeDtypeStruct(s, d) for s, d in...  9.77 us
    ppermute x5, starting transfers between devices, beside(): after = lax.ppermute(cells, axis, [(i + 1, i) for i in range(count - 1)])  8.35 us
    all_to_all x2, waiting for transfers between devices, scatter_to(): return lax.all_to_all(cells, axis, 0, 0, tiled=True)  8.31 us
  transfers between devices with their start and end apart: 12, of which 5 were waited for; matrix products, arithmetic and copies ran while one was open for 4% of the time, Pallas kernels for 0%

profile of v1, /device:TPU:1, one launch (start us, length us, event | category | flops | bytes accessed | tf_op | source)
XLA Modules:
  0.0 139.5 jit_solution(15224823631085683)
XLA Ops:
  0.7 6.8 %collective-permute-start = (bf16[4,4,128]{2,1,0:T(4,128)(2,1)}, bf16[4,4,128]{2,1,0:T(4,128)(2,1)S(1)}, u32[]{:S(2)}, u32[]{:S(2)}) collective-permute-start(bf16[4,4,128]{2,1,0:T(4,128)(2,1)} %param.8), channel_id=1, source_target_pairs={{0,32},{32,64},{64,96},{96,128},{128,160},{160,192},{192,224},{224... | collective-permute-start | bytes 12296 | tf_op jit(solution)/shard_map/ppermute | solution.py:291
  7.4 1.3 collective-permute-start.1
  8.7 0.7 reshape.71
  9.5 0.1 copy.37
  9.6 0.7 constant_dynamic-update-slice_fusion.1
  10.3 5.4 %collective-permute-done.1 = bf16[4,4,128]{2,1,0:T(4,128)(2,1)S(1)} collective-permute-done((bf16[4,4,128]{2,1,0:T(4,128)(2,1)}, bf16[4,4,128]{2,1,0:T(4,128)(2,1)S(1)}, u32[]{:S(2)}, u32[]{:S(2)}) %collective-permute-start.1) | collective-permute-done | bytes 4128 | tf_op jit(solution)/shard_map/ppermute | solution.py:292
  15.7 4.9 %collective-permute-start.2 = (bf16[12,4,128]{2,1,0:T(4,128)(2,1)S(1)}, bf16[12,4,128]{2,1,0:T(4,128)(2,1)S(1)}, u32[]{:S(2)}, u32[]{:S(2)}) collective-permute-start(bf16[12,4,128]{2,1,0:T(4,128)(2,1)S(1)} %constant_dynamic-update-slice_fusion.mid), channel_id=1, source_target_pairs={{0,1},{1,2},{2,3},{3,4},{4,5},{5,6},{6,7},{7,8},{8,9},{9,10},{10,1... | collective-permute-start | bytes 36872 | tf_op jit(solution)/shard_map/ppermute | solution.py:291
  20.6 1.9 %collective-permute-start.3 = (bf16[12,4,128]{2,1,0:T(4,128)(2,1)S(1)}, bf16[12,4,128]{2,1,0:T(4,128)(2,1)S(1)}, u32[]{:S(2)}, u32[]{:S(2)}) collective-permute-start(bf16[12,4,128]{2,1,0:T(4,128)(2,1)S(1)} %constant_dynamic-update-slice_fusion.mid), channel_id=1, source_target_pairs={{1,0},{2,1},{3,2},{4,3},{5,4},{6,5},{7,6},{8,7},{9,8},{10,9},{11,1... | collective-permute-start | bytes 36872 | tf_op jit(solution)/shard_map/ppermute | solution.py:292
  22.5 0.1 pad_add_fusion.pos
  22.6 0.2 copy.49
  22.7 0.2 reshape.74.second
  22.9 0.5 copy-done.4
  23.5 0.1 reshape.76
  23.6 2.0 %collective-permute-done.3.hi = bf16[12,4,128]{2,1,0:T(4,128)(2,1)S(1)} collective-permute-done((bf16[12,4,128]{2,1,0:T(4,128)(2,1)S(1)}, bf16[12,4,128]{2,1,0:T(4,128)(2,1)S(1)}, u32[]{:S(2)}, u32[]{:S(2)}) %collective-permute-start.3) | collective-permute-done | bytes 12320 | tf_op jit(solution)/shard_map/ppermute | solution.py:292
  25.6 4.2 %shard_map.111 = (bf16[16,16,128]{2,1,0:T(8,128)(2,1)S(1)}, bf16[6,192,128]{2,1,0:T(8,128)(2,1)S(1)}, f32[6,192,128]{2,1,0:T(8,128)S(1)}, bf16[6,192,128]{2,1,0:...) custom-call(s32[2]{0:T(128)S(1)} %pad_add_fusion.pos, ...), custom_call_target="tpu_custom_call" | custom-call | tf_op jit(solution)/shard_map/pallas_call | solution.py:279
  29.8 8.6 %all-to-all-start = ((f32[32,16,128]{2,1,0:T(8,128)}), f32[32,16,128]{2,1,0:T(8,128)S(1)}, u32[]{:S(2)}, u32[]{:S(2)}) async-start(f32[32,16,128]{2,1,0:T(8,128)} %get-tuple-element.16), calls=%async_computation | async-start | bytes 524288 | tf_op jit(solution)/shard_map/all_to_all | solution.py:297
  38.5 0.6 copy-done.5
  39.1 0.6 dynamic_slice.6
  41.7 8.3 %all-to-all-done.rays = f32[32,16,128]{2,1,0:T(8,128)S(1)} async-done(((f32[32,16,128]{2,1,0:T(8,128)}), f32[32,16,128]{2,1,0:T(8,128)S(1)}, u32[]{:S(2)}, u32[]{:S(2)}) %all-to-all-start) | async-done | bytes 262176 | tf_op jit(solution)/shard_map/all_to_all | solution.py:297
  50.0 0.7 shard_map.112
  50.7 5.3 %all-to-all-start.1 = ((f32[32,8,128]{2,1,0:T(8,128)}), f32[32,8,128]{2,1,0:T(8,128)S(1)}, u32[]{:S(2)}, u32[]{:S(2)}) async-start(f32[32,8,128]{2,1,0:T(8,128)} %shard_map.112), calls=%async_computation.1 | async-start | bytes 262144 | tf_op jit(solution)/shard_map/all_to_all | solution.py:297
  56.1 3.5 %collective-permute-start.4 = (s32[8,4,128]{2,1,0:T(4,128)S(1)}, s32[8,4,128]{2,1,0:T(4,128)S(1)}, u32[]{:S(2)}, u32[]{:S(2)}) collective-permute-start(s32[8,4,128]{2,1,0:T(4,128)S(1)} %copy-done.1), channel_id=1, source_target_pairs={{0,1},{1,2},{2,3},{3,4},{4,5},{5,6},{6,7},{7,8},{8,9},{9,10},{10,1... | collective-permute-start | bytes 49160 | tf_op jit(solution)/shard_map/ppermute | solution.py:291
  59.6 1.9 %collective-permute-start.5 = (s32[8,4,128]{2,1,0:T(4,128)S(1)}, s32[8,4,128]{2,1,0:T(4,128)S(1)}, u32[]{:S(2)}, u32[]{:S(2)}) collective-permute-start(s32[8,4,128]{2,1,0:T(4,128)S(1)} %copy-done.1), channel_id=1, source_target_pairs={{1,0},{2,1},{3,2},{4,3},{5,4},{6,5},{7,6},{8,7},{9,8},{10,9},{11,1... | collective-permute-start | bytes 49160 | tf_op jit(solution)/shard_map/ppermute | solution.py:292
  61.5 3.6 %collective-permute-start.6 = (f32[4,4,128]{2,1,0:T(4,128)S(1)}, f32[4,4,128]{2,1,0:T(4,128)S(1)}, u32[]{:S(2)}, u32[]{:S(2)}) collective-permute-start(f32[4,4,128]{2,1,0:T(4,128)S(1)} %copy-done.2), channel_id=1, source_target_pairs={{0,1},{1,2},{2,3},{3,4},{4,5},{5,6},{6,7},{7,8},{8,9},{9,10},{10,1... | collective-permute-start | bytes 24584 | tf_op jit(solution)/shard_map/ppermute | solution.py:291
  65.2 1.9 %collective-permute-start.7 = (f32[4,4,128]{2,1,0:T(4,128)S(1)}, f32[4,4,128]{2,1,0:T(4,128)S(1)}, u32[]{:S(2)}, u32[]{:S(2)}) collective-permute-start(f32[4,4,128]{2,1,0:T(4,128)S(1)} %copy-done.2), channel_id=1, source_target_pairs={{1,0},{2,1},{3,2},{4,3},{5,4},{6,5},{7,6},{8,7},{9,8},{10,9},{11,1... | collective-permute-start | bytes 24584 | tf_op jit(solution)/shard_map/ppermute | solution.py:292
  67.3 2.9 %collective-permute-done.7.cot_hi = f32[4,4,128]{2,1,0:T(4,128)S(1)} collective-permute-done((f32[4,4,128]{2,1,0:T(4,128)S(1)}, f32[4,4,128]{2,1,0:T(4,128)S(1)}, u32[]{:S(2)}, u32[]{:S(2)}) %collective-permute-start.7) | collective-permute-done | bytes 8224 | tf_op jit(solution)/shard_map/ppermute | solution.py:292
  70.2 1.3 shard_map.113
  71.5 5.7 %collective-permute-start.8 = (bf16[12,4,128]{2,1,0:T(4,128)(2,1)S(1)}, bf16[12,4,128]{2,1,0:T(4,128)(2,1)S(1)}, u32[]{:S(2)}, u32[]{:S(2)}) collective-permute-start(bf16[12,4,128]{2,1,0:T(4,128)(2,1)S(1)} %get-tuple-element.17.mid), channel_id=1, source_target_pairs={{0,32},{32,64},{64,96},{96,128},{128,160},{160,192},{192,224},{224... | collective-permute-start | bytes 36872 | tf_op jit(solution)/shard_map/ppermute | solution.py:291
  77.3 1.3 collective-permute-start.9
  78.6 0.9 copy.41
  79.5 2.1 %rev.10 = bf16[3,3,3,32,32]{3,1,0,4,2:T(4,128)(2,1)S(1)} reverse(bf16[3,3,3,32,32]{3,1,0,4,2:T(4,128)(2,1)} %copy.41), dimensions={0,1,2} | reverse | bytes 110592 | tf_op jit(solution)/shard_map/rev | solution.py:312
  81.6 0.2 reshape.78.second
  81.9 0.1 reshape.77
  82.0 0.6 collective-permute-done.9.hi
  82.6 3.5 %shard_map.114 = (f32[4,4,128]{2,1,0:T(4,128)}, f32[96,288]{1,0:T(8,128)S(1)}, f32[16,288]{1,0:T(8,128)S(1)}, f32[16,96]{1,0:T(8,128)S(1)}) custom-call(s32[2]{0:T(128)S(1)} %pad_add_fusion.pos, bf16[12,4,128]{2,1,0:T(4,128)(2,1)S(1)} %collective-permute-done.8.lo, bf16[12,4,128]{2,1,0:T(4,128)(2,1)S(1)} %get-tuple-element.17.mid, ...), custom_call_target="tpu_custom_call" | custom-call | tf_op jit(solution)/shard_map/pallas_call | solution.py:279
  86.1 0.1 reshape.80
  86.2 0.1 reshape.81
  86.3 0.1 reshape.82
  86.4 0.1 concatenate.7
  86.5 19.5 %all_to_all.25 = f32[32,8,128]{2,1,0:T(8,128)S(1)} all-to-all(f32[32,8,128]{2,1,0:T(8,128)S(1)} %pad_bitcast_fusion), channel_id=1, replica_groups=mesh['depth'=16,'plane'=32] {'plane'}, dimensions={0} | all-to-all | bytes 262144 | tf_op jit(solution)/shard_map/all_to_all | solution.py:297
  106.0 16.0 %all_to_all.26 = f32[16,8,128]{2,1,0:T(8,128)S(1)} all-to-all(f32[16,8,128]{2,1,0:T(8,128)S(1)} %broadcast_in_dim.4), channel_id=1, replica_groups=mesh['depth'=16,'plane'=32] {'depth'}, dimensions={0} | all-to-all | bytes 131072 | tf_op jit(solution)/shard_map/all_to_all | solution.py:297
  122.0 14.8 %all_to_all.27 = f32[32,8,128]{2,1,0:T(8,128)S(1)} all-to-all(f32[32,8,128]{2,1,0:T(8,128)S(1)} %broadcast_in_dim.5), channel_id=1, replica_groups=mesh['depth'=16,'plane'=32] {'plane'}, dimensions={0} | all-to-all | bytes 262144 | tf_op jit(solution)/shard_map/all_to_all | solution.py:297
  136.9 0.2 mul.15
  137.0 0.3 reshape.84
  137.4 0.8 copy.44
  138.2 0.6 slice.22
  138.8 0.1 reshape.86
  138.9 0.6 reshape.87
  (44 shorter events, 0.5 us)
Async XLA Ops:
  0.6 41.0 %copy-start = (f32[4,32,1024]{2,1,0:T(8,128)S(1)}, f32[4,32,1024]{2,1,0:T(8,128)}, u32[]{:S(2)}) copy-start(f32[4,32,1024]{2,1,0:T(8,128)} %param.13) | copy-start | bytes 1572868
  0.6 21.9 %copy-start.3 = (bf16[27,32,32]{2,1,0:T(8,128)(2,1)S(1)}, bf16[27,32,32]{2,1,0:T(8,128)(2,1)}, u32[]{:S(2)}) copy-start(bf16[27,32,32]{2,1,0:T(8,128)(2,1)} %param.11) | copy-start | bytes 165892
  0.7 8.9 %collective-permute-start = (bf16[4,4,128]{2,1,0:T(4,128)(2,1)}, bf16[4,4,128]{2,1,0:T(4,128)(2,1)S(1)}, u32[]{:S(2)}, u32[]{:S(2)}) collective-permute-start(bf16[4,4,128]{2,1,0:T(4,128)(2,1)} %param.8), channel_id=1, source_target_pairs={{0,32},{32,64},{64,96},{96,128},{128,160},{160,192},{192,224},{224... | collective-permute-start | bytes 12296 | tf_op jit(solution)/shard_map/ppermute | solution.py:291
  7.4 8.2 %collective-permute-start.1 = (bf16[4,4,128]{2,1,0:T(4,128)(2,1)}, bf16[4,4,128]{2,1,0:T(4,128)(2,1)S(1)}, u32[]{:S(2)}, u32[]{:S(2)}) collective-permute-start(bf16[4,4,128]{2,1,0:T(4,128)(2,1)} %param.8), channel_id=1, source_target_pairs={{32,0},{64,32},{96,64},{128,96},{160,128},{192,160},{224,192},{256... | collective-permute-start | bytes 12296 | tf_op jit(solution)/shard_map/ppermute | solution.py:292
  15.7 7.9 %collective-permute-start.2 = (bf16[12,4,128]{2,1,0:T(4,128)(2,1)S(1)}, bf16[12,4,128]{2,1,0:T(4,128)(2,1)S(1)}, u32[]{:S(2)}, u32[]{:S(2)}) collective-permute-start(bf16[12,4,128]{2,1,0:T(4,128)(2,1)S(1)} %constant_dynamic-update-slice_fusion.mid), channel_id=1, source_target_pairs={{0,1},{1,2},{2,3},{3,4},{4,5},{5,6},{6,7},{7,8},{8,9},{9,10},{10,1... | collective-permute-start | bytes 36872 | tf_op jit(solution)/shard_map/ppermute | solution.py:291
  20.6 5.0 %collective-permute-start.3 = (bf16[12,4,128]{2,1,0:T(4,128)(2,1)S(1)}, bf16[12,4,128]{2,1,0:T(4,128)(2,1)S(1)}, u32[]{:S(2)}, u32[]{:S(2)}) collective-permute-start(bf16[12,4,128]{2,1,0:T(4,128)(2,1)S(1)} %constant_dynamic-update-slice_fusion.mid), channel_id=1, source_target_pairs={{1,0},{2,1},{3,2},{4,3},{5,4},{6,5},{7,6},{8,7},{9,8},{10,9},{11,1... | collective-permute-start | bytes 36872 | tf_op jit(solution)/shard_map/ppermute | solution.py:292
  22.7 0.7 copy-start.4
  23.5 2.1 %copy-start.1 = (s32[8,4,128]{2,1,0:T(4,128)S(1)}, s32[8,4,128]{2,1,0:T(4,128)}, u32[]{:S(2)}) copy-start(s32[8,4,128]{2,1,0:T(4,128)} %bins_mid.1) | copy-start | bytes 49156
  23.6 2.0 %copy-start.2 = (f32[4,4,128]{2,1,0:T(4,128)S(1)}, f32[4,4,128]{2,1,0:T(4,128)}, u32[]{:S(2)}) copy-start(f32[4,4,128]{2,1,0:T(4,128)} %cot_mid.1) | copy-start | bytes 24580
  29.8 20.2 %all-to-all-start = ((f32[32,16,128]{2,1,0:T(8,128)}), f32[32,16,128]{2,1,0:T(8,128)S(1)}, u32[]{:S(2)}, u32[]{:S(2)}) async-start(f32[32,16,128]{2,1,0:T(8,128)} %get-tuple-element.16), calls=%async_computation | async-start | bytes 524288 | tf_op jit(solution)/shard_map/all_to_all | solution.py:297
  38.5 0.7 copy-start.5
  50.7 19.5 %all-to-all-start.1 = ((f32[32,8,128]{2,1,0:T(8,128)}), f32[32,8,128]{2,1,0:T(8,128)S(1)}, u32[]{:S(2)}, u32[]{:S(2)}) async-start(f32[32,8,128]{2,1,0:T(8,128)} %shard_map.112), calls=%async_computation.1 | async-start | bytes 262144 | tf_op jit(solution)/shard_map/all_to_all | solution.py:297
  56.1 14.1 %collective-permute-start.4 = (s32[8,4,128]{2,1,0:T(4,128)S(1)}, s32[8,4,128]{2,1,0:T(4,128)S(1)}, u32[]{:S(2)}, u32[]{:S(2)}) collective-permute-start(s32[8,4,128]{2,1,0:T(4,128)S(1)} %copy-done.1), channel_id=1, source_target_pairs={{0,1},{1,2},{2,3},{3,4},{4,5},{5,6},{6,7},{7,8},{8,9},{9,10},{10,1... | collective-permute-start | bytes 49160 | tf_op jit(solution)/shard_map/ppermute | solution.py:291
  59.6 10.6 %collective-permute-start.5 = (s32[8,4,128]{2,1,0:T(4,128)S(1)}, s32[8,4,128]{2,1,0:T(4,128)S(1)}, u32[]{:S(2)}, u32[]{:S(2)}) collective-permute-start(s32[8,4,128]{2,1,0:T(4,128)S(1)} %copy-done.1), channel_id=1, source_target_pairs={{1,0},{2,1},{3,2},{4,3},{5,4},{6,5},{7,6},{8,7},{9,8},{10,9},{11,1... | collective-permute-start | bytes 49160 | tf_op jit(solution)/shard_map/ppermute | solution.py:292
  61.5 5.7 %collective-permute-start.6 = (f32[4,4,128]{2,1,0:T(4,128)S(1)}, f32[4,4,128]{2,1,0:T(4,128)S(1)}, u32[]{:S(2)}, u32[]{:S(2)}) collective-permute-start(f32[4,4,128]{2,1,0:T(4,128)S(1)} %copy-done.2), channel_id=1, source_target_pairs={{0,1},{1,2},{2,3},{3,4},{4,5},{5,6},{6,7},{7,8},{8,9},{9,10},{10,1... | collective-permute-start | bytes 24584 | tf_op jit(solution)/shard_map/ppermute | solution.py:291
  65.2 5.0 %collective-permute-start.7 = (f32[4,4,128]{2,1,0:T(4,128)S(1)}, f32[4,4,128]{2,1,0:T(4,128)S(1)}, u32[]{:S(2)}, u32[]{:S(2)}) collective-permute-start(f32[4,4,128]{2,1,0:T(4,128)S(1)} %copy-done.2), channel_id=1, source_target_pairs={{1,0},{2,1},{3,2},{4,3},{5,4},{6,5},{7,6},{8,7},{9,8},{10,9},{11,1... | collective-permute-start | bytes 24584 | tf_op jit(solution)/shard_map/ppermute | solution.py:292
  71.5 10.5 %collective-permute-start.8 = (bf16[12,4,128]{2,1,0:T(4,128)(2,1)S(1)}, bf16[12,4,128]{2,1,0:T(4,128)(2,1)S(1)}, u32[]{:S(2)}, u32[]{:S(2)}) collective-permute-start(bf16[12,4,128]{2,1,0:T(4,128)(2,1)S(1)} %get-tuple-element.17.mid), channel_id=1, source_target_pairs={{0,32},{32,64},{64,96},{96,128},{128,160},{160,192},{192,224},{224... | collective-permute-start | bytes 36872 | tf_op jit(solution)/shard_map/ppermute | solution.py:291
  77.3 5.3 %collective-permute-start.9 = (bf16[12,4,128]{2,1,0:T(4,128)(2,1)S(1)}, bf16[12,4,128]{2,1,0:T(4,128)(2,1)S(1)}, u32[]{:S(2)}, u32[]{:S(2)}) collective-permute-start(bf16[12,4,128]{2,1,0:T(4,128)(2,1)S(1)} %get-tuple-element.17.mid), channel_id=1, source_target_pairs={{32,0},{64,32},{96,64},{128,96},{160,128},{192,160},{224,192},{256... | collective-permute-start | bytes 36872 | tf_op jit(solution)/shard_map/ppermute | solution.py:292

commit v2 on v1

--- a/solution.py
+++ b/solution.py
@@ -66,7 +66,7 @@
 
 def low_match(low_row):
     n = low_row.shape[1]
-    at = lax.broadcasted_iota(jnp.int32, (128, n), 0)
+    at = lax.broadcasted_iota(jnp.int32, (128, n), 0).astype(low_row.dtype)
     return jnp.where(low_row == at, 1.0, 0.0).astype(BF16)
 
 
@@ -74,6 +74,19 @@
     x = triple(ref, z, row * C, 3 * C)
     y = dot(weights, x)
     return y[C : 2 * C] + from_left(y[0:C]) + from_right(y[2 * C :])
+
+
+def conv_mid_back(ref, weights, z, row):
+    x = jnp.concatenate(
+        [
+            ref[z + 2 - oz, (row + 2 - oy) * C : (row + 3 - oy) * C, :]
+            for oz in range(3)
+            for oy in range(3)
+        ],
+        axis=0,
+    )
+    y = dot(weights, x)
+    return y[C : 2 * C] + from_right(y[0:C]) + from_left(y[2 * C :])
 
 
 def conv_last(ref, weights, z, row):
@@ -99,6 +112,17 @@
     return both[:n] + both[n:]
 
 
+def pack_kernel(before, own, after, cot, bins, out):
+    out[0:4] = before[...]
+    out[4:8] = own[...]
+    out[8:12] = after[...]
+    head = cot[...].astype(BF16)
+    out[12:16] = head
+    out[16:20] = (cot[...] - head.astype(F32)).astype(BF16)
+    out[20:28] = (bins[...] >> 7).astype(F32).astype(BF16)
+    out[28:36] = (bins[...] & 127).astype(F32).astype(BF16)
+
+
 def forward_kernel(depth_count, plane_count, pos, lo, mid, hi, first, second, third, cot, bins,
                    vc_out, act1_out, slope1_out, act2_out, slope2_out, rays_out,
                    vs, v3, vcs, a1, a2):
@@ -106,9 +130,9 @@
     plane_at = pos[1] * H
     nz, nh = depth_count * Z, plane_count * H
     vs[...] = jnp.zeros_like(vs)
-    vs[:, 0:4, :] = lo[...].astype(F32)
-    vs[:, 4:8, :] = mid[...].astype(F32)
-    vs[:, 8:12, :] = hi[...].astype(F32)
+    vs[:, 0:4, :] = lo[0:12].astype(F32)
+    vs[:, 4:8, :] = mid[0:12].astype(F32)
+    vs[:, 8:12, :] = hi[0:12].astype(F32)
     three_shifts(v3, vs[...].reshape(12 * 16, W), 12)
     vcs[...] = jnp.zeros_like(vcs)
     for z in range(Z):
@@ -151,49 +175,50 @@
         field.append(jnp.concatenate(rows, axis=0))
     for a in range(ANG):
         tile = project(field, bins, a).reshape(2, Z, HI, 128)
-        rays_out[a * Z : (a + 1) * Z, 0:HI, :] = tile[0]
-        rays_out[a * Z : (a + 1) * Z, HI : 2 * HI, :] = tile[1]
+        head = tile[0].astype(BF16).astype(F32)
+        rows = jnp.concatenate([head, tile[0] - head, tile[1]], axis=1)
+        rays_out[a * Z : (a + 1) * Z] = rows.astype(BF16)
 
 
 def weigh_kernel(planes, rays, chosen, out):
     each = TILES // planes
-    total = jnp.sum(rays[...], axis=0)
+    total = jnp.sum(rays[...].astype(F32), axis=0)
     for t in range(each):
-        forward = total[t * 2 * HI : t * 2 * HI + HI]
-        turned = total[t * 2 * HI + HI : (t + 1) * 2 * HI]
+        at = t * 3 * HI
+        forward = total[at : at + HI] + total[at + HI : at + 2 * HI]
+        turned = total[at + 2 * HI : at + 3 * HI]
         ratio = (forward - chosen[t]) / delta_scale
         inner = 1.0 + ratio * ratio
         weighted = turned / (inner * jnp.sqrt(inner))
-        out[:, t * HI : (t + 1) * HI, :] = jnp.broadcast_to(weighted[None], (planes, HI, 128))
-
-
-def back_kernel(plane_count, pos, rays, bins_lo, bins_mid, bins_hi, cot_lo, cot_mid, cot_hi,
-                slab_out, own_out, slab):
+        weighted = jnp.broadcast_to(weighted[None], (planes, HI, 128))
+        out[:, t * HI : (t + 1) * HI, :] = weighted.astype(BF16)
+
+
+def back_kernel(plane_count, pos, rays, lo, mid, hi, cot, slab_out, own_out, slab):
     plane_at = pos[1] * H
     nh = plane_count * H
-    pieces = (bins_lo, bins_mid, bins_hi)
-    cots = (cot_lo, cot_mid, cot_hi)
-    at = lax.broadcasted_iota(jnp.int32, (HI, W), 0)
+    packs = [p[12:36].astype(F32) for p in (lo, mid, hi)]
+    at = lax.broadcasted_iota(jnp.int32, (HI, W), 0).astype(F32)
     spans = range(1, 11)
     total = [None] * len(spans)
     for a in range(ANG):
-        rows = rays[a * Z : (a + 1) * Z].reshape(Z * HI, 128)
-        head = rows.astype(BF16)
-        rest = (rows - head.astype(F32)).astype(BF16)
-        both = jnp.concatenate([head, rest], axis=0)
-        bins = [pieces[h // H][a, h % H : h % H + 1, :] for h in spans]
-        low = jnp.concatenate([low_match(b & 127) for b in bins], axis=1)
-        spread = dot(both, low)
-        spread = spread[: Z * HI] + spread[Z * HI :]
-        for i, b in enumerate(bins):
-            match = (b >> 7) == at
-            match = jnp.concatenate([match] * Z, axis=0)
+        rows = rays[a * Z : (a + 1) * Z].astype(F32).reshape(Z * HI, 128).astype(BF16)
+        highs = [packs[h // H][8 + a, h % H : h % H + 1, :] for h in spans]
+        lows = [packs[h // H][16 + a, h % H : h % H + 1, :] for h in spans]
+        spread = dot(rows, jnp.concatenate([low_match(b) for b in lows], axis=1))
+        for i, b in enumerate(highs):
+            match = jnp.concatenate([b == at] * Z, axis=0)
             term = jnp.where(match, spread[:, i * W : (i + 1) * W], 0.0)
             total[i] = term if total[i] is None else total[i] + term
     slab[...] = jnp.zeros_like(slab)
     for i, h in enumerate(spans):
         summed = jnp.sum(total[i].reshape(Z, HI, W), axis=1)
-        field = cots[h // H][:, h % H, :] - (0.25 / ANG) * summed
+        if H <= h < 2 * H:
+            rows = cot[:, h - H, :]
+        else:
+            pack = packs[h // H]
+            rows = pack[0:4, h % H, :] + pack[4:8, h % H, :]
+        field = rows - (0.25 / ANG) * summed
         row = plane_at + h - H
         slab[h] = jnp.where((row >= 0) & (row < nh), -field, 0.0)
         if H <= h < 2 * H:
@@ -203,8 +228,8 @@
 
 def backward_kernel(depth_count, plane_count, pos, lo, mid, hi, own, first, second, third,
                     vc, act1, slope1, act2, slope2,
-                    volume_out, mid_out, out_out, in_out,
-                    gs, v3, gx, gm, gm3, low, low3):
+                    volume_out, terms_out,
+                    gs, v3, gx, gm, gm3, low, low3, terms):
     depth_at = pos[0] * Z
     plane_at = pos[1] * H
     nz, nh = depth_count * Z, plane_count * H
@@ -244,17 +269,27 @@
         )
 
     def windows(ref):
-        return jnp.concatenate(
+        rows = jnp.concatenate(
             [triple(ref, z, h * C, 3 * C) for z in range(Z) for h in range(H)], axis=1
         )
-
-    mid_out[...] = dot_nt(shifted(gm3), windows(act1))
+        return jnp.concatenate([rows, jnp.zeros((96, 16 * W), BF16)], axis=0)
+
+    terms[...] = jnp.zeros_like(terms)
+    term = dot_nt(shifted(gm3), windows(act1))
+    terms[0:96] = term[:, 0:128]
+    terms[96:192] = term[:, 128:256]
+    tail = term[0:24, 256:384]
+    for i in range(1, 4):
+        tail = tail + pltpu.roll(term[24 * i : 24 * i + 24, 256:384], 32 * i, 1)
+    terms[192:216] = tail
     gx_all = jnp.concatenate([gx[i] for i in range(16)], axis=1).astype(BF16)
-    out_out[...] = dot_nt(gx_all, windows(act2))
+    term = dot_nt(gx_all, windows(act2))
+    for i in range(3):
+        terms[216 + 3 * i : 219 + 3 * i] = term[0:3, 128 * i : 128 * i + 128]
     wide = second[...]
     ok_rows = row_ok(6 * C, plane_at - 1, nh)
     for z in range(6):
-        y = jnp.concatenate([conv_mid(gm, wide, z, h) for h in range(6)], axis=0)
+        y = jnp.concatenate([conv_mid_back(gm, wide, z, h) for h in range(6)], axis=0)
         at = depth_at + (z - 1)
         ok = ok_rows & (at >= 0) & (at < nz)
         g = jnp.where(ok, y * slope1[z], 0.0).astype(BF16)
@@ -265,11 +300,30 @@
             low3[z - 1, 1] = g[C : 5 * C]
             low3[z - 1, 2] = from_left(inner).astype(BF16)
     vc_all = jnp.concatenate([vc[i] for i in range(16)], axis=1)
-    in_out[...] = dot_nt(vc_all, shifted(low3))
+    rows = jnp.concatenate([shifted(low3), jnp.zeros((32, 16 * W), BF16)], axis=0)
+    terms[225:234] = dot_nt(vc_all, rows)[0:9]
+    terms_out[...] = terms[...].reshape(terms_out.shape).astype(BF16)
     last = first[...]
     for z in range(Z):
         for h in range(H):
             volume_out[z, h : h + 1, :] = own[h, z : z + 1, :] + conv_last(low, last, z, h)
+
+
+def unpack_kernel(scale, sums, in_out, mid_out, out_out):
+    full = sums[...].astype(F32).reshape(256, 128) * scale
+    quarters = [full] + [pltpu.roll(full, 128 - 32 * j, 1) for j in range(1, 4)]
+    last = jnp.concatenate([q[192:216, 0:C] for q in quarters], axis=0)
+    for q in range(9):
+        for ox in range(3):
+            if q < 8:
+                start = 96 * (q // 4) + C * ox
+                mid_out[q * 3 + ox] = quarters[q % 4][start : start + C, 0:C]
+            else:
+                mid_out[q * 3 + ox] = last[C * ox : C * ox + C]
+        start = 216 + 3 * (q // 4)
+        out_out[q * 3 : q * 3 + 3, :] = quarters[q % 4][start : start + 3, 0:C]
+        for ox in range(3):
+            in_out[q * 3 + ox : q * 3 + ox + 1, :] = quarters[ox][225 + q : 226 + q, 0:C]
 
 
 def call(kernel, out_shapes, scratch, *args):
@@ -303,8 +357,10 @@
     pos = jnp.stack([depth_at, plane_at]).astype(jnp.int32)
 
     v_before, v_after = beside(volume, "depth")
-    tall = jnp.concatenate([v_before, volume, v_after], axis=0)
-    t_before, t_after = beside(tall, "plane")
+    pack = call(
+        pack_kernel, [((36, H, W), BF16)], [], v_before, volume, v_after, cotangent, ray_bins
+    )[0]
+    p_before, p_after = beside(pack, "plane")
 
     in_k = kernel_in.reshape(3, 3, 3, C)
     mid_k = kernel_mid.reshape(3, 3, 3, C, C)
@@ -320,7 +376,7 @@
         return jnp.pad(t, ((0, 13), (0, 0)))
 
     mid_forward = jnp.transpose(mid_k, (2, 3, 0, 1, 4)).reshape(3 * C, 9 * C)
-    mid_back = jnp.transpose(flip(mid_k), (2, 4, 0, 1, 3)).reshape(3 * C, 9 * C)
+    mid_back = jnp.transpose(mid_k, (2, 4, 0, 1, 3)).reshape(3 * C, 9 * C)
 
     vc, act1, slope1, act2, slope2, rays = call(
         functools.partial(forward_kernel, depths, planes),
@@ -330,7 +386,7 @@
             ((6, 6 * C, W), F32),
             ((6, 6 * C, W), BF16),
             ((8, 8 * C, W), F32),
-            ((TILES, 2 * HI, 128), F32),
+            ((TILES, 3 * HI, 128), BF16),
         ],
         [
             ((12, 16, W), F32),
@@ -339,10 +395,10 @@
             ((10, 10 * C, W), BF16),
             ((6, 6 * C, W), BF16),
         ],
-        pos, t_before, tall, t_after, base(in_k), mid_forward, tail(out_k), cotangent, ray_bins,
+        pos, p_before, pack, p_after, base(in_k), mid_forward, tail(out_k), cotangent, ray_bins,
     )
     each = TILES // planes
-    gathered = scatter_to(rays.reshape(planes, each * 2 * HI, 128), "plane")
+    gathered = scatter_to(rays.reshape(planes, each * 3 * HI, 128), "plane")
     tiles = plane_at * each + jnp.arange(each)
     chosen = jnp.stack(
         [
@@ -352,23 +408,21 @@
     ).reshape(each, HI, 128)
     spread = call(
         functools.partial(weigh_kernel, planes),
-        [((planes, each * HI, 128), F32)],
+        [((planes, each * HI, 128), BF16)],
         [],
         gathered, chosen,
     )[0]
     weighted = scatter_to(spread, "plane").reshape(TILES, HI, 128)
-    c_before, c_after = beside(cotangent, "plane")
-    b_before, b_after = beside(ray_bins, "plane")
     slab, own = call(
         functools.partial(back_kernel, planes),
         [((12, Z, W), BF16), ((H, Z, W), F32)],
         [((12, Z, W), F32)],
-        pos, weighted, b_before, ray_bins, b_after, c_before, cotangent, c_after,
+        pos, weighted, p_before, pack, p_after, cotangent,
     )
     s_before, s_after = beside(slab, "depth")
-    grad_volume, term_mid, term_out, term_in = call(
+    grad_volume, terms = call(
         functools.partial(backward_kernel, depths, planes),
-        [((Z, H, W), F32), ((3 * C, 9 * C), F32), ((16, 9 * C), F32), ((16, 3 * C), F32)],
+        [((Z, H, W), F32), ((planes, 256 // planes, 128), BF16)],
         [
             ((10, 16, W), F32),
             ((10, 48, W), BF16),
@@ -377,26 +431,23 @@
             ((4, 3, 4 * C, W), BF16),
             ((6, 6 * C, W), BF16),
             ((4, 3, 4 * C, W), BF16),
+            ((256, 128), F32),
         ],
         pos, s_before, slab, s_after, own, tail(flip(in_k)), mid_back, base(flip(out_k)),
         vc, act1, slope1, act2, slope2,
     )
-    flat = jnp.concatenate(
-        [term_mid.reshape(-1), term_out[:3].reshape(-1), term_in[:9].reshape(-1)]
-    )
-    used = flat.shape[0]
-    room = 32 * 8 * 128
-    sent = jnp.pad(flat, (0, room - used)).reshape(planes, room // planes // 128, 128)
-    part = jnp.sum(scatter_to(sent, "plane"), axis=0)
-    part = scatter_to(jnp.broadcast_to(part[None], (depths,) + part.shape), "depth")
-    part = jnp.sum(part, axis=0)
-    full = scatter_to(jnp.broadcast_to(part[None], (planes,) + part.shape), "plane").reshape(-1)
+    def shared(cells, axis):
+        total = jnp.sum(cells.astype(F32), axis=0, keepdims=True).astype(BF16)
+        return scatter_to(jnp.broadcast_to(total, (lax.axis_size(axis),) + total.shape[1:]), axis)
+
+    sums = shared(shared(scatter_to(terms, "plane"), "depth"), "plane")
     cell_count = Z * depths * H * planes * W
-    full = full * (float(cell_count) ** (-0.5))
-    n_mid = 27 * C * C
-    got_mid = full[:n_mid].reshape(3, C, 3, 3, C).transpose(2, 3, 0, 1, 4).reshape(27, C, C)
-    got_out = full[n_mid : n_mid + 27 * C].reshape(3, 3, 3, C).transpose(1, 2, 0, 3).reshape(27, C)
-    got_in = full[n_mid + 27 * C : used].reshape(27, C)
+    got_in, got_mid, got_out = call(
+        functools.partial(unpack_kernel, float(cell_count) ** (-0.5)),
+        [((27, C), F32), ((27, C, C), F32), ((27, C), F32)],
+        [],
+        sums,
+    )
     return (grad_volume, got_in, got_mid, got_out)
 
 

time: 140 us -> 123 us (0.88)
  starting transfers between devices: 46.9 us -> 35.9 us
  blocking collectives: 50.3 us -> 41.9 us
  waiting for transfers between devices: 19.2 us -> 25.8 us
  local copies, waits for them, and re-layouts: 10.3 us -> 4.65 us
    all_to_all x3, blocking collectives: 50.3 us -> 41.9 us  [scatter_to(): return lax.all_to_all(cells, axis, 0, 0, tiled=True)]
    ppermute x5 -> x3, starting transfers between devices: 24.6 us -> 17.4 us  [beside(): before = lax.ppermute(cells, axis, [(i, i + 1) for i in range(count - 1)])]
    all_to_all x2, waiting for transfers between devices: 8.31 us -> 14.9 us  [scatter_to(): return lax.all_to_all(cells, axis, 0, 0, tiled=True)]
    ppermute x5 -> x3, starting transfers between devices: 8.35 us -> 4.5 us  [beside(): after = lax.ppermute(cells, axis, [(i + 1, i) for i in range(count - 1)])]
    rev x3 -> x2, local copies, waits for them, and re-layouts: 2.22 us -> 0.07 us  [per_device(): flip = lambda k: k[::-1, ::-1, ::-1]]
    pallas_call x4 -> x6, Pallas kernels: 9.77 us -> 10.5 us  [call(): pl.pallas_call(kernel, out_shape=[jax.ShapeDtypeStruct(s, d) for s, d in...]
    ppermute x5 -> x3, waiting for transfers between devices: 10.9 us -> 10.9 us  [beside(): after = lax.ppermute(cells, axis, [(i + 1, i) for i in range(count - 1)])]
  transfers between devices with their start and end apart: 12 -> 8, of which waited for: 5 -> 5; matrix products, arithmetic and copies ran while one was open for 4% -> 3% of each run, Pallas kernels for 0% -> 0%
where the time goes in v2:
time: 123 us; the launch traced here: 122 us
  blocking collectives  41.9 us (34%)
  starting transfers between devices  35.9 us (29%)
  waiting for transfers between devices  25.8 us (21%)
  Pallas kernels  10.5 us (9%)
  local copies, waits for them, and re-layouts  4.65 us (4%)
  between operations  2.86 us (2%)
    all_to_all x3, blocking collectives, scatter_to(): return lax.all_to_all(cells, axis, 0, 0, tiled=True)  41.9 us
    ppermute x3, starting transfers between devices, beside(): before = lax.ppermute(cells, axis, [(i, i + 1) for i in range(count - 1)])  17.4 us
    all_to_all x2, waiting for transfers between devices, scatter_to(): return lax.all_to_all(cells, axis, 0, 0, tiled=True)  14.9 us
    all_to_all x2, starting transfers between devices, scatter_to(): return lax.all_to_all(cells, axis, 0, 0, tiled=True)  14 us
    ppermute x3, waiting for transfers between devices, beside(): after = lax.ppermute(cells, axis, [(i + 1, i) for i in range(count - 1)])  10.9 us
    pallas_call x6, Pallas kernels, call(): pl.pallas_call(kernel, out_shape=[jax.ShapeDtypeStruct(s, d) for s, d in...  10.5 us
    ppermute x3, starting transfers between devices, beside(): after = lax.ppermute(cells, axis, [(i + 1, i) for i in range(count - 1)])  4.5 us
  transfers between devices with their start and end apart: 8, of which 5 were waited for; matrix products, arithmetic and copies ran while one was open for 3% of the time, Pallas kernels for 0%

profile of v2, /device:TPU:1, one launch (start us, length us, event | category | flops | bytes accessed | tf_op | source)
XLA Modules:
  0.0 121.7 jit_solution(158683889576096334)
XLA Ops:
  0.6 0.0 copy-start
  0.6 6.8 %collective-permute-start = (bf16[4,4,128]{2,1,0:T(4,128)(2,1)}, bf16[4,4,128]{2,1,0:T(4,128)(2,1)S(1)}, u32[]{:S(2)}, u32[]{:S(2)}) collective-permute-start(bf16[4,4,128]{2,1,0:T(4,128)(2,1)} %own.1), channel_id=1, source_target_pairs={{0,32},{32,64},{64,96},{96,128},{128,160},{160,192},{192,224},{224... | collective-permute-start | bytes 12296 | tf_op jit(solution)/shard_map/ppermute | solution.py:345
  7.4 1.3 %collective-permute-start.1 = (bf16[4,4,128]{2,1,0:T(4,128)(2,1)}, bf16[4,4,128]{2,1,0:T(4,128)(2,1)S(1)}, u32[]{:S(2)}, u32[]{:S(2)}) collective-permute-start(bf16[4,4,128]{2,1,0:T(4,128)(2,1)} %own.1), channel_id=1, source_target_pairs={{32,0},{64,32},{96,64},{128,96},{160,128},{192,160},{224,192},{256... | collective-permute-start | bytes 12296 | tf_op jit(solution)/shard_map/ppermute | solution.py:346
  8.7 0.7 reshape.43
  9.5 0.1 copy.27
  9.5 0.0 copy-start.3
  9.6 0.0 copy-start.1
  9.6 0.0 collective-permute-done.before
  9.6 6.0 %collective-permute-done.1.after = bf16[4,4,128]{2,1,0:T(4,128)(2,1)S(1)} collective-permute-done((bf16[4,4,128]{2,1,0:T(4,128)(2,1)}, bf16[4,4,128]{2,1,0:T(4,128)(2,1)S(1)}, u32[]{:S(2)}, u32[]{:S(2)}) %collective-permute-start.1) | collective-permute-done | bytes 4128 | tf_op jit(solution)/shard_map/ppermute | solution.py:346
  15.6 0.0 copy-done.2
  15.6 0.0 copy-done.3
  15.6 0.0 copy-done.1
  15.7 4.9 %collective-permute-start.2 = (bf16[36,4,128]{2,1,0:T(4,128)(2,1)S(1)}, bf16[36,4,128]{2,1,0:T(4,128)(2,1)S(1)}, u32[]{:S(2)}, u32[]{:S(2)}) collective-permute-start(bf16[36,4,128]{2,1,0:T(4,128)(2,1)S(1)} %shard_map.111.mid), channel_id=1, source_target_pairs={{0,1},{1,2},{2,3},{3,4},{4,5},{5,6},{6,7},{7,8},{8,9},{9,10},{10,1... | collective-permute-start | bytes 110600 | tf_op jit(solution)/shard_map/ppermute | solution.py:345
  20.6 1.9 %collective-permute-start.3 = (bf16[36,4,128]{2,1,0:T(4,128)(2,1)S(1)}, bf16[36,4,128]{2,1,0:T(4,128)(2,1)S(1)}, u32[]{:S(2)}, u32[]{:S(2)}) collective-permute-start(bf16[36,4,128]{2,1,0:T(4,128)(2,1)S(1)} %shard_map.111.mid), channel_id=1, source_target_pairs={{1,0},{2,1},{3,2},{4,3},{5,4},{6,5},{7,6},{8,7},{9,8},{10,9},{11,1... | collective-permute-start | bytes 110600 | tf_op jit(solution)/shard_map/ppermute | solution.py:346
  22.5 0.1 pad_add_fusion.pos
  22.6 1.1 copy.37
  23.7 0.0 copy-start.5
  23.7 0.2 reshape.46.second
  23.9 0.5 copy-done.5
  24.4 0.1 reshape.48
  24.5 0.0 collective-permute-done.2.lo
  24.5 1.3 %collective-permute-done.3.hi = bf16[36,4,128]{2,1,0:T(4,128)(2,1)S(1)} collective-permute-done((bf16[36,4,128]{2,1,0:T(4,128)(2,1)S(1)}, bf16[36,4,128]{2,1,0:T(4,128)(2,1)S(1)}, u32[]{:S(2)}, u32[]{:S(2)}) %collective-permute-start.3) | collective-permute-done | bytes 36896 | tf_op jit(solution)/shard_map/ppermute | solution.py:346
  25.9 4.2 %shard_map.112 = (bf16[16,16,128]{2,1,0:T(8,128)(2,1)S(1)}, bf16[6,192,128]{2,1,0:T(8,128)(2,1)S(1)}, f32[6,192,128]{2,1,0:T(8,128)S(1)}, bf16[6,192,128]{2,1,0:...) custom-call(s32[2]{0:T(128)S(1)} %pad_add_fusion.pos, ...), custom_call_target="tpu_custom_call" | custom-call | tf_op jit(solution)/shard_map/pallas_call | solution.py:333
  30.1 8.6 %all-to-all-start = ((bf16[32,24,128]{2,1,0:T(8,128)(2,1)}), bf16[32,24,128]{2,1,0:T(8,128)(2,1)S(1)}, u32[]{:S(2)}, u32[]{:S(2)}) async-start(bf16[32,24,128]{2,1,0:T(8,128)(2,1)} %get-tuple-element.17), calls=%async_computation | async-start | bytes 393216 | tf_op jit(solution)/shard_map/all_to_all | solution.py:351
  38.7 0.0 copy-start.6
  38.8 0.6 copy-done.6
  39.4 0.6 dynamic_slice.6
  41.9 0.0 copy-done
  42.0 6.9 %all-to-all-done.rays = bf16[32,24,128]{2,1,0:T(8,128)(2,1)S(1)} async-done(((bf16[32,24,128]{2,1,0:T(8,128)(2,1)}), bf16[32,24,128]{2,1,0:T(8,128)(2,1)S(1)}, u32[]{:S(2)}, u32[]{:S(2)}) %all-to-all-start) | async-done | bytes 196640 | tf_op jit(solution)/shard_map/all_to_all | solution.py:351
  48.8 0.7 shard_map.113
  49.5 5.4 %all-to-all-start.1 = ((bf16[32,8,128]{2,1,0:T(8,128)(2,1)}), bf16[32,8,128]{2,1,0:T(8,128)(2,1)S(1)}, u32[]{:S(2)}, u32[]{:S(2)}) async-start(bf16[32,8,128]{2,1,0:T(8,128)(2,1)} %shard_map.113), calls=%async_computation.1 | async-start | bytes 131072 | tf_op jit(solution)/shard_map/all_to_all | solution.py:351
  54.9 0.0 copy-start.4
  55.0 0.1 copy.33
  55.1 8.0 %all-to-all-done.1.rays = bf16[32,8,128]{2,1,0:T(8,128)(2,1)S(1)} async-done(((bf16[32,8,128]{2,1,0:T(8,128)(2,1)}), bf16[32,8,128]{2,1,0:T(8,128)(2,1)S(1)}, u32[]{:S(2)}, u32[]{:S(2)}) %all-to-all-start.1) | async-done | bytes 65568 | tf_op jit(solution)/shard_map/all_to_all | solution.py:351
  63.1 1.1 shard_map.114
  64.2 5.7 %collective-permute-start.4 = (bf16[12,4,128]{2,1,0:T(4,128)(2,1)S(1)}, bf16[12,4,128]{2,1,0:T(4,128)(2,1)S(1)}, u32[]{:S(2)}, u32[]{:S(2)}) collective-permute-start(bf16[12,4,128]{2,1,0:T(4,128)(2,1)S(1)} %get-tuple-element.18.mid), channel_id=1, source_target_pairs={{0,32},{32,64},{64,96},{96,128},{128,160},{160,192},{192,224},{224... | collective-permute-start | bytes 36872 | tf_op jit(solution)/shard_map/ppermute | solution.py:345
  70.0 1.3 %collective-permute-start.5 = (bf16[12,4,128]{2,1,0:T(4,128)(2,1)S(1)}, bf16[12,4,128]{2,1,0:T(4,128)(2,1)S(1)}, u32[]{:S(2)}, u32[]{:S(2)}) collective-permute-start(bf16[12,4,128]{2,1,0:T(4,128)(2,1)S(1)} %get-tuple-element.18.mid), channel_id=1, source_target_pairs={{32,0},{64,32},{96,64},{128,96},{160,128},{192,160},{224,192},{256... | collective-permute-start | bytes 36872 | tf_op jit(solution)/shard_map/ppermute | solution.py:346
  71.3 0.0 copy-done.4
  71.3 0.2 copy.31
  71.5 0.1 reshape.49
  71.6 0.2 reshape.50.second
  71.8 0.0 collective-permute-done.4.lo
  71.8 3.5 %collective-permute-done.5.hi = bf16[12,4,128]{2,1,0:T(4,128)(2,1)S(1)} collective-permute-done((bf16[12,4,128]{2,1,0:T(4,128)(2,1)S(1)}, bf16[12,4,128]{2,1,0:T(4,128)(2,1)S(1)}, u32[]{:S(2)}, u32[]{:S(2)}) %collective-permute-start.5) | collective-permute-done | bytes 12320 | tf_op jit(solution)/shard_map/ppermute | solution.py:346
  75.3 3.5 %shard_map.115 = (f32[4,4,128]{2,1,0:T(4,128)}, bf16[32,8,128]{2,1,0:T(8,128)(2,1)S(1)}) custom-call(s32[2]{0:T(128)S(1)} %pad_add_fusion.pos, bf16[12,4,128]{2,1,0:T(4,128)(2,1)S(1)} %collective-permute-done.4.lo, bf16[12,4,128]{2,1,0:T(4,128)(2,1)S(1)} %get-tuple-element.18.mid, bf16[12,4,128]{2,1,0:T(4,128)(2,1)S(1)} %collective-permute-done.5.hi, ...), custom_call_target="tpu_custom_call" | custom-call | tf_op jit(solution)/shard_map/pallas_call | solution.py:333
  78.8 13.6 %all_to_all.25 = bf16[32,8,128]{2,1,0:T(8,128)(2,1)S(1)} all-to-all(bf16[32,8,128]{2,1,0:T(8,128)(2,1)S(1)} %get-tuple-element.26), channel_id=1, replica_groups=mesh['depth'=16,'plane'=32] {'plane'}, dimensions={0} | all-to-all | bytes 131072 | tf_op jit(solution)/shard_map/all_to_all | solution.py:351
  92.4 14.9 %all_to_all.26 = bf16[16,8,128]{2,1,0:T(8,128)(2,1)S(1)} all-to-all(bf16[16,8,128]{2,1,0:T(8,128)(2,1)S(1)} %broadcast_in_dim.4), channel_id=1, replica_groups=mesh['depth'=16,'plane'=32] {'depth'}, dimensions={0} | all-to-all | bytes 65536 | tf_op jit(solution)/shard_map/all_to_all | solution.py:351
  107.3 13.4 %all_to_all.27.sums = bf16[32,8,128]{2,1,0:T(8,128)(2,1)S(1)} all-to-all(bf16[32,8,128]{2,1,0:T(8,128)(2,1)S(1)} %broadcast_in_dim.5), channel_id=1, replica_groups=mesh['depth'=16,'plane'=32] {'plane'}, dimensions={0} | all-to-all | bytes 131072 | tf_op jit(solution)/shard_map/all_to_all | solution.py:351
  120.8 0.9 shard_map.116
  (20 shorter events, 0.3 us)
Async XLA Ops:
  0.6 41.3 %copy-start = (f32[4,32,1024]{2,1,0:T(8,128)S(1)}, f32[4,32,1024]{2,1,0:T(8,128)}, u32[]{:S(2)}) copy-start(f32[4,32,1024]{2,1,0:T(8,128)} %param.13) | copy-start | bytes 1572868
  0.6 8.9 %collective-permute-start = (bf16[4,4,128]{2,1,0:T(4,128)(2,1)}, bf16[4,4,128]{2,1,0:T(4,128)(2,1)S(1)}, u32[]{:S(2)}, u32[]{:S(2)}) collective-permute-start(bf16[4,4,128]{2,1,0:T(4,128)(2,1)} %own.1), channel_id=1, source_target_pairs={{0,32},{32,64},{64,96},{96,128},{128,160},{160,192},{192,224},{224... | collective-permute-start | bytes 12296 | tf_op jit(solution)/shard_map/ppermute | solution.py:345
  7.4 8.2 %collective-permute-start.1 = (bf16[4,4,128]{2,1,0:T(4,128)(2,1)}, bf16[4,4,128]{2,1,0:T(4,128)(2,1)S(1)}, u32[]{:S(2)}, u32[]{:S(2)}) collective-permute-start(bf16[4,4,128]{2,1,0:T(4,128)(2,1)} %own.1), channel_id=1, source_target_pairs={{32,0},{64,32},{96,64},{128,96},{160,128},{192,160},{224,192},{256... | collective-permute-start | bytes 12296 | tf_op jit(solution)/shard_map/ppermute | solution.py:346
  9.5 6.1 %copy-start.2 = (s32[8,4,128]{2,1,0:T(4,128)S(1)}, s32[8,4,128]{2,1,0:T(4,128)}, u32[]{:S(2)}) copy-start(s32[8,4,128]{2,1,0:T(4,128)} %bins.3) | copy-start | bytes 49156
  9.5 6.1 %copy-start.3 = (bf16[4,4,128]{2,1,0:T(4,128)(2,1)S(1)}, bf16[4,4,128]{2,1,0:T(4,128)(2,1)}, u32[]{:S(2)}) copy-start(bf16[4,4,128]{2,1,0:T(4,128)(2,1)} %own.1) | copy-start | bytes 12292
  9.6 6.1 %copy-start.1 = (f32[4,4,128]{2,1,0:T(4,128)S(1)}, f32[4,4,128]{2,1,0:T(4,128)}, u32[]{:S(2)}) copy-start(f32[4,4,128]{2,1,0:T(4,128)} %cot.5) | copy-start | bytes 24580
  15.7 8.9 %collective-permute-start.2 = (bf16[36,4,128]{2,1,0:T(4,128)(2,1)S(1)}, bf16[36,4,128]{2,1,0:T(4,128)(2,1)S(1)}, u32[]{:S(2)}, u32[]{:S(2)}) collective-permute-start(bf16[36,4,128]{2,1,0:T(4,128)(2,1)S(1)} %shard_map.111.mid), channel_id=1, source_target_pairs={{0,1},{1,2},{2,3},{3,4},{4,5},{5,6},{6,7},{7,8},{8,9},{9,10},{10,1... | collective-permute-start | bytes 110600 | tf_op jit(solution)/shard_map/ppermute | solution.py:345
  20.6 5.3 %collective-permute-start.3 = (bf16[36,4,128]{2,1,0:T(4,128)(2,1)S(1)}, bf16[36,4,128]{2,1,0:T(4,128)(2,1)S(1)}, u32[]{:S(2)}, u32[]{:S(2)}) collective-permute-start(bf16[36,4,128]{2,1,0:T(4,128)(2,1)S(1)} %shard_map.111.mid), channel_id=1, source_target_pairs={{1,0},{2,1},{3,2},{4,3},{5,4},{6,5},{7,6},{8,7},{9,8},{10,9},{11,1... | collective-permute-start | bytes 110600 | tf_op jit(solution)/shard_map/ppermute | solution.py:346
  23.7 0.7 copy-start.5
  30.1 18.7 %all-to-all-start = ((bf16[32,24,128]{2,1,0:T(8,128)(2,1)}), bf16[32,24,128]{2,1,0:T(8,128)(2,1)S(1)}, u32[]{:S(2)}, u32[]{:S(2)}) async-start(bf16[32,24,128]{2,1,0:T(8,128)(2,1)} %get-tuple-element.17), calls=%async_computation | async-start | bytes 393216 | tf_op jit(solution)/shard_map/all_to_all | solution.py:351
  38.7 0.7 copy-start.6
  49.5 13.6 %all-to-all-start.1 = ((bf16[32,8,128]{2,1,0:T(8,128)(2,1)}), bf16[32,8,128]{2,1,0:T(8,128)(2,1)S(1)}, u32[]{:S(2)}, u32[]{:S(2)}) async-start(bf16[32,8,128]{2,1,0:T(8,128)(2,1)} %shard_map.113), calls=%async_computation.1 | async-start | bytes 131072 | tf_op jit(solution)/shard_map/all_to_all | solution.py:351
  54.9 16.4 %copy-start.4 = (bf16[27,32,32]{2,1,0:T(8,128)(2,1)S(1)}, bf16[27,32,32]{2,1,0:T(8,128)(2,1)}, u32[]{:S(2)}) copy-start(bf16[27,32,32]{2,1,0:T(8,128)(2,1)} %param.11) | copy-start | bytes 165892
  64.2 7.6 %collective-permute-start.4 = (bf16[12,4,128]{2,1,0:T(4,128)(2,1)S(1)}, bf16[12,4,128]{2,1,0:T(4,128)(2,1)S(1)}, u32[]{:S(2)}, u32[]{:S(2)}) collective-permute-start(bf16[12,4,128]{2,1,0:T(4,128)(2,1)S(1)} %get-tuple-element.18.mid), channel_id=1, source_target_pairs={{0,32},{32,64},{64,96},{96,128},{128,160},{160,192},{192,224},{224... | collective-permute-start | bytes 36872 | tf_op jit(solution)/shard_map/ppermute | solution.py:345
  70.0 5.3 %collective-permute-start.5 = (bf16[12,4,128]{2,1,0:T(4,128)(2,1)S(1)}, bf16[12,4,128]{2,1,0:T(4,128)(2,1)S(1)}, u32[]{:S(2)}, u32[]{:S(2)}) collective-permute-start(bf16[12,4,128]{2,1,0:T(4,128)(2,1)S(1)} %get-tuple-element.18.mid), channel_id=1, source_target_pairs={{32,0},{64,32},{96,64},{128,96},{160,128},{192,160},{224,192},{256... | collective-permute-start | bytes 36872 | tf_op jit(solution)/shard_map/ppermute | solution.py:346

commit v3 on v2

--- a/solution.py
+++ b/solution.py
@@ -5,6 +5,7 @@
 from jax import lax
 from jax.experimental import pallas as pl
 from jax.experimental.pallas import tpu as pltpu
+from jax.sharding import Mesh
 from jax.sharding import PartitionSpec as P
 
 BINS = 1024
@@ -17,6 +18,11 @@
 TILES = ANG * Z
 
 delta_scale = 6.0
+
+DEPTH = ("x", "z_hi")
+PLANE = ("z_lo", "y", "core")
+NEAR = ("x", "z_lo", "core")
+FAR = ("z_hi", "y")
 F32 = jnp.float32
 BF16 = jnp.bfloat16
 
@@ -51,6 +57,29 @@
 def banded(base, height, shift):
     rows = [pltpu.roll(base, h + shift, 1) if h + shift else base for h in range(height)]
     return jnp.concatenate(rows, axis=0)[:, :144].astype(BF16)
+
+
+def base_of(kernel, flip):
+    lane = lanes_of((27, 256))
+    oz, ox, oy = lane // 48, (lane % 48) // 16, lane % 16
+    at = oz * 9 + oy * 3 + ox
+    row = lax.broadcasted_iota(jnp.int32, (27, 256), 0)
+    take = ((26 - at if flip else at) == row) & (oy < 3) & (lane < 144)
+    take = jnp.where(take, 1.0, 0.0).astype(BF16)
+    return lax.dot_general(kernel, take, (((0,), (0,)), ((), ())), preferred_element_type=F32)
+
+
+def tail_of(kernel, flip):
+    spot = lax.broadcasted_iota(jnp.int32, (C, 9 * C), 0)
+    spread = jnp.where(lanes_of((C, 9 * C)) % C == spot, 1.0, 0.0).astype(BF16)
+    wide = dot(kernel, spread)
+    row = lax.broadcasted_iota(jnp.int32, (27, 9 * C), 0)
+    row = 26 - row if flip else row
+    wide = jnp.where(row // 3 == lanes_of((27, 9 * C)) // C, wide, 0.0).astype(BF16)
+    lane = lanes_of((16, 27))
+    lane = 26 - lane if flip else lane
+    pick = lane % 3 == lax.broadcasted_iota(jnp.int32, (16, 27), 0)
+    return dot(jnp.where(pick, 1.0, 0.0).astype(BF16), wide).astype(BF16)
 
 
 def triple(ref, z, start, size):
@@ -135,36 +164,37 @@
     vs[:, 8:12, :] = hi[0:12].astype(F32)
     three_shifts(v3, vs[...].reshape(12 * 16, W), 12)
     vcs[...] = jnp.zeros_like(vcs)
-    for z in range(Z):
+    for z in range(8):
         for h in range(H):
             for oz in range(3):
-                vcs[z * H + h, oz * 3 : oz * 3 + 3, :] = vs[z + 3 + oz, h + 3 : h + 6, :]
+                vcs[z * H + h, oz * 3 : oz * 3 + 3, :] = vs[z + 1 + oz, h + 3 : h + 6, :]
     vc_out[...] = vcs[...].astype(BF16)
-    weights = banded(first[...], 10, 0)
+    weights = banded(base_of(first[...], False), 10, 0)
     ok_rows = row_ok(10 * C, plane_at - 3, nh)
-    for z in range(10):
-        p = dot(weights, v3[z : z + 3].reshape(144, W))
-        sigma = jax.nn.sigmoid(p)
-        at = depth_at + (z - 3)
-        ok = ok_rows & (at >= 0) & (at < nz)
-        act = jnp.where(ok, p * sigma, 0.0).astype(BF16)
-        a1[z] = act
-        if 2 <= z < 8:
-            act1_out[z - 2] = act[2 * C : 8 * C]
-            slope1_out[z - 2] = (sigma * (1.0 + p * (1.0 - sigma)))[2 * C : 8 * C]
-    wide = second[...]
-    ok_rows = row_ok(8 * C, plane_at - 2, nh)
     for z in range(8):
-        p = jnp.concatenate([conv_mid(a1, wide, z, h) for h in range(8)], axis=0)
+        p = dot(weights, v3[z + 1 : z + 4].reshape(144, W))
         sigma = jax.nn.sigmoid(p)
         at = depth_at + (z - 2)
         ok = ok_rows & (at >= 0) & (at < nz)
         act = jnp.where(ok, p * sigma, 0.0).astype(BF16)
+        a1[z] = act
+        act1_out[z] = act[2 * C : 8 * C]
+        slope1_out[z] = (sigma * (1.0 + p * (1.0 - sigma)))[2 * C : 8 * C]
+    wide = jnp.concatenate(
+        [jnp.concatenate([second[q * 3 + ox] for q in range(9)], axis=1) for ox in range(3)],
+        axis=0,
+    )
+    ok_rows = row_ok(8 * C, plane_at - 2, nh)
+    for z in range(6):
+        p = jnp.concatenate([conv_mid(a1, wide, z, h) for h in range(8)], axis=0)
+        sigma = jax.nn.sigmoid(p)
+        at = depth_at + (z - 1)
+        ok = ok_rows & (at >= 0) & (at < nz)
+        act = jnp.where(ok, p * sigma, 0.0).astype(BF16)
         slope2_out[z] = sigma * (1.0 + p * (1.0 - sigma))
-        if 1 <= z < 7:
-            a2[z - 1] = act[C : 7 * C]
-            act2_out[z - 1] = act[C : 7 * C]
-    last = third[...]
+        a2[z] = act[C : 7 * C]
+        act2_out[z] = act[C : 7 * C]
+    last = tail_of(third[...], False)
     field = []
     for h in range(H):
         rows = []
@@ -226,56 +256,59 @@
     slab_out[...] = slab[...].astype(BF16)
 
 
-def backward_kernel(depth_count, plane_count, pos, lo, mid, hi, own, first, second, third,
+def backward_kernel(depth_count, plane_count, pos, slab, own, first, second, third,
                     vc, act1, slope1, act2, slope2,
-                    volume_out, terms_out,
+                    volume_out, before_out, after_out, terms_out,
                     gs, v3, gx, gm, gm3, low, low3, terms):
     depth_at = pos[0] * Z
     plane_at = pos[1] * H
     nz, nh = depth_count * Z, plane_count * H
     gs[...] = jnp.zeros_like(gs)
     for h in range(12):
-        gs[0:3, h, :] = lo[h].astype(F32)[1:4]
-        gs[3:7, h, :] = mid[h].astype(F32)
-        gs[7:10, h, :] = hi[h].astype(F32)[0:3]
-    three_shifts(v3, gs[...].reshape(160, W), 10)
+        gs[2:6, h, :] = slab[h].astype(F32)
+    three_shifts(v3, gs[...].reshape(128, W), 8)
     gx[...] = jnp.zeros_like(gx)
-    rows = gs[3:7, 4:8, :].reshape(16, W)
+    rows = gs[2:6, 4:8, :].reshape(16, W)
     gx[:, 0, :] = from_right(rows)
     gx[:, 1, :] = rows
     gx[:, 2, :] = from_left(rows)
-    weights = banded(third[...], 8, 1)
+    edge = jnp.zeros((2, 8 * C, W), BF16)
+    gm[0:2] = edge
+    gm[8:10] = edge
+    edge = jnp.zeros((2, 6 * C, W), BF16)
+    low[0:2] = edge
+    low[10:12] = edge
+    weights = banded(base_of(third[...], True), 8, 1)
     ok_rows = row_ok(8 * C, plane_at - 2, nh)
-    for z in range(8):
+    for z in range(6):
         y = dot(weights, v3[z : z + 3].reshape(144, W))
-        at = depth_at + (z - 2)
+        at = depth_at + (z - 1)
         ok = ok_rows & (at >= 0) & (at < nz)
         g = jnp.where(ok, y * slope2[z], 0.0).astype(BF16)
-        gm[z] = g
-        if 2 <= z < 6:
-            inner = g[2 * C : 6 * C].astype(F32)
-            gm3[z - 2, 0] = from_right(inner).astype(BF16)
-            gm3[z - 2, 1] = g[2 * C : 6 * C]
-            gm3[z - 2, 2] = from_left(inner).astype(BF16)
-
-    def shifted(ref):
+        gm[z + 2] = g
+        inner = g[2 * C : 6 * C].astype(F32)
+        gm3[z, 0] = from_right(inner).astype(BF16)
+        gm3[z, 1] = g[2 * C : 6 * C]
+        gm3[z, 2] = from_left(inner).astype(BF16)
+
+    def shifted(ref, slices):
         return jnp.concatenate(
             [
                 jnp.concatenate([ref[z, ox, h * C : (h + 1) * C, :] for ox in range(3)], axis=0)
-                for z in range(Z)
+                for z in range(slices)
                 for h in range(H)
             ],
             axis=1,
         )
 
-    def windows(ref):
+    def windows(ref, slices):
         rows = jnp.concatenate(
-            [triple(ref, z, h * C, 3 * C) for z in range(Z) for h in range(H)], axis=1
+            [triple(ref, z, h * C, 3 * C) for z in range(slices) for h in range(H)], axis=1
         )
-        return jnp.concatenate([rows, jnp.zeros((96, 16 * W), BF16)], axis=0)
+        return jnp.concatenate([rows, jnp.zeros((96, slices * H * W), BF16)], axis=0)
 
     terms[...] = jnp.zeros_like(terms)
-    term = dot_nt(shifted(gm3), windows(act1))
+    term = dot_nt(shifted(gm3, 6), windows(act1, 6))
     terms[0:96] = term[:, 0:128]
     terms[96:192] = term[:, 128:256]
     tail = term[0:24, 256:384]
@@ -283,33 +316,46 @@
         tail = tail + pltpu.roll(term[24 * i : 24 * i + 24, 256:384], 32 * i, 1)
     terms[192:216] = tail
     gx_all = jnp.concatenate([gx[i] for i in range(16)], axis=1).astype(BF16)
-    term = dot_nt(gx_all, windows(act2))
+    term = dot_nt(gx_all, windows(act2, 4))
     for i in range(3):
         terms[216 + 3 * i : 219 + 3 * i] = term[0:3, 128 * i : 128 * i + 128]
     wide = second[...]
     ok_rows = row_ok(6 * C, plane_at - 1, nh)
-    for z in range(6):
+    for z in range(8):
         y = jnp.concatenate([conv_mid_back(gm, wide, z, h) for h in range(6)], axis=0)
-        at = depth_at + (z - 1)
+        at = depth_at + (z - 2)
         ok = ok_rows & (at >= 0) & (at < nz)
         g = jnp.where(ok, y * slope1[z], 0.0).astype(BF16)
-        low[z] = g
-        if 1 <= z < 5:
-            inner = g[C : 5 * C].astype(F32)
-            low3[z - 1, 0] = from_right(inner).astype(BF16)
-            low3[z - 1, 1] = g[C : 5 * C]
-            low3[z - 1, 2] = from_left(inner).astype(BF16)
-    vc_all = jnp.concatenate([vc[i] for i in range(16)], axis=1)
-    rows = jnp.concatenate([shifted(low3), jnp.zeros((32, 16 * W), BF16)], axis=0)
+        low[z + 2] = g
+        inner = g[C : 5 * C].astype(F32)
+        low3[z, 0] = from_right(inner).astype(BF16)
+        low3[z, 1] = g[C : 5 * C]
+        low3[z, 2] = from_left(inner).astype(BF16)
+    vc_all = jnp.concatenate([vc[i] for i in range(32)], axis=1)
+    rows = jnp.concatenate([shifted(low3, 8), jnp.zeros((32, 32 * W), BF16)], axis=0)
     terms[225:234] = dot_nt(vc_all, rows)[0:9]
     terms_out[...] = terms[...].reshape(terms_out.shape).astype(BF16)
-    last = first[...]
-    for z in range(Z):
+    last = tail_of(first[...], True)
+    for z in range(10):
         for h in range(H):
-            volume_out[z, h : h + 1, :] = own[h, z : z + 1, :] + conv_last(low, last, z, h)
-
-
-def unpack_kernel(scale, sums, in_out, mid_out, out_out):
+            row = conv_last(low, last, z, h)
+            if z < 3:
+                before_out[z, h : h + 1, :] = row
+            elif z < 7:
+                volume_out[z - 3, h : h + 1, :] = own[h, z - 3 : z - 2, :] + row
+            else:
+                after_out[z - 7, h : h + 1, :] = row
+
+
+def sum_kernel(sums, out):
+    total = jnp.sum(sums[...].astype(F32), axis=0, keepdims=True)
+    out[...] = jnp.broadcast_to(total, out.shape).astype(BF16)
+
+
+def unpack_kernel(scale, sums, volume, before, after, volume_out, in_out, mid_out, out_out):
+    volume_out[0] = volume[0] + before[0]
+    volume_out[1:3] = volume[1:3] + before[1:3] + after[0:2]
+    volume_out[3] = volume[3] + after[2]
     full = sums[...].astype(F32).reshape(256, 128) * scale
     quarters = [full] + [pltpu.roll(full, 128 - 32 * j, 1) for j in range(1, 4)]
     last = jnp.concatenate([q[192:216, 0:C] for q in quarters], axis=0)
@@ -352,53 +398,41 @@
 
 
 def per_device(volume, cotangent, kernel_in, kernel_mid, kernel_out, measured, angle_ids, ray_bins):
-    depths, planes = lax.axis_size("depth"), lax.axis_size("plane")
-    depth_at, plane_at = lax.axis_index("depth"), lax.axis_index("plane")
+    depths, planes = lax.axis_size(DEPTH), lax.axis_size(PLANE)
+    near, far = lax.axis_size(NEAR), lax.axis_size(FAR)
+    depth_at, plane_at = lax.axis_index(DEPTH), lax.axis_index(PLANE)
     pos = jnp.stack([depth_at, plane_at]).astype(jnp.int32)
 
-    v_before, v_after = beside(volume, "depth")
+    v_before, v_after = beside(volume, DEPTH)
     pack = call(
         pack_kernel, [((36, H, W), BF16)], [], v_before, volume, v_after, cotangent, ray_bins
     )[0]
-    p_before, p_after = beside(pack, "plane")
-
-    in_k = kernel_in.reshape(3, 3, 3, C)
-    mid_k = kernel_mid.reshape(3, 3, 3, C, C)
-    out_k = kernel_out.reshape(3, 3, 3, C)
-    flip = lambda k: k[::-1, ::-1, ::-1]
-
-    def base(k):
-        t = jnp.pad(jnp.transpose(k, (3, 0, 2, 1)), ((0, 0), (0, 0), (0, 0), (0, 13)))
-        return jnp.pad(t.reshape(C, 144), ((0, 0), (0, 112))).astype(F32)
-
-    def tail(k):
-        t = jnp.transpose(k, (2, 0, 1, 3)).reshape(3, 9 * C)
-        return jnp.pad(t, ((0, 13), (0, 0)))
-
-    mid_forward = jnp.transpose(mid_k, (2, 3, 0, 1, 4)).reshape(3 * C, 9 * C)
-    mid_back = jnp.transpose(mid_k, (2, 4, 0, 1, 3)).reshape(3 * C, 9 * C)
+    p_before, p_after = beside(pack, PLANE)
+
+    mid_back = jnp.transpose(kernel_mid.reshape(3, 3, 3, C, C), (2, 4, 0, 1, 3))
+    mid_back = mid_back.reshape(3 * C, 9 * C)
 
     vc, act1, slope1, act2, slope2, rays = call(
         functools.partial(forward_kernel, depths, planes),
         [
-            ((16, 16, W), BF16),
+            ((32, 16, W), BF16),
+            ((8, 6 * C, W), BF16),
+            ((8, 6 * C, W), F32),
             ((6, 6 * C, W), BF16),
-            ((6, 6 * C, W), F32),
-            ((6, 6 * C, W), BF16),
-            ((8, 8 * C, W), F32),
+            ((6, 8 * C, W), F32),
             ((TILES, 3 * HI, 128), BF16),
         ],
         [
             ((12, 16, W), F32),
             ((12, 48, W), BF16),
-            ((16, 16, W), F32),
-            ((10, 10 * C, W), BF16),
+            ((32, 16, W), F32),
+            ((8, 10 * C, W), BF16),
             ((6, 6 * C, W), BF16),
         ],
-        pos, p_before, pack, p_after, base(in_k), mid_forward, tail(out_k), cotangent, ray_bins,
+        pos, p_before, pack, p_after, kernel_in, kernel_mid, kernel_out, cotangent, ray_bins,
     )
     each = TILES // planes
-    gathered = scatter_to(rays.reshape(planes, each * 3 * HI, 128), "plane")
+    gathered = scatter_to(rays.reshape(planes, each * 3 * HI, 128), PLANE)
     tiles = plane_at * each + jnp.arange(each)
     chosen = jnp.stack(
         [
@@ -412,60 +446,72 @@
         [],
         gathered, chosen,
     )[0]
-    weighted = scatter_to(spread, "plane").reshape(TILES, HI, 128)
+    weighted = scatter_to(spread, PLANE).reshape(TILES, HI, 128)
     slab, own = call(
         functools.partial(back_kernel, planes),
         [((12, Z, W), BF16), ((H, Z, W), F32)],
         [((12, Z, W), F32)],
         pos, weighted, p_before, pack, p_after, cotangent,
     )
-    s_before, s_after = beside(slab, "depth")
-    grad_volume, terms = call(
+    partial, before, after, terms = call(
         functools.partial(backward_kernel, depths, planes),
-        [((Z, H, W), F32), ((planes, 256 // planes, 128), BF16)],
         [
-            ((10, 16, W), F32),
-            ((10, 48, W), BF16),
+            ((Z, H, W), F32),
+            ((3, H, W), F32),
+            ((3, H, W), F32),
+            ((near, 256 // near, 128), BF16),
+        ],
+        [
+            ((8, 16, W), F32),
+            ((8, 48, W), BF16),
             ((16, 16, W), F32),
-            ((8, 8 * C, W), BF16),
-            ((4, 3, 4 * C, W), BF16),
-            ((6, 6 * C, W), BF16),
-            ((4, 3, 4 * C, W), BF16),
+            ((10, 8 * C, W), BF16),
+            ((6, 3, 4 * C, W), BF16),
+            ((12, 6 * C, W), BF16),
+            ((8, 3, 4 * C, W), BF16),
             ((256, 128), F32),
         ],
-        pos, s_before, slab, s_after, own, tail(flip(in_k)), mid_back, base(flip(out_k)),
-        vc, act1, slope1, act2, slope2,
-    )
-    def shared(cells, axis):
-        total = jnp.sum(cells.astype(F32), axis=0, keepdims=True).astype(BF16)
-        return scatter_to(jnp.broadcast_to(total, (lax.axis_size(axis),) + total.shape[1:]), axis)
-
-    sums = shared(shared(scatter_to(terms, "plane"), "depth"), "plane")
+        pos, slab, own, kernel_in, mid_back, kernel_out, vc, act1, slope1, act2, slope2,
+    )
+    got_before = lax.ppermute(after, DEPTH, [(i, i + 1) for i in range(depths - 1)])
+    got_after = lax.ppermute(before, DEPTH, [(i + 1, i) for i in range(depths - 1)])
+
+    def spread_sum(cells, count):
+        return call(sum_kernel, [((count,) + cells.shape[1:], BF16)], [], cells)[0]
+
+    sums = scatter_to(terms, NEAR)
+    sums = scatter_to(spread_sum(sums, far), FAR)
+    sums = scatter_to(spread_sum(sums, near), NEAR)
     cell_count = Z * depths * H * planes * W
-    got_in, got_mid, got_out = call(
+    grad_volume, got_in, got_mid, got_out = call(
         functools.partial(unpack_kernel, float(cell_count) ** (-0.5)),
-        [((27, C), F32), ((27, C, C), F32), ((27, C), F32)],
+        [((Z, H, W), F32), ((27, C), F32), ((27, C, C), F32), ((27, C), F32)],
         [],
-        sums,
+        sums, partial, got_before, got_after,
     )
     return (grad_volume, got_in, got_mid, got_out)
 
 
 def solution(mesh):
+    depths, planes = mesh.devices.shape
+    x = 4 if depths % 16 == 0 else 2
+    fine = Mesh(
+        mesh.devices.reshape(x, depths // x, 2, planes // 4, 2), DEPTH + PLANE
+    )
     placed = (
-        P("depth", "plane", None),
-        P("depth", "plane", None),
+        P(DEPTH, PLANE, None),
+        P(DEPTH, PLANE, None),
         P(),
         P(),
         P(),
-        P("depth", None, None),
+        P(DEPTH, None, None),
         P(),
-        P(None, "plane", None),
+        P(None, PLANE, None),
     )
     return jax.shard_map(
         per_device,
-        mesh=mesh,
+        mesh=fine,
         in_specs=placed,
-        out_specs=(P("depth", "plane", None), P(), P(), P()),
+        out_specs=(P(DEPTH, PLANE, None), P(), P(), P()),
         check_vma=False,
     )

time: 123 us -> 115 us (0.935)
  the two profiles are of different devices: /device:TPU:1 before, /device:TPU:2 now
where the time goes in v3:
time: 115 us; the launch traced here: 114 us
  starting transfers between devices  43.9 us (38%)
  blocking collectives  28.7 us (25%)
  waiting for transfers between devices  22.7 us (20%)
  Pallas kernels  11.6 us (10%)
  local copies, waits for them, and re-layouts  4.26 us (4%)
  between operations  2.82 us (2%)
    all_to_all x2, blocking collectives, scatter_to(): return lax.all_to_all(cells, axis, 0, 0, tiled=True)  28.7 us
    all_to_all x3, starting transfers between devices, scatter_to(): return lax.all_to_all(cells, axis, 0, 0, tiled=True)  19.5 us
    all_to_all x3, waiting for transfers between devices, scatter_to(): return lax.all_to_all(cells, axis, 0, 0, tiled=True)  15.5 us
    pallas_call x8, Pallas kernels, call(): pl.pallas_call(kernel, out_shape=[jax.ShapeDtypeStruct(s, d) for s, d in...  11.6 us
    ppermute x2, starting transfers between devices, beside(): after = lax.ppermute(cells, axis, [(i + 1, i) for i in range(count - 1)])  8.03 us
    ppermute x2, starting transfers between devices, beside(): before = lax.ppermute(cells, axis, [(i, i + 1) for i in range(count - 1)])  7.51 us
    ppermute x1, starting transfers between devices, per_device(): lax.ppermute(before, DEPTH, [(i + 1, i) for i in range(depths - 1)])  6.27 us
    ppermute x2, waiting for transfers between devices, beside(): after = lax.ppermute(cells, axis, [(i + 1, i) for i in range(count - 1)])  5.82 us
  transfers between devices with their start and end apart: 9, of which 5 were waited for; matrix products, arithmetic and copies ran while one was open for 2% of the time, Pallas kernels for 0%

profile of v3, /device:TPU:2, one launch (start us, length us, event | category | flops | bytes accessed | tf_op | source)
XLA Modules:
  0.0 113.9 jit_solution(5595454001875802727)
XLA Ops:
  0.6 0.0 copy-start
  0.6 6.2 %collective-permute-start = (bf16[4,4,128]{2,1,0:T(4,128)(2,1)}, bf16[4,4,128]{2,1,0:T(4,128)(2,1)S(1)}, u32[]{:S(2)}, u32[]{:S(2)}) collective-permute-start(bf16[4,4,128]{2,1,0:T(4,128)(2,1)} %own.1), channel_id=1, source_target_pairs={{0,32},{32,64},{64,96},{96,128},{128,160},{160,192},{192,224},{224... | collective-permute-start | bytes 12296 | tf_op jit(solution)/shard_map/ppermute | solution.py:391
  6.9 6.7 %collective-permute-start.1 = (bf16[4,4,128]{2,1,0:T(4,128)(2,1)}, bf16[4,4,128]{2,1,0:T(4,128)(2,1)S(1)}, u32[]{:S(2)}, u32[]{:S(2)}) collective-permute-start(bf16[4,4,128]{2,1,0:T(4,128)(2,1)} %own.1), channel_id=1, source_target_pairs={{32,0},{64,32},{96,64},{128,96},{160,128},{192,160},{224,192},{256... | collective-permute-start | bytes 12296 | tf_op jit(solution)/shard_map/ppermute | solution.py:392
  13.6 0.0 copy-start.4
  13.6 0.0 copy-start.3
  13.7 0.0 copy-start.7
  13.7 0.0 collective-permute-done.before
  13.7 2.3 %collective-permute-done.1.after = bf16[4,4,128]{2,1,0:T(4,128)(2,1)S(1)} collective-permute-done((bf16[4,4,128]{2,1,0:T(4,128)(2,1)}, bf16[4,4,128]{2,1,0:T(4,128)(2,1)S(1)}, u32[]{:S(2)}, u32[]{:S(2)}) %collective-permute-start.1) | collective-permute-done | bytes 4128 | tf_op jit(solution)/shard_map/ppermute | solution.py:392
  16.0 0.0 copy-done.4
  16.0 0.0 copy-done.3
  16.0 0.0 copy-done.7
  16.0 0.0 copy-start.5
  16.0 0.0 copy-start.6
  16.0 1.3 %collective-permute-start.2 = (bf16[36,4,128]{2,1,0:T(4,128)(2,1)S(1)}, bf16[36,4,128]{2,1,0:T(4,128)(2,1)S(1)}, u32[]{:S(2)}, u32[]{:S(2)}) collective-permute-start(bf16[36,4,128]{2,1,0:T(4,128)(2,1)S(1)} %shard_map.111.mid), channel_id=1, source_target_pairs={{0,1},{1,2},{2,3},{3,4},{4,5},{5,6},{6,7},{7,8},{8,9},{9,10},{10,1... | collective-permute-start | bytes 110600 | tf_op jit(solution)/shard_map/ppermute | solution.py:391
  17.3 1.3 %collective-permute-start.3 = (bf16[36,4,128]{2,1,0:T(4,128)(2,1)S(1)}, bf16[36,4,128]{2,1,0:T(4,128)(2,1)S(1)}, u32[]{:S(2)}, u32[]{:S(2)}) collective-permute-start(bf16[36,4,128]{2,1,0:T(4,128)(2,1)S(1)} %shard_map.111.mid), channel_id=1, source_target_pairs={{1,0},{2,1},{3,2},{4,3},{5,4},{6,5},{7,6},{8,7},{9,8},{10,9},{11,1... | collective-permute-start | bytes 110600 | tf_op jit(solution)/shard_map/ppermute | solution.py:392
  18.6 0.1 pad_add_fusion.pos
  18.7 0.0 collective-permute-done.2.lo
  18.7 3.5 %collective-permute-done.3.hi = bf16[36,4,128]{2,1,0:T(4,128)(2,1)S(1)} collective-permute-done((bf16[36,4,128]{2,1,0:T(4,128)(2,1)S(1)}, bf16[36,4,128]{2,1,0:T(4,128)(2,1)S(1)}, u32[]{:S(2)}, u32[]{:S(2)}) %collective-permute-start.3) | collective-permute-done | bytes 36896 | tf_op jit(solution)/shard_map/ppermute | solution.py:392
  22.2 0.0 copy-done.5
  22.2 0.0 copy-done.6
  22.2 0.0 copy-start.1
  22.2 0.9 copy-done.1
  23.2 4.2 %shard_map.112 = (bf16[32,16,128]{2,1,0:T(8,128)(2,1)S(1)}, bf16[8,192,128]{2,1,0:T(8,128)(2,1)S(1)}, f32[8,192,128]{2,1,0:T(8,128)S(1)}, bf16[6,192,128]{2,1,0:...) custom-call(s32[2]{0:T(128)S(1)} %pad_add_fusion.pos, ...), custom_call_target="tpu_custom_call" | custom-call | tf_op jit(solution)/shard_map/pallas_call | solution.py:379
  27.3 10.9 %all-to-all-start = ((bf16[32,24,128]{2,1,0:T(8,128)(2,1)}), bf16[32,24,128]{2,1,0:T(8,128)(2,1)S(1)}, u32[]{:S(2)}, u32[]{:S(2)}) async-start(bf16[32,24,128]{2,1,0:T(8,128)(2,1)} %get-tuple-element.16), calls=%async_computation | async-start | bytes 393216 | tf_op jit(solution)/shard_map/all_to_all | solution.py:397
  38.2 0.0 copy-start.8
  38.3 0.0 copy-start.2
  38.3 0.6 copy-done.8
  38.9 0.6 dynamic_slice.6
  41.4 0.0 copy-done
  41.5 8.6 %all-to-all-done.rays = bf16[32,24,128]{2,1,0:T(8,128)(2,1)S(1)} async-done(((bf16[32,24,128]{2,1,0:T(8,128)(2,1)}), bf16[32,24,128]{2,1,0:T(8,128)(2,1)S(1)}, u32[]{:S(2)}, u32[]{:S(2)}) %all-to-all-start) | async-done | bytes 196640 | tf_op jit(solution)/shard_map/all_to_all | solution.py:397
  50.0 0.7 shard_map.113
  50.7 3.8 %all-to-all-start.1 = ((bf16[32,8,128]{2,1,0:T(8,128)(2,1)}), bf16[32,8,128]{2,1,0:T(8,128)(2,1)S(1)}, u32[]{:S(2)}, u32[]{:S(2)}) async-start(bf16[32,8,128]{2,1,0:T(8,128)(2,1)} %shard_map.113), calls=%async_computation.1 | async-start | bytes 131072 | tf_op jit(solution)/shard_map/all_to_all | solution.py:397
  54.5 0.0 copy-done.2
  54.5 0.9 copy.13
  55.4 1.2 %reshape.15.second = bf16[96,288]{1,0:T(8,128)(2,1)S(1)} reshape(bf16[3,32,3,3,32]{4,3,2,1,0:T(4,128)(2,1)} %bitcast.8) | data formatting | bytes 110592 | tf_op jit(solution)/shard_map/reshape | solution.py:413
  56.6 7.0 %all-to-all-done.1.rays = bf16[32,8,128]{2,1,0:T(8,128)(2,1)S(1)} async-done(((bf16[32,8,128]{2,1,0:T(8,128)(2,1)}), bf16[32,8,128]{2,1,0:T(8,128)(2,1)S(1)}, u32[]{:S(2)}, u32[]{:S(2)}) %all-to-all-start.1) | async-done | bytes 65568 | tf_op jit(solution)/shard_map/all_to_all | solution.py:397
  63.6 1.1 shard_map.114
  64.7 4.0 %shard_map.115 = (f32[4,4,128]{2,1,0:T(4,128)S(1)}, f32[3,4,128]{2,1,0:T(4,128)S(1)}, f32[3,4,128]{2,1,0:T(4,128)S(1)}, bf16[16,16,128]{2,1,0:T(8,128)(2,1)S(1)}) custom-call(s32[2]{0:T(128)S(1)} %pad_add_fusion.pos, bf16[12,4,128]{2,1,0:T(4,128)(2,1)S(1)} %get-tuple-element.17.slab, f32[4,4,128]{2,1,0:T(4,128)S(1)} %get-tuple-element.18.own, ...), custom_call_target="tpu_custom_call" | custom-call | tf_op jit(solution)/shard_map/pallas_call | solution.py:379
  68.7 9.4 %all_to_all.25.sums = bf16[16,16,128]{2,1,0:T(8,128)(2,1)S(1)} all-to-all(bf16[16,16,128]{2,1,0:T(8,128)(2,1)S(1)} %get-tuple-element.24), channel_id=1, replica_groups=mesh['x'=4,'z_hi'=4,'z_lo'=2,'y'=8,'core'=2] {'x','z_lo','core'}, dimensions={0} | all-to-all | bytes 131072 | tf_op jit(solution)/shard_map/all_to_all | solution.py:397
  78.1 19.3 %all_to_all.26.sums = bf16[32,16,128]{2,1,0:T(8,128)(2,1)S(1)} all-to-all(bf16[32,16,128]{2,1,0:T(8,128)(2,1)S(1)} %shard_map.116), channel_id=1, replica_groups=mesh['x'=4,'z_hi'=4,'z_lo'=2,'y'=8,'core'=2] {'z_hi','y'}, dimensions={0} | all-to-all | bytes 262144 | tf_op jit(solution)/shard_map/all_to_all | solution.py:397
  97.4 0.7 shard_map.117
  98.0 4.8 %all-to-all-start.4 = ((bf16[16,16,128]{2,1,0:T(8,128)(2,1)}), bf16[16,16,128]{2,1,0:T(8,128)(2,1)S(1)}, u32[]{:S(2)}, u32[]{:S(2)}) async-start(bf16[16,16,128]{2,1,0:T(8,128)(2,1)} %shard_map.117), calls=%async_computation.4 | async-start | bytes 131072 | tf_op jit(solution)/shard_map/all_to_all | solution.py:397
  102.8 2.6 %collective-permute-start.4 = (f32[3,4,128]{2,1,0:T(4,128)S(1)}, f32[3,4,128]{2,1,0:T(4,128)S(1)}, u32[]{:S(2)}, u32[]{:S(2)}) collective-permute-start(f32[3,4,128]{2,1,0:T(4,128)S(1)} %get-tuple-element.26), channel_id=1, source_target_pairs={{0,32},{32,64},{64,96},{96,128},{128,160},{160,192},{192,224},{224... | collective-permute-start | bytes 18440 | tf_op jit(solution)/shard_map/ppermute | solution.py:476
  105.4 6.3 %collective-permute-start.5 = (f32[3,4,128]{2,1,0:T(4,128)S(1)}, f32[3,4,128]{2,1,0:T(4,128)S(1)}, u32[]{:S(2)}, u32[]{:S(2)}) collective-permute-start(f32[3,4,128]{2,1,0:T(4,128)S(1)} %get-tuple-element.27), channel_id=1, source_target_pairs={{32,0},{64,32},{96,64},{128,96},{160,128},{192,160},{224,192},{256... | collective-permute-start | bytes 18440 | tf_op jit(solution)/shard_map/ppermute | solution.py:477
  111.7 0.0 collective-permute-done.4.before
  111.7 1.3 %collective-permute-done.5.after = f32[3,4,128]{2,1,0:T(4,128)S(1)} collective-permute-done((f32[3,4,128]{2,1,0:T(4,128)S(1)}, f32[3,4,128]{2,1,0:T(4,128)S(1)}, u32[]{:S(2)}, u32[]{:S(2)}) %collective-permute-start.5) | collective-permute-done | bytes 6176 | tf_op jit(solution)/shard_map/ppermute | solution.py:477
  113.0 0.0 all-to-all-done.4.sums
  113.0 0.9 shard_map.118
  (3 shorter events, 0.1 us)
Async XLA Ops:
  0.6 40.8 %copy-start = (f32[4,32,1024]{2,1,0:T(8,128)S(1)}, f32[4,32,1024]{2,1,0:T(8,128)}, u32[]{:S(2)}) copy-start(f32[4,32,1024]{2,1,0:T(8,128)} %param.13) | copy-start | bytes 1572868
  0.6 13.0 %collective-permute-start = (bf16[4,4,128]{2,1,0:T(4,128)(2,1)}, bf16[4,4,128]{2,1,0:T(4,128)(2,1)S(1)}, u32[]{:S(2)}, u32[]{:S(2)}) collective-permute-start(bf16[4,4,128]{2,1,0:T(4,128)(2,1)} %own.1), channel_id=1, source_target_pairs={{0,32},{32,64},{64,96},{96,128},{128,160},{160,192},{192,224},{224... | collective-permute-start | bytes 12296 | tf_op jit(solution)/shard_map/ppermute | solution.py:391
  6.9 9.1 %collective-permute-start.1 = (bf16[4,4,128]{2,1,0:T(4,128)(2,1)}, bf16[4,4,128]{2,1,0:T(4,128)(2,1)S(1)}, u32[]{:S(2)}, u32[]{:S(2)}) collective-permute-start(bf16[4,4,128]{2,1,0:T(4,128)(2,1)} %own.1), channel_id=1, source_target_pairs={{32,0},{64,32},{96,64},{128,96},{160,128},{192,160},{224,192},{256... | collective-permute-start | bytes 12296 | tf_op jit(solution)/shard_map/ppermute | solution.py:392
  13.6 2.3 %copy-start.4 = (s32[8,4,128]{2,1,0:T(4,128)S(1)}, s32[8,4,128]{2,1,0:T(4,128)}, u32[]{:S(2)}) copy-start(s32[8,4,128]{2,1,0:T(4,128)} %bins.3) | copy-start | bytes 49156
  13.6 2.3 %copy-start.3 = (f32[4,4,128]{2,1,0:T(4,128)S(1)}, f32[4,4,128]{2,1,0:T(4,128)}, u32[]{:S(2)}) copy-start(f32[4,4,128]{2,1,0:T(4,128)} %cot.5) | copy-start | bytes 24580
  13.7 2.3 %copy-start.7 = (bf16[4,4,128]{2,1,0:T(4,128)(2,1)S(1)}, bf16[4,4,128]{2,1,0:T(4,128)(2,1)}, u32[]{:S(2)}) copy-start(bf16[4,4,128]{2,1,0:T(4,128)(2,1)} %own.1) | copy-start | bytes 12292
  16.0 6.3 %copy-start.5 = (bf16[27,32]{1,0:T(8,128)(2,1)S(1)}, bf16[27,32]{1,0:T(8,128)(2,1)}, u32[]{:S(2)}) copy-start(bf16[27,32]{1,0:T(8,128)(2,1)} %first.3) | copy-start | bytes 5188
  16.0 6.3 %copy-start.6 = (bf16[27,32]{1,0:T(8,128)(2,1)S(1)}, bf16[27,32]{1,0:T(8,128)(2,1)}, u32[]{:S(2)}) copy-start(bf16[27,32]{1,0:T(8,128)(2,1)} %third.3) | copy-start | bytes 5188
  16.0 2.7 %collective-permute-start.2 = (bf16[36,4,128]{2,1,0:T(4,128)(2,1)S(1)}, bf16[36,4,128]{2,1,0:T(4,128)(2,1)S(1)}, u32[]{:S(2)}, u32[]{:S(2)}) collective-permute-start(bf16[36,4,128]{2,1,0:T(4,128)(2,1)S(1)} %shard_map.111.mid), channel_id=1, source_target_pairs={{0,1},{1,2},{2,3},{3,4},{4,5},{5,6},{6,7},{7,8},{8,9},{9,10},{10,1... | collective-permute-start | bytes 110600 | tf_op jit(solution)/shard_map/ppermute | solution.py:391
  17.3 4.9 %collective-permute-start.3 = (bf16[36,4,128]{2,1,0:T(4,128)(2,1)S(1)}, bf16[36,4,128]{2,1,0:T(4,128)(2,1)S(1)}, u32[]{:S(2)}, u32[]{:S(2)}) collective-permute-start(bf16[36,4,128]{2,1,0:T(4,128)(2,1)S(1)} %shard_map.111.mid), channel_id=1, source_target_pairs={{1,0},{2,1},{3,2},{4,3},{5,4},{6,5},{7,6},{8,7},{9,8},{10,9},{11,1... | collective-permute-start | bytes 110600 | tf_op jit(solution)/shard_map/ppermute | solution.py:392
  22.2 0.9 copy-start.1
  27.3 22.7 %all-to-all-start = ((bf16[32,24,128]{2,1,0:T(8,128)(2,1)}), bf16[32,24,128]{2,1,0:T(8,128)(2,1)S(1)}, u32[]{:S(2)}, u32[]{:S(2)}) async-start(bf16[32,24,128]{2,1,0:T(8,128)(2,1)} %get-tuple-element.16), calls=%async_computation | async-start | bytes 393216 | tf_op jit(solution)/shard_map/all_to_all | solution.py:397
  38.2 0.7 copy-start.8
  38.3 16.3 %copy-start.2 = (bf16[27,32,32]{2,1,0:T(8,128)(2,1)S(1)}, bf16[27,32,32]{2,1,0:T(8,128)(2,1)}, u32[]{:S(2)}) copy-start(bf16[27,32,32]{2,1,0:T(8,128)(2,1)} %second.1) | copy-start | bytes 165892
  50.7 12.9 %all-to-all-start.1 = ((bf16[32,8,128]{2,1,0:T(8,128)(2,1)}), bf16[32,8,128]{2,1,0:T(8,128)(2,1)S(1)}, u32[]{:S(2)}, u32[]{:S(2)}) async-start(bf16[32,8,128]{2,1,0:T(8,128)(2,1)} %shard_map.113), calls=%async_computation.1 | async-start | bytes 131072 | tf_op jit(solution)/shard_map/all_to_all | solution.py:397
  98.0 14.9 %all-to-all-start.4 = ((bf16[16,16,128]{2,1,0:T(8,128)(2,1)}), bf16[16,16,128]{2,1,0:T(8,128)(2,1)S(1)}, u32[]{:S(2)}, u32[]{:S(2)}) async-start(bf16[16,16,128]{2,1,0:T(8,128)(2,1)} %shard_map.117), calls=%async_computation.4 | async-start | bytes 131072 | tf_op jit(solution)/shard_map/all_to_all | solution.py:397
  102.8 8.9 %collective-permute-start.4 = (f32[3,4,128]{2,1,0:T(4,128)S(1)}, f32[3,4,128]{2,1,0:T(4,128)S(1)}, u32[]{:S(2)}, u32[]{:S(2)}) collective-permute-start(f32[3,4,128]{2,1,0:T(4,128)S(1)} %get-tuple-element.26), channel_id=1, source_target_pairs={{0,32},{32,64},{64,96},{96,128},{128,160},{160,192},{192,224},{224... | collective-permute-start | bytes 18440 | tf_op jit(solution)/shard_map/ppermute | solution.py:476
  105.4 7.6 %collective-permute-start.5 = (f32[3,4,128]{2,1,0:T(4,128)S(1)}, f32[3,4,128]{2,1,0:T(4,128)S(1)}, u32[]{:S(2)}, u32[]{:S(2)}) collective-permute-start(f32[3,4,128]{2,1,0:T(4,128)S(1)} %get-tuple-element.27), channel_id=1, source_target_pairs={{32,0},{64,32},{96,64},{128,96},{160,128},{192,160},{224,192},{256... | collective-permute-start | bytes 18440 | tf_op jit(solution)/shard_map/ppermute | solution.py:477

commit v4 on v3

--- a/solution.py
+++ b/solution.py
@@ -5,7 +5,6 @@
 from jax import lax
 from jax.experimental import pallas as pl
 from jax.experimental.pallas import tpu as pltpu
-from jax.sharding import Mesh
 from jax.sharding import PartitionSpec as P
 
 BINS = 1024
@@ -19,10 +18,8 @@
 
 delta_scale = 6.0
 
-DEPTH = ("x", "z_hi")
-PLANE = ("z_lo", "y", "core")
-NEAR = ("x", "z_lo", "core")
-FAR = ("z_hi", "y")
+DEPTH = "depth"
+PLANE = "plane"
 F32 = jnp.float32
 BF16 = jnp.bfloat16
 
@@ -141,10 +138,35 @@
     return both[:n] + both[n:]
 
 
-def pack_kernel(before, own, after, cot, bins, out):
-    out[0:4] = before[...]
+def weights_kernel(first, second, third, first_out, wide_out, last_out,
+                   first_back, wide_back, last_back):
+    first_out[...] = banded(base_of(first[...], False), 10, 0)
+    first_back[...] = banded(base_of(third[...], True), 8, 1)
+    last_out[...] = tail_of(third[...], False)
+    last_back[...] = tail_of(first[...], True)
+    for ox in range(3):
+        blocks = [second[q * 3 + ox] for q in range(9)]
+        wide_out[ox * C : (ox + 1) * C, :] = jnp.concatenate(blocks, axis=1)
+        blocks = jnp.concatenate(blocks, axis=0).astype(F32)
+        wide_back[ox * C : (ox + 1) * C, :] = blocks.T.astype(BF16)
+
+
+def near_slot(pos, count, slots, step):
+    at = pos[0] + step
+    rows = slots[jnp.clip(at, 0, count - 1)].astype(F32)
+    return jnp.where((at >= 0) & (at < count), rows, 0.0)
+
+
+def in_order(at, first, second):
+    even = (at & 1) == 0
+    return jnp.where(even, second, first), jnp.where(even, first, second)
+
+
+def pack_kernel(pos, first, second, own, cot, bins, out):
+    before, after = in_order(pos[0], first[...].astype(F32), second[...].astype(F32))
+    out[0:4] = before.astype(BF16)
     out[4:8] = own[...]
-    out[8:12] = after[...]
+    out[8:12] = after.astype(BF16)
     head = cot[...].astype(BF16)
     out[12:16] = head
     out[16:20] = (cot[...] - head.astype(F32)).astype(BF16)
@@ -152,16 +174,17 @@
     out[28:36] = (bins[...] & 127).astype(F32).astype(BF16)
 
 
-def forward_kernel(depth_count, plane_count, pos, lo, mid, hi, first, second, third, cot, bins,
+def forward_kernel(depth_count, plane_count, pos, swap_a, swap_b, mid, first, second, third, cot, bins,
                    vc_out, act1_out, slope1_out, act2_out, slope2_out, rays_out,
                    vs, v3, vcs, a1, a2):
     depth_at = pos[0] * Z
     plane_at = pos[1] * H
     nz, nh = depth_count * Z, plane_count * H
     vs[...] = jnp.zeros_like(vs)
-    vs[:, 0:4, :] = lo[0:12].astype(F32)
+    lo, hi = in_order(pos[1], swap_a[0:12].astype(F32), swap_b[0:12].astype(F32))
+    vs[:, 0:4, :] = lo
     vs[:, 4:8, :] = mid[0:12].astype(F32)
-    vs[:, 8:12, :] = hi[0:12].astype(F32)
+    vs[:, 8:12, :] = hi
     three_shifts(v3, vs[...].reshape(12 * 16, W), 12)
     vcs[...] = jnp.zeros_like(vcs)
     for z in range(8):
@@ -169,7 +192,7 @@
             for oz in range(3):
                 vcs[z * H + h, oz * 3 : oz * 3 + 3, :] = vs[z + 1 + oz, h + 3 : h + 6, :]
     vc_out[...] = vcs[...].astype(BF16)
-    weights = banded(base_of(first[...], False), 10, 0)
+    weights = first[...]
     ok_rows = row_ok(10 * C, plane_at - 3, nh)
     for z in range(8):
         p = dot(weights, v3[z + 1 : z + 4].reshape(144, W))
@@ -180,10 +203,7 @@
         a1[z] = act
         act1_out[z] = act[2 * C : 8 * C]
         slope1_out[z] = (sigma * (1.0 + p * (1.0 - sigma)))[2 * C : 8 * C]
-    wide = jnp.concatenate(
-        [jnp.concatenate([second[q * 3 + ox] for q in range(9)], axis=1) for ox in range(3)],
-        axis=0,
-    )
+    wide = second[...]
     ok_rows = row_ok(8 * C, plane_at - 2, nh)
     for z in range(6):
         p = jnp.concatenate([conv_mid(a1, wide, z, h) for h in range(8)], axis=0)
@@ -194,7 +214,7 @@
         slope2_out[z] = sigma * (1.0 + p * (1.0 - sigma))
         a2[z] = act[C : 7 * C]
         act2_out[z] = act[C : 7 * C]
-    last = tail_of(third[...], False)
+    last = third[...]
     field = []
     for h in range(H):
         rows = []
@@ -224,10 +244,11 @@
         out[:, t * HI : (t + 1) * HI, :] = weighted.astype(BF16)
 
 
-def back_kernel(plane_count, pos, rays, lo, mid, hi, cot, slab_out, own_out, slab):
+def back_kernel(plane_count, pos, rays, swap_a, swap_b, mid, cot, slab_out, own_out, slab):
     plane_at = pos[1] * H
     nh = plane_count * H
-    packs = [p[12:36].astype(F32) for p in (lo, mid, hi)]
+    lo, hi = in_order(pos[1], swap_a[12:36].astype(F32), swap_b[12:36].astype(F32))
+    packs = [lo, mid[12:36].astype(F32), hi]
     at = lax.broadcasted_iota(jnp.int32, (HI, W), 0).astype(F32)
     spans = range(1, 11)
     total = [None] * len(spans)
@@ -258,8 +279,8 @@
 
 def backward_kernel(depth_count, plane_count, pos, slab, own, first, second, third,
                     vc, act1, slope1, act2, slope2,
-                    volume_out, before_out, after_out, terms_out,
-                    gs, v3, gx, gm, gm3, low, low3, terms):
+                    volume_out, terms_out,
+                    gs, v3, gx, gm, gm3, low, low3, terms, side):
     depth_at = pos[0] * Z
     plane_at = pos[1] * H
     nz, nh = depth_count * Z, plane_count * H
@@ -278,7 +299,7 @@
     edge = jnp.zeros((2, 6 * C, W), BF16)
     low[0:2] = edge
     low[10:12] = edge
-    weights = banded(base_of(third[...], True), 8, 1)
+    weights = third[...]
     ok_rows = row_ok(8 * C, plane_at - 2, nh)
     for z in range(6):
         y = dot(weights, v3[z : z + 3].reshape(144, W))
@@ -334,17 +355,42 @@
     vc_all = jnp.concatenate([vc[i] for i in range(32)], axis=1)
     rows = jnp.concatenate([shifted(low3, 8), jnp.zeros((32, 32 * W), BF16)], axis=0)
     terms[225:234] = dot_nt(vc_all, rows)[0:9]
-    terms_out[...] = terms[...].reshape(terms_out.shape).astype(BF16)
-    last = tail_of(first[...], True)
+    chunk = 256 // depth_count
+    terms_out[:, 0:chunk, :] = terms[...].reshape(depth_count, chunk, 128).astype(BF16)
+    terms_out[:, chunk : chunk + 16, :] = jnp.zeros((depth_count, 16, 128), BF16)
+    side[...] = jnp.zeros_like(side)
+    last = first[...]
     for z in range(10):
         for h in range(H):
             row = conv_last(low, last, z, h)
-            if z < 3:
-                before_out[z, h : h + 1, :] = row
-            elif z < 7:
+            if 3 <= z < 7:
                 volume_out[z - 3, h : h + 1, :] = own[h, z - 3 : z - 2, :] + row
             else:
-                after_out[z - 7, h : h + 1, :] = row
+                at = (z % 7) * H + h
+                side[z // 7, at : at + 1, :] = row
+
+    @pl.when(pos[0] > 0)
+    def _():
+        terms_out[pos[0] - 1, chunk : chunk + 16, :] = side[0].astype(BF16)
+
+    @pl.when(pos[0] < depth_count - 1)
+    def _():
+        terms_out[pos[0] + 1, chunk : chunk + 16, :] = side[1].astype(BF16)
+
+
+def first_sum_kernel(count, pos, slots, volume, out, volume_out):
+    chunk = 256 // count
+    total = jnp.sum(slots[:, 0:chunk, :].astype(F32), axis=0, keepdims=True)
+    out[...] = jnp.broadcast_to(total, out.shape).astype(BF16)
+    before = near_slot(pos, count, slots, -1)[chunk:]
+    after = near_slot(pos, count, slots, 1)[chunk:]
+    for z in range(Z):
+        rows = volume[z]
+        if z < 3:
+            rows = rows + before[z * H : (z + 1) * H]
+        if z > 0:
+            rows = rows + after[(z - 1) * H : z * H]
+        volume_out[z] = rows
 
 
 def sum_kernel(sums, out):
@@ -352,10 +398,7 @@
     out[...] = jnp.broadcast_to(total, out.shape).astype(BF16)
 
 
-def unpack_kernel(scale, sums, volume, before, after, volume_out, in_out, mid_out, out_out):
-    volume_out[0] = volume[0] + before[0]
-    volume_out[1:3] = volume[1:3] + before[1:3] + after[0:2]
-    volume_out[3] = volume[3] + after[2]
+def unpack_kernel(scale, sums, in_out, mid_out, out_out):
     full = sums[...].astype(F32).reshape(256, 128) * scale
     quarters = [full] + [pltpu.roll(full, 128 - 32 * j, 1) for j in range(1, 4)]
     last = jnp.concatenate([q[192:216, 0:C] for q in quarters], axis=0)
@@ -386,11 +429,11 @@
     )(*args)
 
 
-def beside(cells, axis):
+def swaps(cells, axis):
     count = lax.axis_size(axis)
-    before = lax.ppermute(cells, axis, [(i, i + 1) for i in range(count - 1)])
-    after = lax.ppermute(cells, axis, [(i + 1, i) for i in range(count - 1)])
-    return before, after
+    first = [(i, i ^ 1) for i in range(count)]
+    second = [(i, i + 1 if i % 2 else i - 1) for i in range(1, count - 1)]
+    return lax.ppermute(cells, axis, first), lax.ppermute(cells, axis, second)
 
 
 def scatter_to(cells, axis):
@@ -399,18 +442,30 @@
 
 def per_device(volume, cotangent, kernel_in, kernel_mid, kernel_out, measured, angle_ids, ray_bins):
     depths, planes = lax.axis_size(DEPTH), lax.axis_size(PLANE)
-    near, far = lax.axis_size(NEAR), lax.axis_size(FAR)
     depth_at, plane_at = lax.axis_index(DEPTH), lax.axis_index(PLANE)
     pos = jnp.stack([depth_at, plane_at]).astype(jnp.int32)
 
-    v_before, v_after = beside(volume, DEPTH)
+    v_first, v_second = swaps(volume, DEPTH)
+    first, wide, last, first_back, wide_back, last_back = call(
+        weights_kernel,
+        [
+            ((10 * C, 144), BF16),
+            ((3 * C, 9 * C), BF16),
+            ((16, 9 * C), BF16),
+            ((8 * C, 144), BF16),
+            ((3 * C, 9 * C), BF16),
+            ((16, 9 * C), BF16),
+        ],
+        [],
+        kernel_in, kernel_mid, kernel_out,
+    )
     pack = call(
-        pack_kernel, [((36, H, W), BF16)], [], v_before, volume, v_after, cotangent, ray_bins
+        pack_kernel,
+        [((36, H, W), BF16)],
+        [],
+        pos, v_first, v_second, volume, cotangent, ray_bins,
     )[0]
-    p_before, p_after = beside(pack, PLANE)
-
-    mid_back = jnp.transpose(kernel_mid.reshape(3, 3, 3, C, C), (2, 4, 0, 1, 3))
-    mid_back = mid_back.reshape(3 * C, 9 * C)
+    p_first, p_second = swaps(pack, PLANE)
 
     vc, act1, slope1, act2, slope2, rays = call(
         functools.partial(forward_kernel, depths, planes),
@@ -429,7 +484,7 @@
             ((8, 10 * C, W), BF16),
             ((6, 6 * C, W), BF16),
         ],
-        pos, p_before, pack, p_after, kernel_in, kernel_mid, kernel_out, cotangent, ray_bins,
+        pos, p_first, p_second, pack, first, wide, last, cotangent, ray_bins,
     )
     each = TILES // planes
     gathered = scatter_to(rays.reshape(planes, each * 3 * HI, 128), PLANE)
@@ -451,16 +506,11 @@
         functools.partial(back_kernel, planes),
         [((12, Z, W), BF16), ((H, Z, W), F32)],
         [((12, Z, W), F32)],
-        pos, weighted, p_before, pack, p_after, cotangent,
-    )
-    partial, before, after, terms = call(
+        pos, weighted, p_first, p_second, pack, cotangent,
+    )
+    partial, terms = call(
         functools.partial(backward_kernel, depths, planes),
-        [
-            ((Z, H, W), F32),
-            ((3, H, W), F32),
-            ((3, H, W), F32),
-            ((near, 256 // near, 128), BF16),
-        ],
+        [((Z, H, W), F32), ((depths, 256 // depths + 16, 128), BF16)],
         [
             ((8, 16, W), F32),
             ((8, 48, W), BF16),
@@ -470,34 +520,34 @@
             ((12, 6 * C, W), BF16),
             ((8, 3, 4 * C, W), BF16),
             ((256, 128), F32),
+            ((2, 16, W), F32),
         ],
-        pos, slab, own, kernel_in, mid_back, kernel_out, vc, act1, slope1, act2, slope2,
-    )
-    got_before = lax.ppermute(after, DEPTH, [(i, i + 1) for i in range(depths - 1)])
-    got_after = lax.ppermute(before, DEPTH, [(i + 1, i) for i in range(depths - 1)])
-
-    def spread_sum(cells, count):
-        return call(sum_kernel, [((count,) + cells.shape[1:], BF16)], [], cells)[0]
-
-    sums = scatter_to(terms, NEAR)
-    sums = scatter_to(spread_sum(sums, far), FAR)
-    sums = scatter_to(spread_sum(sums, near), NEAR)
+        pos, slab, own, last_back, wide_back, first_back, vc, act1, slope1, act2, slope2,
+    )
+    sums, grad_volume = call(
+        functools.partial(first_sum_kernel, depths),
+        [((planes, 256 // depths, 128), BF16), ((Z, H, W), F32)],
+        [],
+        pos, scatter_to(terms, DEPTH), partial,
+    )
+    sums = call(
+        sum_kernel,
+        [((depths, 256 // depths, 128), BF16)],
+        [],
+        scatter_to(sums, PLANE),
+    )[0]
+    sums = scatter_to(sums, DEPTH)
     cell_count = Z * depths * H * planes * W
-    grad_volume, got_in, got_mid, got_out = call(
+    got_in, got_mid, got_out = call(
         functools.partial(unpack_kernel, float(cell_count) ** (-0.5)),
-        [((Z, H, W), F32), ((27, C), F32), ((27, C, C), F32), ((27, C), F32)],
+        [((27, C), F32), ((27, C, C), F32), ((27, C), F32)],
         [],
-        sums, partial, got_before, got_after,
+        sums,
     )
     return (grad_volume, got_in, got_mid, got_out)
 
 
 def solution(mesh):
-    depths, planes = mesh.devices.shape
-    x = 4 if depths % 16 == 0 else 2
-    fine = Mesh(
-        mesh.devices.reshape(x, depths // x, 2, planes // 4, 2), DEPTH + PLANE
-    )
     placed = (
         P(DEPTH, PLANE, None),
         P(DEPTH, PLANE, None),
@@ -510,7 +560,7 @@
     )
     return jax.shard_map(
         per_device,
-        mesh=fine,
+        mesh=mesh,
         in_specs=placed,
         out_specs=(P(DEPTH, PLANE, None), P(), P(), P()),
         check_vma=False,

time: 115 us -> 115 us (level)
  the two profiles are of different devices: /device:TPU:2 before, /device:TPU:1 now
where the time goes in v4:
time: 115 us; the launch traced here: 114 us
  blocking collectives  64 us (56%)
  starting transfers between devices  22.9 us (20%)
  Pallas kernels  11.9 us (10%)
  waiting for transfers between devices  9.24 us (8%)
  local copies, waits for them, and re-layouts  3.09 us (3%)
  between operations  2.75 us (2%)
    all_to_all x4, blocking collectives, scatter_to(): return lax.all_to_all(cells, axis, 0, 0, tiled=True)  64 us
    ppermute x4, starting transfers between devices, swaps(): return (lax.ppermute(cells, axis, first), lax.ppermute(cells, axis, second))  16.7 us
    pallas_call x9, Pallas kernels, call(): pl.pallas_call(kernel, out_shape=[jax.ShapeDtypeStruct(s, d) for s, d in...  11.9 us
    all_to_all x1, waiting for transfers between devices, scatter_to(): return lax.all_to_all(cells, axis, 0, 0, tiled=True)  6.87 us
    all_to_all x1, starting transfers between devices, scatter_to(): return lax.all_to_all(cells, axis, 0, 0, tiled=True)  6.21 us
    unnamed x18, local copies, waits for them, and re-layouts  2.5 us
    ppermute x4, waiting for transfers between devices, swaps(): return (lax.ppermute(cells, axis, first), lax.ppermute(cells, axis, second))  2.37 us
  transfers between devices with their start and end apart: 5, of which 3 were waited for; matrix products, arithmetic and copies ran while one was open for 1% of the time, Pallas kernels for 0%

profile of v4, /device:TPU:1, one launch (start us, length us, event | category | flops | bytes accessed | tf_op | source)
XLA Modules:
  0.0 113.9 jit_solution(4433707873347126854)
XLA Ops:
  0.6 0.0 copy-start
  0.6 6.8 %collective-permute-start = (bf16[4,4,128]{2,1,0:T(4,128)(2,1)}, bf16[4,4,128]{2,1,0:T(4,128)(2,1)S(1)}, u32[]{:S(2)}, u32[]{:S(2)}) collective-permute-start(bf16[4,4,128]{2,1,0:T(4,128)(2,1)} %own.1), channel_id=1, source_target_pairs={{0,32},{32,0},{64,96},{96,64},{128,160},{160,128},{192,224},{224,1... | collective-permute-start | bytes 12296 | tf_op jit(solution)/shard_map/ppermute | solution.py:436
  7.4 0.7 collective-permute-start.1
  8.1 0.0 copy-start.2
  8.1 0.0 copy-start.7
  8.1 0.1 pad_add_fusion.pos
  8.2 0.4 collective-permute-done.first
  8.6 0.0 collective-permute-done.1.second
  8.6 0.2 copy-done.2
  8.8 0.0 copy-done.7
  8.8 0.0 copy-start.3
  8.8 0.7 copy-done.3
  9.5 0.0 copy-start.5
  9.5 0.0 copy-start.6
  9.5 0.6 shard_map.111.mid
  10.1 7.4 %collective-permute-start.2 = (bf16[36,4,128]{2,1,0:T(4,128)(2,1)S(1)}, bf16[36,4,128]{2,1,0:T(4,128)(2,1)S(1)}, u32[]{:S(2)}, u32[]{:S(2)}) collective-permute-start(bf16[36,4,128]{2,1,0:T(4,128)(2,1)S(1)} %shard_map.111.mid), channel_id=1, source_target_pairs={{0,1},{1,0},{2,3},{3,2},{4,5},{5,4},{6,7},{7,6},{8,9},{9,8},{10,11... | collective-permute-start | bytes 110600 | tf_op jit(solution)/shard_map/ppermute | solution.py:436
  17.4 1.9 %collective-permute-start.3 = (bf16[36,4,128]{2,1,0:T(4,128)(2,1)S(1)}, bf16[36,4,128]{2,1,0:T(4,128)(2,1)S(1)}, u32[]{:S(2)}, u32[]{:S(2)}) collective-permute-start(bf16[36,4,128]{2,1,0:T(4,128)(2,1)S(1)} %shard_map.111.mid), channel_id=1, source_target_pairs={{1,2},{2,1},{3,4},{4,3},{5,6},{6,5},{7,8},{8,7},{9,10},{10,9},{11,... | collective-permute-start | bytes 110600 | tf_op jit(solution)/shard_map/ppermute | solution.py:436
  19.4 0.0 copy-done.5
  19.4 0.0 copy-done.6
  19.4 0.0 copy-start.1
  19.4 0.9 copy-done.1
  20.3 0.0 copy-start.4
  20.3 0.4 shard_map.112
  20.8 0.0 collective-permute-done.2.swap_a
  20.8 1.9 %collective-permute-done.3.swap_b = bf16[36,4,128]{2,1,0:T(4,128)(2,1)S(1)} collective-permute-done((bf16[36,4,128]{2,1,0:T(4,128)(2,1)S(1)}, bf16[36,4,128]{2,1,0:T(4,128)(2,1)S(1)}, u32[]{:S(2)}, u32[]{:S(2)}) %collective-permute-start.3) | collective-permute-done | bytes 36896 | tf_op jit(solution)/shard_map/ppermute | solution.py:436
  22.7 0.0 copy-done.4
  22.7 3.9 %shard_map.113 = (bf16[32,16,128]{2,1,0:T(8,128)(2,1)S(1)}, bf16[8,192,128]{2,1,0:T(8,128)(2,1)S(1)}, f32[8,192,128]{2,1,0:T(8,128)S(1)}, bf16[6,192,128]{2,1,0:...) custom-call(s32[2]{0:T(128)S(1)} %pad_add_fusion.pos, ...), custom_call_target="tpu_custom_call" | custom-call | tf_op jit(solution)/shard_map/pallas_call | solution.py:422
  26.6 6.2 %all-to-all-start = ((bf16[32,24,128]{2,1,0:T(8,128)(2,1)}), bf16[32,24,128]{2,1,0:T(8,128)(2,1)S(1)}, u32[]{:S(2)}, u32[]{:S(2)}) async-start(bf16[32,24,128]{2,1,0:T(8,128)(2,1)} %get-tuple-element.28), calls=%async_computation | async-start | bytes 393216 | tf_op jit(solution)/shard_map/all_to_all | solution.py:440
  32.9 0.0 copy-start.8
  32.9 0.6 copy-done.8
  33.5 0.6 dynamic_slice.6
  36.1 0.0 copy-done
  36.1 6.9 %all-to-all-done.rays = bf16[32,24,128]{2,1,0:T(8,128)(2,1)S(1)} async-done(((bf16[32,24,128]{2,1,0:T(8,128)(2,1)}), bf16[32,24,128]{2,1,0:T(8,128)(2,1)S(1)}, u32[]{:S(2)}, u32[]{:S(2)}) %all-to-all-start) | async-done | bytes 196640 | tf_op jit(solution)/shard_map/all_to_all | solution.py:440
  43.0 0.1 shard_map.114
  43.0 12.7 %all_to_all.25.rays = bf16[32,8,128]{2,1,0:T(8,128)(2,1)S(1)} all-to-all(bf16[32,8,128]{2,1,0:T(8,128)(2,1)S(1)} %shard_map.114), channel_id=1, replica_groups=mesh['depth'=16,'plane'=32] {'plane'}, dimensions={0} | all-to-all | bytes 131072 | tf_op jit(solution)/shard_map/all_to_all | solution.py:440
  55.7 1.1 shard_map.115
  56.8 3.7 %shard_map.116 = (f32[4,4,128]{2,1,0:T(4,128)S(1)}, bf16[16,32,128]{2,1,0:T(8,128)(2,1)S(1)}) custom-call(s32[2]{0:T(128)S(1)} %pad_add_fusion.pos, bf16[12,4,128]{2,1,0:T(4,128)(2,1)S(1)} %get-tuple-element.29.slab, f32[4,4,128]{2,1,0:T(4,128)S(1)} %get-tuple-element.30.own, bf16[16,288]{1,0:T(8,128)(2,1)S(1)} %get-tuple-element.31.first, ...), custom_call_target="tpu_custom_call" | custom-call | tf_op jit(solution)/shard_map/pallas_call | solution.py:422
  60.5 25.7 %all_to_all.26.slots = bf16[16,32,128]{2,1,0:T(8,128)(2,1)S(1)} all-to-all(bf16[16,32,128]{2,1,0:T(8,128)(2,1)S(1)} %get-tuple-element.39), channel_id=1, replica_groups=mesh['depth'=16,'plane'=32] {'depth'}, dimensions={0} | all-to-all | bytes 262144 | tf_op jit(solution)/shard_map/all_to_all | solution.py:440
  86.2 1.2 %shard_map.117 = (bf16[32,16,128]{2,1,0:T(8,128)(2,1)S(1)}, f32[4,4,128]{2,1,0:T(4,128)}) custom-call(s32[2]{0:T(128)S(1)} %pad_add_fusion.pos, bf16[16,32,128]{2,1,0:T(8,128)(2,1)S(1)} %all_to_all.26.slots, f32[4,4,128]{2,1,0:T(4,128)S(1)} %get-tuple-element.40.volume), custom_call_target="tpu_custom_call" | custom-call | tf_op jit(solution)/shard_map/pallas_call | solution.py:422
  87.4 13.9 %all_to_all.27.sums = bf16[32,16,128]{2,1,0:T(8,128)(2,1)S(1)} all-to-all(bf16[32,16,128]{2,1,0:T(8,128)(2,1)S(1)} %get-tuple-element.42), channel_id=1, replica_groups=mesh['depth'=16,'plane'=32] {'plane'}, dimensions={0} | all-to-all | bytes 262144 | tf_op jit(solution)/shard_map/all_to_all | solution.py:440
  101.3 11.7 %all_to_all.28.sums = bf16[16,16,128]{2,1,0:T(8,128)(2,1)S(1)} all-to-all(bf16[16,16,128]{2,1,0:T(8,128)(2,1)S(1)} %shard_map.118), channel_id=1, replica_groups=mesh['depth'=16,'plane'=32] {'depth'}, dimensions={0} | all-to-all | bytes 131072 | tf_op jit(solution)/shard_map/all_to_all | solution.py:440
  113.0 0.9 shard_map.119
  (2 shorter events, 0.1 us)
Async XLA Ops:
  0.6 35.4 %copy-start = (f32[4,32,1024]{2,1,0:T(8,128)S(1)}, f32[4,32,1024]{2,1,0:T(8,128)}, u32[]{:S(2)}) copy-start(f32[4,32,1024]{2,1,0:T(8,128)} %param.13) | copy-start | bytes 1572868
  0.6 8.0 %collective-permute-start = (bf16[4,4,128]{2,1,0:T(4,128)(2,1)}, bf16[4,4,128]{2,1,0:T(4,128)(2,1)S(1)}, u32[]{:S(2)}, u32[]{:S(2)}) collective-permute-start(bf16[4,4,128]{2,1,0:T(4,128)(2,1)} %own.1), channel_id=1, source_target_pairs={{0,32},{32,0},{64,96},{96,64},{128,160},{160,128},{192,224},{224,1... | collective-permute-start | bytes 12296 | tf_op jit(solution)/shard_map/ppermute | solution.py:436
  7.4 1.2 %collective-permute-start.1 = (bf16[4,4,128]{2,1,0:T(4,128)(2,1)}, bf16[4,4,128]{2,1,0:T(4,128)(2,1)S(1)}, u32[]{:S(2)}, u32[]{:S(2)}) collective-permute-start(bf16[4,4,128]{2,1,0:T(4,128)(2,1)} %own.1), channel_id=1, source_target_pairs={{32,64},{64,32},{96,128},{128,96},{160,192},{192,160},{224,256},{2... | collective-permute-start | bytes 12296 | tf_op jit(solution)/shard_map/ppermute | solution.py:436
  8.1 0.7 copy-start.2
  8.1 0.7 copy-start.7
  8.8 0.7 copy-start.3
  9.5 9.9 %copy-start.5 = (bf16[27,32]{1,0:T(8,128)(2,1)S(1)}, bf16[27,32]{1,0:T(8,128)(2,1)}, u32[]{:S(2)}) copy-start(bf16[27,32]{1,0:T(8,128)(2,1)} %first.1) | copy-start | bytes 5188
  9.5 9.9 %copy-start.6 = (bf16[27,32]{1,0:T(8,128)(2,1)S(1)}, bf16[27,32]{1,0:T(8,128)(2,1)}, u32[]{:S(2)}) copy-start(bf16[27,32]{1,0:T(8,128)(2,1)} %third.1) | copy-start | bytes 5188
  10.1 10.7 %collective-permute-start.2 = (bf16[36,4,128]{2,1,0:T(4,128)(2,1)S(1)}, bf16[36,4,128]{2,1,0:T(4,128)(2,1)S(1)}, u32[]{:S(2)}, u32[]{:S(2)}) collective-permute-start(bf16[36,4,128]{2,1,0:T(4,128)(2,1)S(1)} %shard_map.111.mid), channel_id=1, source_target_pairs={{0,1},{1,0},{2,3},{3,2},{4,5},{5,4},{6,7},{7,6},{8,9},{9,8},{10,11... | collective-permute-start | bytes 110600 | tf_op jit(solution)/shard_map/ppermute | solution.py:436
  17.4 5.3 %collective-permute-start.3 = (bf16[36,4,128]{2,1,0:T(4,128)(2,1)S(1)}, bf16[36,4,128]{2,1,0:T(4,128)(2,1)S(1)}, u32[]{:S(2)}, u32[]{:S(2)}) collective-permute-start(bf16[36,4,128]{2,1,0:T(4,128)(2,1)S(1)} %shard_map.111.mid), channel_id=1, source_target_pairs={{1,2},{2,1},{3,4},{4,3},{5,6},{6,5},{7,8},{8,7},{9,10},{10,9},{11,... | collective-permute-start | bytes 110600 | tf_op jit(solution)/shard_map/ppermute | solution.py:436
  19.4 0.9 copy-start.1
  20.3 2.4 %copy-start.4 = (s32[8,4,128]{2,1,0:T(4,128)S(1)}, s32[8,4,128]{2,1,0:T(4,128)}, u32[]{:S(2)}) copy-start(s32[8,4,128]{2,1,0:T(4,128)} %bins.3) | copy-start | bytes 49156
  26.6 16.3 %all-to-all-start = ((bf16[32,24,128]{2,1,0:T(8,128)(2,1)}), bf16[32,24,128]{2,1,0:T(8,128)(2,1)S(1)}, u32[]{:S(2)}, u32[]{:S(2)}) async-start(bf16[32,24,128]{2,1,0:T(8,128)(2,1)} %get-tuple-element.28), calls=%async_computation | async-start | bytes 393216 | tf_op jit(solution)/shard_map/all_to_all | solution.py:440
  32.9 0.7 copy-start.8

commit v5 on v4

--- a/solution.py
+++ b/solution.py
@@ -120,15 +120,14 @@
     return y[1:2] + from_left(y[0:1]) + from_right(y[2:3])
 
 
-def project(field, bins_ref, a):
+def project(field, high, low):
     parts, lows = [], []
-    at = lax.broadcasted_iota(jnp.int32, (HI, W), 0)
+    at = lax.broadcasted_iota(jnp.int32, (HI, W), 0).astype(F32)
     for h in range(H):
-        bins = bins_ref[a, h : h + 1, :]
-        match = (bins >> 7) == at
+        match = high[h : h + 1, :] == at
         rows = [jnp.where(match, field[h][r : r + 1, :], 0.0) for r in range(field[h].shape[0])]
         parts.append(jnp.concatenate(rows, axis=0))
-        lows.append(low_match(bins & 127))
+        lows.append(low_match(low[h : h + 1, :]))
     part = jnp.concatenate(parts, axis=1)
     low = jnp.concatenate(lows, axis=1)
     head = part.astype(BF16)
@@ -138,8 +137,13 @@
     return both[:n] + both[n:]
 
 
-def weights_kernel(first, second, third, first_out, wide_out, last_out,
-                   first_back, wide_back, last_back):
+def local_kernel(cot, bins, first, second, third, pack_out, first_out, wide_out, last_out,
+                 first_back, wide_back, last_back):
+    head = cot[...].astype(BF16)
+    pack_out[0:4] = head
+    pack_out[4:8] = (cot[...] - head.astype(F32)).astype(BF16)
+    pack_out[8:16] = (bins[...] >> 7).astype(F32).astype(BF16)
+    pack_out[16:24] = (bins[...] & 127).astype(F32).astype(BF16)
     first_out[...] = banded(base_of(first[...], False), 10, 0)
     first_back[...] = banded(base_of(third[...], True), 8, 1)
     last_out[...] = tail_of(third[...], False)
@@ -162,19 +166,15 @@
     return jnp.where(even, second, first), jnp.where(even, first, second)
 
 
-def pack_kernel(pos, first, second, own, cot, bins, out):
+def pack_kernel(pos, first, second, own, local, out):
     before, after = in_order(pos[0], first[...].astype(F32), second[...].astype(F32))
     out[0:4] = before.astype(BF16)
     out[4:8] = own[...]
     out[8:12] = after.astype(BF16)
-    head = cot[...].astype(BF16)
-    out[12:16] = head
-    out[16:20] = (cot[...] - head.astype(F32)).astype(BF16)
-    out[20:28] = (bins[...] >> 7).astype(F32).astype(BF16)
-    out[28:36] = (bins[...] & 127).astype(F32).astype(BF16)
-
-
-def forward_kernel(depth_count, plane_count, pos, swap_a, swap_b, mid, first, second, third, cot, bins,
+    out[12:36] = local[...]
+
+
+def forward_kernel(depth_count, plane_count, pos, swap_a, swap_b, mid, first, second, third,
                    vc_out, act1_out, slope1_out, act2_out, slope2_out, rays_out,
                    vs, v3, vcs, a1, a2):
     depth_at = pos[0] * Z
@@ -215,6 +215,8 @@
         a2[z] = act[C : 7 * C]
         act2_out[z] = act[C : 7 * C]
     last = third[...]
+    local = mid[12:36].astype(F32)
+    cot = local[0:4] + local[4:8]
     field = []
     for h in range(H):
         rows = []
@@ -224,7 +226,7 @@
             rows.append(cot[z, h : h + 1, :])
         field.append(jnp.concatenate(rows, axis=0))
     for a in range(ANG):
-        tile = project(field, bins, a).reshape(2, Z, HI, 128)
+        tile = project(field, local[8 + a], local[16 + a]).reshape(2, Z, HI, 128)
         head = tile[0].astype(BF16).astype(F32)
         rows = jnp.concatenate([head, tile[0] - head, tile[1]], axis=1)
         rays_out[a * Z : (a + 1) * Z] = rows.astype(BF16)
@@ -378,12 +380,9 @@
         terms_out[pos[0] + 1, chunk : chunk + 16, :] = side[1].astype(BF16)
 
 
-def first_sum_kernel(count, pos, slots, volume, out, volume_out):
-    chunk = 256 // count
-    total = jnp.sum(slots[:, 0:chunk, :].astype(F32), axis=0, keepdims=True)
-    out[...] = jnp.broadcast_to(total, out.shape).astype(BF16)
-    before = near_slot(pos, count, slots, -1)[chunk:]
-    after = near_slot(pos, count, slots, 1)[chunk:]
+def unpack_kernel(scale, count, pos, sums, slots, volume, volume_out, in_out, mid_out, out_out):
+    before = near_slot(pos, count, slots, -1)[256 // count :]
+    after = near_slot(pos, count, slots, 1)[256 // count :]
     for z in range(Z):
         rows = volume[z]
         if z < 3:
@@ -391,14 +390,6 @@
         if z > 0:
             rows = rows + after[(z - 1) * H : z * H]
         volume_out[z] = rows
-
-
-def sum_kernel(sums, out):
-    total = jnp.sum(sums[...].astype(F32), axis=0, keepdims=True)
-    out[...] = jnp.broadcast_to(total, out.shape).astype(BF16)
-
-
-def unpack_kernel(scale, sums, in_out, mid_out, out_out):
     full = sums[...].astype(F32).reshape(256, 128) * scale
     quarters = [full] + [pltpu.roll(full, 128 - 32 * j, 1) for j in range(1, 4)]
     last = jnp.concatenate([q[192:216, 0:C] for q in quarters], axis=0)
@@ -446,9 +437,10 @@
     pos = jnp.stack([depth_at, plane_at]).astype(jnp.int32)
 
     v_first, v_second = swaps(volume, DEPTH)
-    first, wide, last, first_back, wide_back, last_back = call(
-        weights_kernel,
+    local, first, wide, last, first_back, wide_back, last_back = call(
+        local_kernel,
         [
+            ((24, H, W), BF16),
             ((10 * C, 144), BF16),
             ((3 * C, 9 * C), BF16),
             ((16, 9 * C), BF16),
@@ -457,14 +449,9 @@
             ((16, 9 * C), BF16),
         ],
         [],
-        kernel_in, kernel_mid, kernel_out,
-    )
-    pack = call(
-        pack_kernel,
-        [((36, H, W), BF16)],
-        [],
-        pos, v_first, v_second, volume, cotangent, ray_bins,
-    )[0]
+        cotangent, ray_bins, kernel_in, kernel_mid, kernel_out,
+    )
+    pack = call(pack_kernel, [((36, H, W), BF16)], [], pos, v_first, v_second, volume, local)[0]
     p_first, p_second = swaps(pack, PLANE)
 
     vc, act1, slope1, act2, slope2, rays = call(
@@ -484,7 +471,7 @@
             ((8, 10 * C, W), BF16),
             ((6, 6 * C, W), BF16),
         ],
-        pos, p_first, p_second, pack, first, wide, last, cotangent, ray_bins,
+        pos, p_first, p_second, pack, first, wide, last,
     )
     each = TILES // planes
     gathered = scatter_to(rays.reshape(planes, each * 3 * HI, 128), PLANE)
@@ -524,25 +511,21 @@
         ],
         pos, slab, own, last_back, wide_back, first_back, vc, act1, slope1, act2, slope2,
     )
-    sums, grad_volume = call(
-        functools.partial(first_sum_kernel, depths),
-        [((planes, 256 // depths, 128), BF16), ((Z, H, W), F32)],
+    chunk = 256 // depths
+
+    def spread_sum(cells, count):
+        total = jnp.sum(cells[:, :chunk].astype(F32), axis=0, keepdims=True).astype(BF16)
+        return jnp.broadcast_to(total, (count,) + total.shape[1:])
+
+    slots = scatter_to(terms, DEPTH)
+    sums = scatter_to(spread_sum(slots, planes), PLANE)
+    sums = scatter_to(spread_sum(sums, depths), DEPTH)
+    cell_count = Z * depths * H * planes * W
+    grad_volume, got_in, got_mid, got_out = call(
+        functools.partial(unpack_kernel, float(cell_count) ** (-0.5), depths),
+        [((Z, H, W), F32), ((27, C), F32), ((27, C, C), F32), ((27, C), F32)],
         [],
-        pos, scatter_to(terms, DEPTH), partial,
-    )
-    sums = call(
-        sum_kernel,
-        [((depths, 256 // depths, 128), BF16)],
-        [],
-        scatter_to(sums, PLANE),
-    )[0]
-    sums = scatter_to(sums, DEPTH)
-    cell_count = Z * depths * H * planes * W
-    got_in, got_mid, got_out = call(
-        functools.partial(unpack_kernel, float(cell_count) ** (-0.5)),
-        [((27, C), F32), ((27, C, C), F32), ((27, C), F32)],
-        [],
-        sums,
+        pos, sums, slots, partial,
     )
     return (grad_volume, got_in, got_mid, got_out)
 

time: 115 us -> 114 us (level)
  blocking collectives: 64 us -> 61.4 us
  local copies, waits for them, and re-layouts: 3.09 us -> 4.47 us
    ppermute x4, starting transfers between devices: 16.7 us -> 13.7 us  [swaps(): return (lax.ppermute(cells, axis, first), lax.ppermute(cells, axis, second))]
    all_to_all x1, starting transfers between devices: 6.21 us -> 8.84 us  [scatter_to(): return lax.all_to_all(cells, axis, 0, 0, tiled=True)]
    all_to_all x4, blocking collectives: 64 us -> 61.4 us  [scatter_to(): return lax.all_to_all(cells, axis, 0, 0, tiled=True)]
    unnamed x18 -> x16, local copies, waits for them, and re-layouts: 2.5 us -> 3.84 us
    pallas_call x9 -> x7, Pallas kernels: 11.9 us -> 11.1 us  [call(): pl.pallas_call(kernel, out_shape=[jax.ShapeDtypeStruct(s, d) for s, d in...]
  transfers between devices with their start and end apart: 5 -> 5, of which waited for: 3 -> 2; matrix products, arithmetic and copies ran while one was open for 1% -> 1% of each run, Pallas kernels for 0% -> 0%
where the time goes in v5:
time: 114 us; the launch traced here: 113 us
  blocking collectives  61.4 us (54%)
  starting transfers between devices  22.5 us (20%)
  Pallas kernels  11.1 us (10%)
  waiting for transfers between devices  10.2 us (9%)
  local copies, waits for them, and re-layouts  4.47 us (4%)
  between operations  2.75 us (2%)
    all_to_all x4, blocking collectives, scatter_to(): return lax.all_to_all(cells, axis, 0, 0, tiled=True)  61.4 us
    ppermute x4, starting transfers between devices, swaps(): return (lax.ppermute(cells, axis, first), lax.ppermute(cells, axis, second))  13.7 us
    pallas_call x7, Pallas kernels, call(): pl.pallas_call(kernel, out_shape=[jax.ShapeDtypeStruct(s, d) for s, d in...  11.1 us
    all_to_all x1, starting transfers between devices, scatter_to(): return lax.all_to_all(cells, axis, 0, 0, tiled=True)  8.84 us
    all_to_all x1, waiting for transfers between devices, scatter_to(): return lax.all_to_all(cells, axis, 0, 0, tiled=True)  6.87 us
    unnamed x16, local copies, waits for them, and re-layouts  3.84 us
    ppermute x4, waiting for transfers between devices, swaps(): return (lax.ppermute(cells, axis, first), lax.ppermute(cells, axis, second))  3.35 us
  transfers between devices with their start and end apart: 5, of which 2 were waited for; matrix products, arithmetic and copies ran while one was open for 1% of the time, Pallas kernels for 0%

profile of v5, /device:TPU:1, one launch (start us, length us, event | category | flops | bytes accessed | tf_op | source)
XLA Modules:
  0.0 112.6 jit_solution(10615893135312123539)
XLA Ops:
  0.6 0.0 copy-start
  0.6 6.8 %collective-permute-start = (bf16[4,4,128]{2,1,0:T(4,128)(2,1)}, bf16[4,4,128]{2,1,0:T(4,128)(2,1)S(1)}, u32[]{:S(2)}, u32[]{:S(2)}) collective-permute-start(bf16[4,4,128]{2,1,0:T(4,128)(2,1)} %own.1), channel_id=1, source_target_pairs={{0,32},{32,0},{64,96},{96,64},{128,160},{160,128},{192,224},{224,1... | collective-permute-start | bytes 12296 | tf_op jit(solution)/shard_map/ppermute | solution.py:427
  7.4 0.7 collective-permute-start.1
  8.1 0.0 copy-start.4
  8.1 0.0 copy-start.2
  8.1 0.1 pad_add_fusion.pos
  8.2 0.6 copy-done.4
  8.8 0.0 copy-done.2
  8.8 0.0 copy-start.1
  8.8 0.9 copy-done.1
  9.7 0.0 copy-start.3
  9.7 0.7 copy-done.3
  10.5 0.0 copy-start.5
  10.5 0.7 copy-done.5
  11.2 0.0 copy-start.6
  11.2 0.5 shard_map.111
  11.6 0.0 collective-permute-done.first
  11.6 0.0 collective-permute-done.1.second
  11.6 0.2 copy-done.6
  11.8 0.5 shard_map.112.mid
  12.4 4.3 %collective-permute-start.2 = (bf16[36,4,128]{2,1,0:T(4,128)(2,1)S(1)}, bf16[36,4,128]{2,1,0:T(4,128)(2,1)S(1)}, u32[]{:S(2)}, u32[]{:S(2)}) collective-permute-start(bf16[36,4,128]{2,1,0:T(4,128)(2,1)S(1)} %shard_map.112.mid), channel_id=1, source_target_pairs={{0,1},{1,0},{2,3},{3,2},{4,5},{5,4},{6,7},{7,6},{8,9},{9,8},{10,11... | collective-permute-start | bytes 110600 | tf_op jit(solution)/shard_map/ppermute | solution.py:427
  16.7 1.9 %collective-permute-start.3 = (bf16[36,4,128]{2,1,0:T(4,128)(2,1)S(1)}, bf16[36,4,128]{2,1,0:T(4,128)(2,1)S(1)}, u32[]{:S(2)}, u32[]{:S(2)}) collective-permute-start(bf16[36,4,128]{2,1,0:T(4,128)(2,1)S(1)} %shard_map.112.mid), channel_id=1, source_target_pairs={{1,2},{2,1},{3,4},{4,3},{5,6},{6,5},{7,8},{8,7},{9,10},{10,9},{11,... | collective-permute-start | bytes 110600 | tf_op jit(solution)/shard_map/ppermute | solution.py:427
  18.6 0.0 collective-permute-done.2.swap_a
  18.6 3.3 %collective-permute-done.3.swap_b = bf16[36,4,128]{2,1,0:T(4,128)(2,1)S(1)} collective-permute-done((bf16[36,4,128]{2,1,0:T(4,128)(2,1)S(1)}, bf16[36,4,128]{2,1,0:T(4,128)(2,1)S(1)}, u32[]{:S(2)}, u32[]{:S(2)}) %collective-permute-start.3) | collective-permute-done | bytes 36896 | tf_op jit(solution)/shard_map/ppermute | solution.py:427
  22.0 3.8 %shard_map.113 = (bf16[32,16,128]{2,1,0:T(8,128)(2,1)S(1)}, bf16[8,192,128]{2,1,0:T(8,128)(2,1)S(1)}, f32[8,192,128]{2,1,0:T(8,128)S(1)}, bf16[6,192,128]{2,1,0:...) custom-call(s32[2]{0:T(128)S(1)} %pad_add_fusion.pos, ...), custom_call_target="tpu_custom_call" | custom-call | tf_op jit(solution)/shard_map/pallas_call | solution.py:413
  25.8 8.8 %all-to-all-start = ((bf16[32,24,128]{2,1,0:T(8,128)(2,1)}), bf16[32,24,128]{2,1,0:T(8,128)(2,1)S(1)}, u32[]{:S(2)}, u32[]{:S(2)}) async-start(bf16[32,24,128]{2,1,0:T(8,128)(2,1)} %get-tuple-element.25), calls=%async_computation | async-start | bytes 393216 | tf_op jit(solution)/shard_map/all_to_all | solution.py:431
  34.7 0.0 copy-start.7
  34.7 0.6 copy-done.7
  35.3 0.6 dynamic_slice.6
  37.9 0.0 copy-done
  37.9 6.9 %all-to-all-done.rays = bf16[32,24,128]{2,1,0:T(8,128)(2,1)S(1)} async-done(((bf16[32,24,128]{2,1,0:T(8,128)(2,1)}), bf16[32,24,128]{2,1,0:T(8,128)(2,1)S(1)}, u32[]{:S(2)}, u32[]{:S(2)}) %all-to-all-start) | async-done | bytes 196640 | tf_op jit(solution)/shard_map/all_to_all | solution.py:431
  44.8 0.1 shard_map.114
  44.8 12.7 %all_to_all.25.rays = bf16[32,8,128]{2,1,0:T(8,128)(2,1)S(1)} all-to-all(bf16[32,8,128]{2,1,0:T(8,128)(2,1)S(1)} %shard_map.114), channel_id=1, replica_groups=mesh['depth'=16,'plane'=32] {'plane'}, dimensions={0} | all-to-all | bytes 131072 | tf_op jit(solution)/shard_map/all_to_all | solution.py:431
  57.5 1.1 shard_map.115
  58.6 3.7 %shard_map.116 = (f32[4,4,128]{2,1,0:T(4,128)S(1)}, bf16[16,32,128]{2,1,0:T(8,128)(2,1)S(1)}) custom-call(s32[2]{0:T(128)S(1)} %pad_add_fusion.pos, bf16[12,4,128]{2,1,0:T(4,128)(2,1)S(1)} %get-tuple-element.26.slab, f32[4,4,128]{2,1,0:T(4,128)S(1)} %get-tuple-element.27.own, bf16[16,288]{1,0:T(8,128)(2,1)S(1)} %get-tuple-element.28.first, ...), custom_call_target="tpu_custom_call" | custom-call | tf_op jit(solution)/shard_map/pallas_call | solution.py:413
  62.3 23.1 %all_to_all.26.slots = bf16[16,32,128]{2,1,0:T(8,128)(2,1)S(1)} all-to-all(bf16[16,32,128]{2,1,0:T(8,128)(2,1)S(1)} %get-tuple-element.36), channel_id=1, replica_groups=mesh['depth'=16,'plane'=32] {'depth'}, dimensions={0} | all-to-all | bytes 262144 | tf_op jit(solution)/shard_map/all_to_all | solution.py:431
  85.4 13.9 %all_to_all.27 = bf16[32,16,128]{2,1,0:T(8,128)(2,1)S(1)} all-to-all(bf16[32,16,128]{2,1,0:T(8,128)(2,1)S(1)} %broadcast_in_dim.4), channel_id=1, replica_groups=mesh['depth'=16,'plane'=32] {'plane'}, dimensions={0} | all-to-all | bytes 262144 | tf_op jit(solution)/shard_map/all_to_all | solution.py:431
  99.4 11.7 %all_to_all.28.sums = bf16[16,16,128]{2,1,0:T(8,128)(2,1)S(1)} all-to-all(bf16[16,16,128]{2,1,0:T(8,128)(2,1)S(1)} %broadcast_in_dim.5), channel_id=1, replica_groups=mesh['depth'=16,'plane'=32] {'depth'}, dimensions={0} | all-to-all | bytes 131072 | tf_op jit(solution)/shard_map/all_to_all | solution.py:431
  111.1 1.5 %shard_map.117 = (f32[4,4,128]{2,1,0:T(4,128)}, f32[27,32]{1,0:T(8,128)}, f32[27,32,32]{2,1,0:T(8,128)}, f32[27,32]{1,0:T(8,128)}) custom-call(s32[2]{0:T(128)S(1)} %pad_add_fusion.pos, bf16[16,16,128]{2,1,0:T(8,128)(2,1)S(1)} %all_to_all.28.sums, bf16[16,32,128]{2,1,0:T(8,128)(2,1)S(1)} %all_to_all.26.slots, f32[4,4,128]{2,1,0:T(4,128)S(1)} %get-tuple-element.37.volume), custom_call_target="tpu_custom_call" | custom-call | tf_op jit(solution)/shard_map/pallas_call | solution.py:413
  (5 shorter events, 0.1 us)
Async XLA Ops:
  0.6 37.2 %copy-start = (f32[4,32,1024]{2,1,0:T(8,128)S(1)}, f32[4,32,1024]{2,1,0:T(8,128)}, u32[]{:S(2)}) copy-start(f32[4,32,1024]{2,1,0:T(8,128)} %param.13) | copy-start | bytes 1572868
  0.6 11.0 %collective-permute-start = (bf16[4,4,128]{2,1,0:T(4,128)(2,1)}, bf16[4,4,128]{2,1,0:T(4,128)(2,1)S(1)}, u32[]{:S(2)}, u32[]{:S(2)}) collective-permute-start(bf16[4,4,128]{2,1,0:T(4,128)(2,1)} %own.1), channel_id=1, source_target_pairs={{0,32},{32,0},{64,96},{96,64},{128,160},{160,128},{192,224},{224,1... | collective-permute-start | bytes 12296 | tf_op jit(solution)/shard_map/ppermute | solution.py:427
  7.4 4.2 %collective-permute-start.1 = (bf16[4,4,128]{2,1,0:T(4,128)(2,1)}, bf16[4,4,128]{2,1,0:T(4,128)(2,1)S(1)}, u32[]{:S(2)}, u32[]{:S(2)}) collective-permute-start(bf16[4,4,128]{2,1,0:T(4,128)(2,1)} %own.1), channel_id=1, source_target_pairs={{32,64},{64,32},{96,128},{128,96},{160,192},{192,160},{224,256},{2... | collective-permute-start | bytes 12296 | tf_op jit(solution)/shard_map/ppermute | solution.py:427
  8.1 0.7 copy-start.4
  8.1 0.7 copy-start.2
  8.8 0.9 copy-start.1
  9.7 0.7 copy-start.3
  10.5 0.7 copy-start.5
  11.2 0.7 copy-start.6
  12.4 6.2 %collective-permute-start.2 = (bf16[36,4,128]{2,1,0:T(4,128)(2,1)S(1)}, bf16[36,4,128]{2,1,0:T(4,128)(2,1)S(1)}, u32[]{:S(2)}, u32[]{:S(2)}) collective-permute-start(bf16[36,4,128]{2,1,0:T(4,128)(2,1)S(1)} %shard_map.112.mid), channel_id=1, source_target_pairs={{0,1},{1,0},{2,3},{3,2},{4,5},{5,4},{6,7},{7,6},{8,9},{9,8},{10,11... | collective-permute-start | bytes 110600 | tf_op jit(solution)/shard_map/ppermute | solution.py:427
  16.7 5.3 %collective-permute-start.3 = (bf16[36,4,128]{2,1,0:T(4,128)(2,1)S(1)}, bf16[36,4,128]{2,1,0:T(4,128)(2,1)S(1)}, u32[]{:S(2)}, u32[]{:S(2)}) collective-permute-start(bf16[36,4,128]{2,1,0:T(4,128)(2,1)S(1)} %shard_map.112.mid), channel_id=1, source_target_pairs={{1,2},{2,1},{3,4},{4,3},{5,6},{6,5},{7,8},{8,7},{9,10},{10,9},{11,... | collective-permute-start | bytes 110600 | tf_op jit(solution)/shard_map/ppermute | solution.py:427
  25.8 19.0 %all-to-all-start = ((bf16[32,24,128]{2,1,0:T(8,128)(2,1)}), bf16[32,24,128]{2,1,0:T(8,128)(2,1)S(1)}, u32[]{:S(2)}, u32[]{:S(2)}) async-start(bf16[32,24,128]{2,1,0:T(8,128)(2,1)} %get-tuple-element.25), calls=%async_computation | async-start | bytes 393216 | tf_op jit(solution)/shard_map/all_to_all | solution.py:431
  34.7 0.7 copy-start.7

commit v6 on v5

--- a/solution.py
+++ b/solution.py
@@ -76,7 +76,7 @@
     lane = lanes_of((16, 27))
     lane = 26 - lane if flip else lane
     pick = lane % 3 == lax.broadcasted_iota(jnp.int32, (16, 27), 0)
-    return dot(jnp.where(pick, 1.0, 0.0).astype(BF16), wide).astype(BF16)
+    return banded_tail(dot(jnp.where(pick, 1.0, 0.0).astype(BF16), wide))
 
 
 def triple(ref, z, start, size):
@@ -96,40 +96,72 @@
     return jnp.where(low_row == at, 1.0, 0.0).astype(BF16)
 
 
-def conv_mid(ref, weights, z, row):
-    x = triple(ref, z, row * C, 3 * C)
-    y = dot(weights, x)
-    return y[C : 2 * C] + from_left(y[0:C]) + from_right(y[2 * C :])
-
-
-def conv_mid_back(ref, weights, z, row):
-    x = jnp.concatenate(
-        [
-            ref[z + 2 - oz, (row + 2 - oy) * C : (row + 3 - oy) * C, :]
-            for oz in range(3)
-            for oy in range(3)
-        ],
-        axis=0,
-    )
-    y = dot(weights, x)
-    return y[C : 2 * C] + from_right(y[0:C]) + from_left(y[2 * C :])
-
-
-def conv_last(ref, weights, z, row):
-    y = dot(weights, triple(ref, z, row * C, 3 * C))
-    return y[1:2] + from_left(y[0:1]) + from_right(y[2:3])
+def join(y):
+    n = y.shape[0] // 3
+    return y[n : 2 * n] + from_left(y[0:n]) + from_right(y[2 * n :])
+
+
+def pairs(weights, windows):
+    out = []
+    for i in range(0, len(windows), 2):
+        y = dot(weights, jnp.concatenate(windows[i : i + 2], axis=1))
+        out += [y[:, :W], y[:, W:]]
+    return out
+
+
+def conv_mid(ref, weights, z, count):
+    ys = pairs(weights, [triple(ref, z, h * C, 3 * C) for h in range(count)])
+    return jnp.concatenate([join(y) for y in ys], axis=0)
+
+
+def conv_mid_back(ref, weights, z, count):
+    windows = [
+        jnp.concatenate(
+            [
+                ref[z + 2 - oz, (row + 2 - oy) * C : (row + 3 - oy) * C, :]
+                for oz in range(3)
+                for oy in range(3)
+            ],
+            axis=0,
+        )
+        for row in range(count)
+    ]
+    ys = pairs(weights, windows)
+    return jnp.concatenate(
+        [y[C : 2 * C] + from_right(y[0:C]) + from_left(y[2 * C :]) for y in ys], axis=0
+    )
+
+
+def conv_last(ref, weights, slices):
+    ys = pairs(weights, [triple(ref, z, 0, 6 * C) for z in range(slices)])
+    return [join(y) for y in ys]
+
+
+def banded_tail(tail):
+    moved = []
+    for h in range(H):
+        parts = []
+        for oz in range(3):
+            if h:
+                parts.append(jnp.zeros((16, C * h), F32))
+            parts.append(tail[:, 96 * oz : 96 * oz + 96])
+            if h < 3:
+                parts.append(jnp.zeros((16, 96 - C * h), F32))
+        moved.append(jnp.concatenate(parts, axis=1))
+    rows = []
+    for ox in range(3):
+        rows += [m[ox : ox + 1] for m in moved] + [jnp.zeros((8 - H, 18 * C), F32)]
+    return jnp.concatenate(rows, axis=0).astype(BF16)
 
 
 def project(field, high, low):
-    parts, lows = [], []
+    parts = []
     at = lax.broadcasted_iota(jnp.int32, (HI, W), 0).astype(F32)
     for h in range(H):
         match = high[h : h + 1, :] == at
         rows = [jnp.where(match, field[h][r : r + 1, :], 0.0) for r in range(field[h].shape[0])]
         parts.append(jnp.concatenate(rows, axis=0))
-        lows.append(low_match(low[h : h + 1, :]))
     part = jnp.concatenate(parts, axis=1)
-    low = jnp.concatenate(lows, axis=1)
     head = part.astype(BF16)
     rest = (part - head.astype(F32)).astype(BF16)
     n = part.shape[0]
@@ -137,13 +169,16 @@
     return both[:n] + both[n:]
 
 
-def local_kernel(cot, bins, first, second, third, pack_out, first_out, wide_out, last_out,
+def local_kernel(cot, bins, first, second, third, pack_out, lows_out, first_out, wide_out, last_out,
                  first_back, wide_back, last_back):
     head = cot[...].astype(BF16)
     pack_out[0:4] = head
     pack_out[4:8] = (cot[...] - head.astype(F32)).astype(BF16)
     pack_out[8:16] = (bins[...] >> 7).astype(F32).astype(BF16)
     pack_out[16:24] = (bins[...] & 127).astype(F32).astype(BF16)
+    for a in range(ANG):
+        for h in range(H):
+            lows_out[a, :, h * W : (h + 1) * W] = low_match(bins[a, h : h + 1, :] & 127)
     first_out[...] = banded(base_of(first[...], False), 10, 0)
     first_back[...] = banded(base_of(third[...], True), 8, 1)
     last_out[...] = tail_of(third[...], False)
@@ -174,7 +209,7 @@
     out[12:36] = local[...]
 
 
-def forward_kernel(depth_count, plane_count, pos, swap_a, swap_b, mid, first, second, third,
+def forward_kernel(depth_count, plane_count, pos, swap_a, swap_b, mid, lows, first, second, third,
                    vc_out, act1_out, slope1_out, act2_out, slope2_out, rays_out,
                    vs, v3, vcs, a1, a2):
     depth_at = pos[0] * Z
@@ -194,8 +229,9 @@
     vc_out[...] = vcs[...].astype(BF16)
     weights = first[...]
     ok_rows = row_ok(10 * C, plane_at - 3, nh)
+    ps = pairs(weights, [v3[z + 1 : z + 4].reshape(144, W) for z in range(8)])
     for z in range(8):
-        p = dot(weights, v3[z + 1 : z + 4].reshape(144, W))
+        p = ps[z]
         sigma = jax.nn.sigmoid(p)
         at = depth_at + (z - 2)
         ok = ok_rows & (at >= 0) & (at < nz)
@@ -206,7 +242,7 @@
     wide = second[...]
     ok_rows = row_ok(8 * C, plane_at - 2, nh)
     for z in range(6):
-        p = jnp.concatenate([conv_mid(a1, wide, z, h) for h in range(8)], axis=0)
+        p = conv_mid(a1, wide, z, 8)
         sigma = jax.nn.sigmoid(p)
         at = depth_at + (z - 1)
         ok = ok_rows & (at >= 0) & (at < nz)
@@ -218,15 +254,14 @@
     local = mid[12:36].astype(F32)
     cot = local[0:4] + local[4:8]
     field = []
+    dens = [vs[z + 4, 4:8, :] - y[0:H] for z, y in enumerate(conv_last(a2, last, Z))]
     for h in range(H):
-        rows = []
-        for z in range(Z):
-            rows.append(vs[z + 4, h + 4 : h + 5, :] - conv_last(a2, last, z, h))
+        rows = [den[h : h + 1] for den in dens]
         for z in range(Z):
             rows.append(cot[z, h : h + 1, :])
         field.append(jnp.concatenate(rows, axis=0))
     for a in range(ANG):
-        tile = project(field, local[8 + a], local[16 + a]).reshape(2, Z, HI, 128)
+        tile = project(field, local[8 + a], lows[a]).reshape(2, Z, HI, 128)
         head = tile[0].astype(BF16).astype(F32)
         rows = jnp.concatenate([head, tile[0] - head, tile[1]], axis=1)
         rays_out[a * Z : (a + 1) * Z] = rows.astype(BF16)
@@ -303,8 +338,9 @@
     low[10:12] = edge
     weights = third[...]
     ok_rows = row_ok(8 * C, plane_at - 2, nh)
+    ys = pairs(weights, [v3[z : z + 3].reshape(144, W) for z in range(6)])
     for z in range(6):
-        y = dot(weights, v3[z : z + 3].reshape(144, W))
+        y = ys[z]
         at = depth_at + (z - 1)
         ok = ok_rows & (at >= 0) & (at < nz)
         g = jnp.where(ok, y * slope2[z], 0.0).astype(BF16)
@@ -345,7 +381,7 @@
     wide = second[...]
     ok_rows = row_ok(6 * C, plane_at - 1, nh)
     for z in range(8):
-        y = jnp.concatenate([conv_mid_back(gm, wide, z, h) for h in range(6)], axis=0)
+        y = conv_mid_back(gm, wide, z, 6)
         at = depth_at + (z - 2)
         ok = ok_rows & (at >= 0) & (at < nz)
         g = jnp.where(ok, y * slope1[z], 0.0).astype(BF16)
@@ -362,14 +398,12 @@
     terms_out[:, chunk : chunk + 16, :] = jnp.zeros((depth_count, 16, 128), BF16)
     side[...] = jnp.zeros_like(side)
     last = first[...]
-    for z in range(10):
-        for h in range(H):
-            row = conv_last(low, last, z, h)
-            if 3 <= z < 7:
-                volume_out[z - 3, h : h + 1, :] = own[h, z - 3 : z - 2, :] + row
-            else:
-                at = (z % 7) * H + h
-                side[z // 7, at : at + 1, :] = row
+    for z, y in enumerate(conv_last(low, last, 10)):
+        if 3 <= z < 7:
+            volume_out[z - 3] = own[:, z - 3, :] + y[0:H]
+        else:
+            at = (z % 7) * H
+            side[z // 7, at : at + H, :] = y[0:H]
 
     @pl.when(pos[0] > 0)
     def _():
@@ -437,16 +471,17 @@
     pos = jnp.stack([depth_at, plane_at]).astype(jnp.int32)
 
     v_first, v_second = swaps(volume, DEPTH)
-    local, first, wide, last, first_back, wide_back, last_back = call(
+    local, lows, first, wide, last, first_back, wide_back, last_back = call(
         local_kernel,
         [
             ((24, H, W), BF16),
+            ((ANG, 128, H * W), BF16),
             ((10 * C, 144), BF16),
             ((3 * C, 9 * C), BF16),
-            ((16, 9 * C), BF16),
+            ((24, 18 * C), BF16),
             ((8 * C, 144), BF16),
             ((3 * C, 9 * C), BF16),
-            ((16, 9 * C), BF16),
+            ((24, 18 * C), BF16),
         ],
         [],
         cotangent, ray_bins, kernel_in, kernel_mid, kernel_out,
@@ -471,7 +506,7 @@
             ((8, 10 * C, W), BF16),
             ((6, 6 * C, W), BF16),
         ],
-        pos, p_first, p_second, pack, first, wide, last,
+        pos, p_first, p_second, pack, lows, first, wide, last,
     )
     each = TILES // planes
     gathered = scatter_to(rays.reshape(planes, each * 3 * HI, 128), PLANE)

time: 114 us -> 113 us (level)
  transfers between devices with their start and end apart: 5 -> 5, of which waited for: 2 -> 2; matrix products, arithmetic and copies ran while one was open for 1% -> 1% of each run, Pallas kernels for 0% -> 1%
where the time goes in v6:
time: 113 us; the launch traced here: 112 us
  blocking collectives  61.3 us (54%)
  starting transfers between devices  22.5 us (20%)
  Pallas kernels  10.5 us (9%)
  waiting for transfers between devices  10.2 us (9%)
  local copies, waits for them, and re-layouts  4.26 us (4%)
  between operations  2.77 us (2%)
    all_to_all x4, blocking collectives, scatter_to(): return lax.all_to_all(cells, axis, 0, 0, tiled=True)  61.3 us
    ppermute x4, starting transfers between devices, swaps(): return (lax.ppermute(cells, axis, first), lax.ppermute(cells, axis, second))  13.5 us
    pallas_call x7, Pallas kernels, call(): pl.pallas_call(kernel, out_shape=[jax.ShapeDtypeStruct(s, d) for s, d in...  10.5 us
    all_to_all x1, starting transfers between devices, scatter_to(): return lax.all_to_all(cells, axis, 0, 0, tiled=True)  8.95 us
    all_to_all x1, waiting for transfers between devices, scatter_to(): return lax.all_to_all(cells, axis, 0, 0, tiled=True)  6.87 us
    unnamed x16, local copies, waits for them, and re-layouts  3.63 us
    ppermute x4, waiting for transfers between devices, swaps(): return (lax.ppermute(cells, axis, first), lax.ppermute(cells, axis, second))  3.35 us
  transfers between devices with their start and end apart: 5, of which 2 were waited for; matrix products, arithmetic and copies ran while one was open for 1% of the time, Pallas kernels for 1%

profile of v6, /device:TPU:1, one launch (start us, length us, event | category | flops | bytes accessed | tf_op | source)
XLA Modules:
  0.0 111.6 jit_solution(11533259646109124570)
XLA Ops:
  0.6 0.0 copy-start
  0.6 6.8 %collective-permute-start = (bf16[4,4,128]{2,1,0:T(4,128)(2,1)}, bf16[4,4,128]{2,1,0:T(4,128)(2,1)S(1)}, u32[]{:S(2)}, u32[]{:S(2)}) collective-permute-start(bf16[4,4,128]{2,1,0:T(4,128)(2,1)} %own.1), channel_id=1, source_target_pairs={{0,32},{32,0},{64,96},{96,64},{128,160},{160,128},{192,224},{224,1... | collective-permute-start | bytes 12296 | tf_op jit(solution)/shard_map/ppermute | solution.py:461
  7.4 0.7 collective-permute-start.1
  8.1 0.0 copy-start.4
  8.1 0.0 copy-start.2
  8.1 0.1 pad_add_fusion.pos
  8.2 0.6 copy-done.4
  8.8 0.0 copy-done.2
  8.8 0.0 copy-start.1
  8.8 0.9 copy-done.1
  9.7 0.0 copy-start.3
  9.7 0.7 copy-done.3
  10.5 0.0 copy-start.5
  10.5 0.7 copy-done.5
  11.2 0.0 copy-start.6
  11.2 0.8 shard_map.111
  11.9 0.0 collective-permute-done.first
  11.9 0.0 collective-permute-done.1.second
  11.9 0.0 copy-done.6
  11.9 0.6 shard_map.112.mid
  12.5 4.2 %collective-permute-start.2 = (bf16[36,4,128]{2,1,0:T(4,128)(2,1)S(1)}, bf16[36,4,128]{2,1,0:T(4,128)(2,1)S(1)}, u32[]{:S(2)}, u32[]{:S(2)}) collective-permute-start(bf16[36,4,128]{2,1,0:T(4,128)(2,1)S(1)} %shard_map.112.mid), channel_id=1, source_target_pairs={{0,1},{1,0},{2,3},{3,2},{4,5},{5,4},{6,7},{7,6},{8,9},{9,8},{10,11... | collective-permute-start | bytes 110600 | tf_op jit(solution)/shard_map/ppermute | solution.py:461
  16.7 1.9 %collective-permute-start.3 = (bf16[36,4,128]{2,1,0:T(4,128)(2,1)S(1)}, bf16[36,4,128]{2,1,0:T(4,128)(2,1)S(1)}, u32[]{:S(2)}, u32[]{:S(2)}) collective-permute-start(bf16[36,4,128]{2,1,0:T(4,128)(2,1)S(1)} %shard_map.112.mid), channel_id=1, source_target_pairs={{1,2},{2,1},{3,4},{4,3},{5,6},{6,5},{7,8},{8,7},{9,10},{10,9},{11,... | collective-permute-start | bytes 110600 | tf_op jit(solution)/shard_map/ppermute | solution.py:461
  18.6 0.0 collective-permute-done.2.swap_a
  18.6 3.3 %collective-permute-done.3.swap_b = bf16[36,4,128]{2,1,0:T(4,128)(2,1)S(1)} collective-permute-done((bf16[36,4,128]{2,1,0:T(4,128)(2,1)S(1)}, bf16[36,4,128]{2,1,0:T(4,128)(2,1)S(1)}, u32[]{:S(2)}, u32[]{:S(2)}) %collective-permute-start.3) | collective-permute-done | bytes 36896 | tf_op jit(solution)/shard_map/ppermute | solution.py:461
  22.0 3.3 %shard_map.113 = (bf16[32,16,128]{2,1,0:T(8,128)(2,1)S(1)}, bf16[8,192,128]{2,1,0:T(8,128)(2,1)S(1)}, f32[8,192,128]{2,1,0:T(8,128)S(1)}, bf16[6,192,128]{2,1,0:...) custom-call(s32[2]{0:T(128)S(1)} %pad_add_fusion.pos, ...), custom_call_target="tpu_custom_call" | custom-call | tf_op jit(solution)/shard_map/pallas_call | solution.py:447
  25.3 8.9 %all-to-all-start = ((bf16[32,24,128]{2,1,0:T(8,128)(2,1)}), bf16[32,24,128]{2,1,0:T(8,128)(2,1)S(1)}, u32[]{:S(2)}, u32[]{:S(2)}) async-start(bf16[32,24,128]{2,1,0:T(8,128)(2,1)} %get-tuple-element.27), calls=%async_computation | async-start | bytes 393216 | tf_op jit(solution)/shard_map/all_to_all | solution.py:465
  34.3 0.0 copy-start.7
  34.3 0.6 copy-done.7
  35.0 0.6 dynamic_slice.6
  37.5 0.0 copy-done
  37.5 6.9 %all-to-all-done.rays = bf16[32,24,128]{2,1,0:T(8,128)(2,1)S(1)} async-done(((bf16[32,24,128]{2,1,0:T(8,128)(2,1)}), bf16[32,24,128]{2,1,0:T(8,128)(2,1)S(1)}, u32[]{:S(2)}, u32[]{:S(2)}) %all-to-all-start) | async-done | bytes 196640 | tf_op jit(solution)/shard_map/all_to_all | solution.py:465
  44.4 0.1 shard_map.114
  44.5 12.7 %all_to_all.25.rays = bf16[32,8,128]{2,1,0:T(8,128)(2,1)S(1)} all-to-all(bf16[32,8,128]{2,1,0:T(8,128)(2,1)S(1)} %shard_map.114), channel_id=1, replica_groups=mesh['depth'=16,'plane'=32] {'plane'}, dimensions={0} | all-to-all | bytes 131072 | tf_op jit(solution)/shard_map/all_to_all | solution.py:465
  57.2 1.1 shard_map.115
  58.3 3.2 %shard_map.116 = (f32[4,4,128]{2,1,0:T(4,128)S(1)}, bf16[16,32,128]{2,1,0:T(8,128)(2,1)S(1)}) custom-call(s32[2]{0:T(128)S(1)} %pad_add_fusion.pos, bf16[12,4,128]{2,1,0:T(4,128)(2,1)S(1)} %get-tuple-element.28.slab, f32[4,4,128]{2,1,0:T(4,128)S(1)} %get-tuple-element.29.own, bf16[24,576]{1,0:T(8,128)(2,1)S(1)} %get-tuple-element.30.first, ...), custom_call_target="tpu_custom_call" | custom-call | tf_op jit(solution)/shard_map/pallas_call | solution.py:447
  61.5 23.0 %all_to_all.26.slots = bf16[16,32,128]{2,1,0:T(8,128)(2,1)S(1)} all-to-all(bf16[16,32,128]{2,1,0:T(8,128)(2,1)S(1)} %get-tuple-element.38), channel_id=1, replica_groups=mesh['depth'=16,'plane'=32] {'depth'}, dimensions={0} | all-to-all | bytes 262144 | tf_op jit(solution)/shard_map/all_to_all | solution.py:465
  84.5 13.9 %all_to_all.27 = bf16[32,16,128]{2,1,0:T(8,128)(2,1)S(1)} all-to-all(bf16[32,16,128]{2,1,0:T(8,128)(2,1)S(1)} %broadcast_in_dim.4), channel_id=1, replica_groups=mesh['depth'=16,'plane'=32] {'plane'}, dimensions={0} | all-to-all | bytes 262144 | tf_op jit(solution)/shard_map/all_to_all | solution.py:465
  98.5 11.7 %all_to_all.28.sums = bf16[16,16,128]{2,1,0:T(8,128)(2,1)S(1)} all-to-all(bf16[16,16,128]{2,1,0:T(8,128)(2,1)S(1)} %broadcast_in_dim.5), channel_id=1, replica_groups=mesh['depth'=16,'plane'=32] {'depth'}, dimensions={0} | all-to-all | bytes 131072 | tf_op jit(solution)/shard_map/all_to_all | solution.py:465
  110.2 1.5 %shard_map.117 = (f32[4,4,128]{2,1,0:T(4,128)}, f32[27,32]{1,0:T(8,128)}, f32[27,32,32]{2,1,0:T(8,128)}, f32[27,32]{1,0:T(8,128)}) custom-call(s32[2]{0:T(128)S(1)} %pad_add_fusion.pos, bf16[16,16,128]{2,1,0:T(8,128)(2,1)S(1)} %all_to_all.28.sums, bf16[16,32,128]{2,1,0:T(8,128)(2,1)S(1)} %all_to_all.26.slots, f32[4,4,128]{2,1,0:T(4,128)S(1)} %get-tuple-element.39.volume), custom_call_target="tpu_custom_call" | custom-call | tf_op jit(solution)/shard_map/pallas_call | solution.py:447
  (5 shorter events, 0.1 us)
Async XLA Ops:
  0.6 36.9 %copy-start = (f32[4,32,1024]{2,1,0:T(8,128)S(1)}, f32[4,32,1024]{2,1,0:T(8,128)}, u32[]{:S(2)}) copy-start(f32[4,32,1024]{2,1,0:T(8,128)} %param.13) | copy-start | bytes 1572868
  0.6 11.3 %collective-permute-start = (bf16[4,4,128]{2,1,0:T(4,128)(2,1)}, bf16[4,4,128]{2,1,0:T(4,128)(2,1)S(1)}, u32[]{:S(2)}, u32[]{:S(2)}) collective-permute-start(bf16[4,4,128]{2,1,0:T(4,128)(2,1)} %own.1), channel_id=1, source_target_pairs={{0,32},{32,0},{64,96},{96,64},{128,160},{160,128},{192,224},{224,1... | collective-permute-start | bytes 12296 | tf_op jit(solution)/shard_map/ppermute | solution.py:461
  7.4 4.5 %collective-permute-start.1 = (bf16[4,4,128]{2,1,0:T(4,128)(2,1)}, bf16[4,4,128]{2,1,0:T(4,128)(2,1)S(1)}, u32[]{:S(2)}, u32[]{:S(2)}) collective-permute-start(bf16[4,4,128]{2,1,0:T(4,128)(2,1)} %own.1), channel_id=1, source_target_pairs={{32,64},{64,32},{96,128},{128,96},{160,192},{192,160},{224,256},{2... | collective-permute-start | bytes 12296 | tf_op jit(solution)/shard_map/ppermute | solution.py:461
  8.1 0.7 copy-start.4
  8.1 0.7 copy-start.2
  8.8 0.9 copy-start.1
  9.7 0.7 copy-start.3
  10.5 0.7 copy-start.5
  11.2 0.8 copy-start.6
  12.5 6.1 %collective-permute-start.2 = (bf16[36,4,128]{2,1,0:T(4,128)(2,1)S(1)}, bf16[36,4,128]{2,1,0:T(4,128)(2,1)S(1)}, u32[]{:S(2)}, u32[]{:S(2)}) collective-permute-start(bf16[36,4,128]{2,1,0:T(4,128)(2,1)S(1)} %shard_map.112.mid), channel_id=1, source_target_pairs={{0,1},{1,0},{2,3},{3,2},{4,5},{5,4},{6,7},{7,6},{8,9},{9,8},{10,11... | collective-permute-start | bytes 110600 | tf_op jit(solution)/shard_map/ppermute | solution.py:461
  16.7 5.3 %collective-permute-start.3 = (bf16[36,4,128]{2,1,0:T(4,128)(2,1)S(1)}, bf16[36,4,128]{2,1,0:T(4,128)(2,1)S(1)}, u32[]{:S(2)}, u32[]{:S(2)}) collective-permute-start(bf16[36,4,128]{2,1,0:T(4,128)(2,1)S(1)} %shard_map.112.mid), channel_id=1, source_target_pairs={{1,2},{2,1},{3,4},{4,3},{5,6},{6,5},{7,8},{8,7},{9,10},{10,9},{11,... | collective-permute-start | bytes 110600 | tf_op jit(solution)/shard_map/ppermute | solution.py:461
  25.3 19.1 %all-to-all-start = ((bf16[32,24,128]{2,1,0:T(8,128)(2,1)}), bf16[32,24,128]{2,1,0:T(8,128)(2,1)S(1)}, u32[]{:S(2)}, u32[]{:S(2)}) async-start(bf16[32,24,128]{2,1,0:T(8,128)(2,1)} %get-tuple-element.27), calls=%async_computation | async-start | bytes 393216 | tf_op jit(solution)/shard_map/all_to_all | solution.py:465
  34.3 0.7 copy-start.7

commit v7 on v6

--- a/solution.py
+++ b/solution.py
@@ -293,7 +293,8 @@
         rows = rays[a * Z : (a + 1) * Z].astype(F32).reshape(Z * HI, 128).astype(BF16)
         highs = [packs[h // H][8 + a, h % H : h % H + 1, :] for h in spans]
         lows = [packs[h // H][16 + a, h % H : h % H + 1, :] for h in spans]
-        spread = dot(rows, jnp.concatenate([low_match(b) for b in lows], axis=1))
+        low = jnp.concatenate([low_match(b) for b in lows], axis=1)
+        spread = dot(rows, low)
         for i, b in enumerate(highs):
             match = jnp.concatenate([b == at] * Z, axis=0)
             term = jnp.where(match, spread[:, i * W : (i + 1) * W], 0.0)
@@ -414,7 +415,7 @@
         terms_out[pos[0] + 1, chunk : chunk + 16, :] = side[1].astype(BF16)
 
 
-def unpack_kernel(scale, count, pos, sums, slots, volume, volume_out, in_out, mid_out, out_out):
+def volume_kernel(count, pos, slots, volume, volume_out):
     before = near_slot(pos, count, slots, -1)[256 // count :]
     after = near_slot(pos, count, slots, 1)[256 // count :]
     for z in range(Z):
@@ -424,6 +425,9 @@
         if z > 0:
             rows = rows + after[(z - 1) * H : z * H]
         volume_out[z] = rows
+
+
+def unpack_kernel(scale, sums, in_out, mid_out, out_out):
     full = sums[...].astype(F32).reshape(256, 128) * scale
     quarters = [full] + [pltpu.roll(full, 128 - 32 * j, 1) for j in range(1, 4)]
     last = jnp.concatenate([q[192:216, 0:C] for q in quarters], axis=0)
@@ -556,11 +560,14 @@
     sums = scatter_to(spread_sum(slots, planes), PLANE)
     sums = scatter_to(spread_sum(sums, depths), DEPTH)
     cell_count = Z * depths * H * planes * W
-    grad_volume, got_in, got_mid, got_out = call(
-        functools.partial(unpack_kernel, float(cell_count) ** (-0.5), depths),
-        [((Z, H, W), F32), ((27, C), F32), ((27, C, C), F32), ((27, C), F32)],
+    grad_volume = call(
+        functools.partial(volume_kernel, depths), [((Z, H, W), F32)], [], pos, slots, partial
+    )[0]
+    got_in, got_mid, got_out = call(
+        functools.partial(unpack_kernel, float(cell_count) ** (-0.5)),
+        [((27, C), F32), ((27, C, C), F32), ((27, C), F32)],
         [],
-        pos, sums, slots, partial,
+        sums,
     )
     return (grad_volume, got_in, got_mid, got_out)
 

time: 113 us -> 114 us (level)
  blocking collectives: 61.3 us -> 49.6 us
  waiting for transfers between devices: 10.2 us -> 18.1 us
  starting transfers between devices: 22.5 us -> 26 us
    all_to_all x4 -> x3, blocking collectives: 61.3 us -> 49.6 us  [scatter_to(): return lax.all_to_all(cells, axis, 0, 0, tiled=True)]
    all_to_all x1 -> x2, waiting for transfers between devices: 6.87 us -> 14.8 us  [scatter_to(): return lax.all_to_all(cells, axis, 0, 0, tiled=True)]
    all_to_all x1 -> x2, starting transfers between devices: 8.95 us -> 12.5 us  [scatter_to(): return lax.all_to_all(cells, axis, 0, 0, tiled=True)]
    pallas_call x7 -> x8, Pallas kernels: 10.5 us -> 11.1 us  [call(): pl.pallas_call(kernel, out_shape=[jax.ShapeDtypeStruct(s, d) for s, d in...]
  transfers between devices with their start and end apart: 5 -> 6, of which waited for: 2 -> 3; matrix products, arithmetic and copies ran while one was open for 1% -> 1% of each run, Pallas kernels for 1% -> 2%
where the time goes in v7:
time: 114 us; the launch traced here: 113 us
  blocking collectives  49.6 us (44%)
  starting transfers between devices  26 us (23%)
  waiting for transfers between devices  18.1 us (16%)
  Pallas kernels  11.1 us (10%)
  local copies, waits for them, and re-layouts  4.89 us (4%)
  between operations  2.77 us (2%)
    all_to_all x3, blocking collectives, scatter_to(): return lax.all_to_all(cells, axis, 0, 0, tiled=True)  49.6 us
    all_to_all x2, waiting for transfers between devices, scatter_to(): return lax.all_to_all(cells, axis, 0, 0, tiled=True)  14.8 us
    ppermute x4, starting transfers between devices, swaps(): return (lax.ppermute(cells, axis, first), lax.ppermute(cells, axis, second))  13.5 us
    all_to_all x2, starting transfers between devices, scatter_to(): return lax.all_to_all(cells, axis, 0, 0, tiled=True)  12.5 us
    pallas_call x8, Pallas kernels, call(): pl.pallas_call(kernel, out_shape=[jax.ShapeDtypeStruct(s, d) for s, d in...  11.1 us
    unnamed x16, local copies, waits for them, and re-layouts  3.63 us
    ppermute x4, waiting for transfers between devices, swaps(): return (lax.ppermute(cells, axis, first), lax.ppermute(cells, axis, second))  3.35 us
  transfers between devices with their start and end apart: 6, of which 3 were waited for; matrix products, arithmetic and copies ran while one was open for 1% of the time, Pallas kernels for 2%

profile of v7, /device:TPU:1, one launch (start us, length us, event | category | flops | bytes accessed | tf_op | source)
XLA Modules:
  0.0 112.6 jit_solution(18317251598180988715)
XLA Ops:
  0.6 0.0 copy-start
  0.6 6.8 %collective-permute-start = (bf16[4,4,128]{2,1,0:T(4,128)(2,1)}, bf16[4,4,128]{2,1,0:T(4,128)(2,1)S(1)}, u32[]{:S(2)}, u32[]{:S(2)}) collective-permute-start(bf16[4,4,128]{2,1,0:T(4,128)(2,1)} %own.1), channel_id=1, source_target_pairs={{0,32},{32,0},{64,96},{96,64},{128,160},{160,128},{192,224},{224,1... | collective-permute-start | bytes 12296 | tf_op jit(solution)/shard_map/ppermute | solution.py:465
  7.4 0.7 collective-permute-start.1
  8.1 0.0 copy-start.4
  8.1 0.0 copy-start.2
  8.1 0.1 pad_add_fusion.pos
  8.2 0.6 copy-done.4
  8.8 0.0 copy-done.2
  8.8 0.0 copy-start.1
  8.8 0.9 copy-done.1
  9.7 0.0 copy-start.3
  9.7 0.7 copy-done.3
  10.5 0.0 copy-start.5
  10.5 0.7 copy-done.5
  11.2 0.0 copy-start.6
  11.2 0.8 shard_map.111
  11.9 0.0 collective-permute-done.first
  11.9 0.0 collective-permute-done.1.second
  11.9 0.0 copy-done.6
  11.9 0.6 shard_map.112.mid
  12.5 4.2 %collective-permute-start.2 = (bf16[36,4,128]{2,1,0:T(4,128)(2,1)S(1)}, bf16[36,4,128]{2,1,0:T(4,128)(2,1)S(1)}, u32[]{:S(2)}, u32[]{:S(2)}) collective-permute-start(bf16[36,4,128]{2,1,0:T(4,128)(2,1)S(1)} %shard_map.112.mid), channel_id=1, source_target_pairs={{0,1},{1,0},{2,3},{3,2},{4,5},{5,4},{6,7},{7,6},{8,9},{9,8},{10,11... | collective-permute-start | bytes 110600 | tf_op jit(solution)/shard_map/ppermute | solution.py:465
  16.7 1.9 %collective-permute-start.3 = (bf16[36,4,128]{2,1,0:T(4,128)(2,1)S(1)}, bf16[36,4,128]{2,1,0:T(4,128)(2,1)S(1)}, u32[]{:S(2)}, u32[]{:S(2)}) collective-permute-start(bf16[36,4,128]{2,1,0:T(4,128)(2,1)S(1)} %shard_map.112.mid), channel_id=1, source_target_pairs={{1,2},{2,1},{3,4},{4,3},{5,6},{6,5},{7,8},{8,7},{9,10},{10,9},{11,... | collective-permute-start | bytes 110600 | tf_op jit(solution)/shard_map/ppermute | solution.py:465
  18.6 0.0 collective-permute-done.2.swap_a
  18.6 3.3 %collective-permute-done.3.swap_b = bf16[36,4,128]{2,1,0:T(4,128)(2,1)S(1)} collective-permute-done((bf16[36,4,128]{2,1,0:T(4,128)(2,1)S(1)}, bf16[36,4,128]{2,1,0:T(4,128)(2,1)S(1)}, u32[]{:S(2)}, u32[]{:S(2)}) %collective-permute-start.3) | collective-permute-done | bytes 36896 | tf_op jit(solution)/shard_map/ppermute | solution.py:465
  22.0 3.3 %shard_map.113 = (bf16[32,16,128]{2,1,0:T(8,128)(2,1)S(1)}, bf16[8,192,128]{2,1,0:T(8,128)(2,1)S(1)}, f32[8,192,128]{2,1,0:T(8,128)S(1)}, bf16[6,192,128]{2,1,0:...) custom-call(s32[2]{0:T(128)S(1)} %pad_add_fusion.pos, ...), custom_call_target="tpu_custom_call" | custom-call | tf_op jit(solution)/shard_map/pallas_call | solution.py:451
  25.3 8.9 %all-to-all-start = ((bf16[32,24,128]{2,1,0:T(8,128)(2,1)}), bf16[32,24,128]{2,1,0:T(8,128)(2,1)S(1)}, u32[]{:S(2)}, u32[]{:S(2)}) async-start(bf16[32,24,128]{2,1,0:T(8,128)(2,1)} %get-tuple-element.30), calls=%async_computation | async-start | bytes 393216 | tf_op jit(solution)/shard_map/all_to_all | solution.py:469
  34.3 0.0 copy-start.7
  34.3 0.6 copy-done.7
  35.0 0.6 dynamic_slice.6
  37.5 0.0 copy-done
  37.5 6.9 %all-to-all-done.rays = bf16[32,24,128]{2,1,0:T(8,128)(2,1)S(1)} async-done(((bf16[32,24,128]{2,1,0:T(8,128)(2,1)}), bf16[32,24,128]{2,1,0:T(8,128)(2,1)S(1)}, u32[]{:S(2)}, u32[]{:S(2)}) %all-to-all-start) | async-done | bytes 196640 | tf_op jit(solution)/shard_map/all_to_all | solution.py:469
  44.4 0.1 shard_map.114
  44.5 12.7 %all_to_all.25.rays = bf16[32,8,128]{2,1,0:T(8,128)(2,1)S(1)} all-to-all(bf16[32,8,128]{2,1,0:T(8,128)(2,1)S(1)} %shard_map.114), channel_id=1, replica_groups=mesh['depth'=16,'plane'=32] {'plane'}, dimensions={0} | all-to-all | bytes 131072 | tf_op jit(solution)/shard_map/all_to_all | solution.py:469
  57.2 1.1 shard_map.115
  58.3 3.2 %shard_map.116 = (f32[4,4,128]{2,1,0:T(4,128)S(1)}, bf16[16,32,128]{2,1,0:T(8,128)(2,1)S(1)}) custom-call(s32[2]{0:T(128)S(1)} %pad_add_fusion.pos, bf16[12,4,128]{2,1,0:T(4,128)(2,1)S(1)} %get-tuple-element.31.slab, f32[4,4,128]{2,1,0:T(4,128)S(1)} %get-tuple-element.32.own, bf16[24,576]{1,0:T(8,128)(2,1)S(1)} %get-tuple-element.33.first, ...), custom_call_target="tpu_custom_call" | custom-call | tf_op jit(solution)/shard_map/pallas_call | solution.py:451
  61.5 23.0 %all_to_all.26.slots = bf16[16,32,128]{2,1,0:T(8,128)(2,1)S(1)} all-to-all(bf16[16,32,128]{2,1,0:T(8,128)(2,1)S(1)} %get-tuple-element.41), channel_id=1, replica_groups=mesh['depth'=16,'plane'=32] {'depth'}, dimensions={0} | all-to-all | bytes 262144 | tf_op jit(solution)/shard_map/all_to_all | solution.py:469
  84.5 13.9 %all_to_all.27 = bf16[32,16,128]{2,1,0:T(8,128)(2,1)S(1)} all-to-all(bf16[32,16,128]{2,1,0:T(8,128)(2,1)S(1)} %broadcast_in_dim.4), channel_id=1, replica_groups=mesh['depth'=16,'plane'=32] {'plane'}, dimensions={0} | all-to-all | bytes 262144 | tf_op jit(solution)/shard_map/all_to_all | solution.py:469
  98.4 0.6 broadcast_in_dim.5
  99.1 3.5 %all-to-all-start.4 = ((bf16[16,16,128]{2,1,0:T(8,128)(2,1)}), bf16[16,16,128]{2,1,0:T(8,128)(2,1)S(1)}, u32[]{:S(2)}, u32[]{:S(2)}) async-start(bf16[16,16,128]{2,1,0:T(8,128)(2,1)} %broadcast_in_dim.5), calls=%async_computation.4 | async-start | bytes 131072 | tf_op jit(solution)/shard_map/all_to_all | solution.py:469
  102.6 1.2 %shard_map.117 = f32[4,4,128]{2,1,0:T(4,128)} custom-call(s32[2]{0:T(128)S(1)} %pad_add_fusion.pos, bf16[16,32,128]{2,1,0:T(8,128)(2,1)S(1)} %all_to_all.26.slots, f32[4,4,128]{2,1,0:T(4,128)S(1)} %get-tuple-element.42.volume), custom_call_target="tpu_custom_call" | custom-call | tf_op jit(solution)/shard_map/pallas_call | solution.py:451
  103.8 7.9 %all-to-all-done.4.sums = bf16[16,16,128]{2,1,0:T(8,128)(2,1)S(1)} async-done(((bf16[16,16,128]{2,1,0:T(8,128)(2,1)}), bf16[16,16,128]{2,1,0:T(8,128)(2,1)S(1)}, u32[]{:S(2)}, u32[]{:S(2)}) %all-to-all-start.4) | async-done | bytes 65568 | tf_op jit(solution)/shard_map/all_to_all | solution.py:469
  111.7 0.9 shard_map.118
  (4 shorter events, 0.1 us)
Async XLA Ops:
  0.6 36.9 %copy-start = (f32[4,32,1024]{2,1,0:T(8,128)S(1)}, f32[4,32,1024]{2,1,0:T(8,128)}, u32[]{:S(2)}) copy-start(f32[4,32,1024]{2,1,0:T(8,128)} %param.13) | copy-start | bytes 1572868
  0.6 11.3 %collective-permute-start = (bf16[4,4,128]{2,1,0:T(4,128)(2,1)}, bf16[4,4,128]{2,1,0:T(4,128)(2,1)S(1)}, u32[]{:S(2)}, u32[]{:S(2)}) collective-permute-start(bf16[4,4,128]{2,1,0:T(4,128)(2,1)} %own.1), channel_id=1, source_target_pairs={{0,32},{32,0},{64,96},{96,64},{128,160},{160,128},{192,224},{224,1... | collective-permute-start | bytes 12296 | tf_op jit(solution)/shard_map/ppermute | solution.py:465
  7.4 4.5 %collective-permute-start.1 = (bf16[4,4,128]{2,1,0:T(4,128)(2,1)}, bf16[4,4,128]{2,1,0:T(4,128)(2,1)S(1)}, u32[]{:S(2)}, u32[]{:S(2)}) collective-permute-start(bf16[4,4,128]{2,1,0:T(4,128)(2,1)} %own.1), channel_id=1, source_target_pairs={{32,64},{64,32},{96,128},{128,96},{160,192},{192,160},{224,256},{2... | collective-permute-start | bytes 12296 | tf_op jit(solution)/shard_map/ppermute | solution.py:465
  8.1 0.7 copy-start.4
  8.1 0.7 copy-start.2
  8.8 0.9 copy-start.1
  9.7 0.7 copy-start.3
  10.5 0.7 copy-start.5
  11.2 0.8 copy-start.6
  12.5 6.1 %collective-permute-start.2 = (bf16[36,4,128]{2,1,0:T(4,128)(2,1)S(1)}, bf16[36,4,128]{2,1,0:T(4,128)(2,1)S(1)}, u32[]{:S(2)}, u32[]{:S(2)}) collective-permute-start(bf16[36,4,128]{2,1,0:T(4,128)(2,1)S(1)} %shard_map.112.mid), channel_id=1, source_target_pairs={{0,1},{1,0},{2,3},{3,2},{4,5},{5,4},{6,7},{7,6},{8,9},{9,8},{10,11... | collective-permute-start | bytes 110600 | tf_op jit(solution)/shard_map/ppermute | solution.py:465
  16.7 5.3 %collective-permute-start.3 = (bf16[36,4,128]{2,1,0:T(4,128)(2,1)S(1)}, bf16[36,4,128]{2,1,0:T(4,128)(2,1)S(1)}, u32[]{:S(2)}, u32[]{:S(2)}) collective-permute-start(bf16[36,4,128]{2,1,0:T(4,128)(2,1)S(1)} %shard_map.112.mid), channel_id=1, source_target_pairs={{1,2},{2,1},{3,4},{4,3},{5,6},{6,5},{7,8},{8,7},{9,10},{10,9},{11,... | collective-permute-start | bytes 110600 | tf_op jit(solution)/shard_map/ppermute | solution.py:465
  25.3 19.1 %all-to-all-start = ((bf16[32,24,128]{2,1,0:T(8,128)(2,1)}), bf16[32,24,128]{2,1,0:T(8,128)(2,1)S(1)}, u32[]{:S(2)}, u32[]{:S(2)}) async-start(bf16[32,24,128]{2,1,0:T(8,128)(2,1)} %get-tuple-element.30), calls=%async_computation | async-start | bytes 393216 | tf_op jit(solution)/shard_map/all_to_all | solution.py:469
  34.3 0.7 copy-start.7
  99.1 12.6 %all-to-all-start.4 = ((bf16[16,16,128]{2,1,0:T(8,128)(2,1)}), bf16[16,16,128]{2,1,0:T(8,128)(2,1)S(1)}, u32[]{:S(2)}, u32[]{:S(2)}) async-start(bf16[16,16,128]{2,1,0:T(8,128)(2,1)} %broadcast_in_dim.5), calls=%async_computation.4 | async-start | bytes 131072 | tf_op jit(solution)/shard_map/all_to_all | solution.py:469

commit v8 on v6

--- a/solution.py
+++ b/solution.py
@@ -209,7 +209,7 @@
     out[12:36] = local[...]
 
 
-def forward_kernel(depth_count, plane_count, pos, swap_a, swap_b, mid, lows, first, second, third,
+def forward_kernel(depth_count, plane_count, pos, swap_b, swap_a, mid, lows, first, second, third,
                    vc_out, act1_out, slope1_out, act2_out, slope2_out, rays_out,
                    vs, v3, vcs, a1, a2):
     depth_at = pos[0] * Z
@@ -281,7 +281,7 @@
         out[:, t * HI : (t + 1) * HI, :] = weighted.astype(BF16)
 
 
-def back_kernel(plane_count, pos, rays, swap_a, swap_b, mid, cot, slab_out, own_out, slab):
+def back_kernel(plane_count, pos, rays, swap_b, swap_a, mid, cot, slab_out, own_out, slab):
     plane_at = pos[1] * H
     nh = plane_count * H
     lo, hi = in_order(pos[1], swap_a[12:36].astype(F32), swap_b[12:36].astype(F32))
@@ -458,7 +458,8 @@
     count = lax.axis_size(axis)
     first = [(i, i ^ 1) for i in range(count)]
     second = [(i, i + 1 if i % 2 else i - 1) for i in range(1, count - 1)]
-    return lax.ppermute(cells, axis, first), lax.ppermute(cells, axis, second)
+    after = lax.ppermute(cells, axis, second)
+    return lax.ppermute(cells, axis, first), after
 
 
 def scatter_to(cells, axis):
@@ -506,7 +507,7 @@
             ((8, 10 * C, W), BF16),
             ((6, 6 * C, W), BF16),
         ],
-        pos, p_first, p_second, pack, lows, first, wide, last,
+        pos, p_second, p_first, pack, lows, first, wide, last,
     )
     each = TILES // planes
     gathered = scatter_to(rays.reshape(planes, each * 3 * HI, 128), PLANE)
@@ -528,7 +529,7 @@
         functools.partial(back_kernel, planes),
         [((12, Z, W), BF16), ((H, Z, W), F32)],
         [((12, Z, W), F32)],
-        pos, weighted, p_first, p_second, pack, cotangent,
+        pos, weighted, p_second, p_first, pack, cotangent,
     )
     partial, terms = call(
         functools.partial(backward_kernel, depths, planes),

time: 113 us -> 111 us (0.982)
  waiting for transfers between devices: 10.2 us -> 8.05 us
    ppermute x4, waiting for transfers between devices: 3.35 us -> 1.18 us  [the longest x2 1.17 us: swaps(): return (lax.ppermute(cells, axis, first), after)]
where the time goes in v8:
time: 111 us; the launch traced here: 110 us
  blocking collectives  61.2 us (55%)
  starting transfers between devices  22.7 us (20%)
  Pallas kernels  10.5 us (9%)
  waiting for transfers between devices  8.05 us (7%)
  local copies, waits for them, and re-layouts  4.26 us (4%)
  between operations  2.77 us (2%)
    all_to_all x4, blocking collectives, scatter_to(): return lax.all_to_all(cells, axis, 0, 0, tiled=True)  61.2 us
    pallas_call x7, Pallas kernels, call(): pl.pallas_call(kernel, out_shape=[jax.ShapeDtypeStruct(s, d) for s, d in...  10.5 us
    all_to_all x1, starting transfers between devices, scatter_to(): return lax.all_to_all(cells, axis, 0, 0, tiled=True)  9.35 us
    ppermute x2, starting transfers between devices, swaps(): return (lax.ppermute(cells, axis, first), after)  8.68 us
    all_to_all x1, waiting for transfers between devices, scatter_to(): return lax.all_to_all(cells, axis, 0, 0, tiled=True)  6.87 us
    ppermute x2, starting transfers between devices, swaps(): after = lax.ppermute(cells, axis, second)  4.71 us
    unnamed x16, local copies, waits for them, and re-layouts  3.63 us
  transfers between devices with their start and end apart: 5, of which 2 were waited for; matrix products, arithmetic and copies ran while one was open for 1% of the time, Pallas kernels for 1%

profile of v8, /device:TPU:1, one launch (start us, length us, event | category | flops | bytes accessed | tf_op | source)
XLA Modules:
  0.0 109.7 jit_solution(14566732135301270897)
XLA Ops:
  0.6 0.0 copy-start
  0.6 6.8 %collective-permute-start = (bf16[4,4,128]{2,1,0:T(4,128)(2,1)}, bf16[4,4,128]{2,1,0:T(4,128)(2,1)S(1)}, u32[]{:S(2)}, u32[]{:S(2)}) collective-permute-start(bf16[4,4,128]{2,1,0:T(4,128)(2,1)} %own.1), channel_id=1, source_target_pairs={{0,32},{32,0},{64,96},{96,64},{128,160},{160,128},{192,224},{224,1... | collective-permute-start | bytes 12296 | tf_op jit(solution)/shard_map/ppermute | solution.py:462
  7.4 0.7 collective-permute-start.1
  8.1 0.0 copy-start.4
  8.1 0.0 copy-start.2
  8.1 0.1 pad_add_fusion.pos
  8.2 0.6 copy-done.4
  8.8 0.0 copy-done.2
  8.8 0.0 copy-start.1
  8.8 0.9 copy-done.1
  9.7 0.0 copy-start.3
  9.7 0.7 copy-done.3
  10.5 0.0 copy-start.5
  10.5 0.7 copy-done.5
  11.2 0.0 copy-start.6
  11.2 0.8 shard_map.111
  11.9 0.0 collective-permute-done.first
  11.9 0.0 collective-permute-done.1.second
  11.9 0.0 copy-done.6
  11.9 0.6 shard_map.112.mid
  12.5 4.0 %collective-permute-start.2 = (bf16[36,4,128]{2,1,0:T(4,128)(2,1)S(1)}, bf16[36,4,128]{2,1,0:T(4,128)(2,1)S(1)}, u32[]{:S(2)}, u32[]{:S(2)}) collective-permute-start(bf16[36,4,128]{2,1,0:T(4,128)(2,1)S(1)} %shard_map.112.mid), channel_id=1, source_target_pairs={{1,2},{2,1},{3,4},{4,3},{5,6},{6,5},{7,8},{8,7},{9,10},{10,9},{11,... | collective-permute-start | bytes 110600 | tf_op jit(solution)/shard_map/ppermute | solution.py:461
  16.6 1.9 %collective-permute-start.3 = (bf16[36,4,128]{2,1,0:T(4,128)(2,1)S(1)}, bf16[36,4,128]{2,1,0:T(4,128)(2,1)S(1)}, u32[]{:S(2)}, u32[]{:S(2)}) collective-permute-start(bf16[36,4,128]{2,1,0:T(4,128)(2,1)S(1)} %shard_map.112.mid), channel_id=1, source_target_pairs={{0,1},{1,0},{2,3},{3,2},{4,5},{5,4},{6,7},{7,6},{8,9},{9,8},{10,11... | collective-permute-start | bytes 110600 | tf_op jit(solution)/shard_map/ppermute | solution.py:462
  18.5 0.0 collective-permute-done.2.swap_b
  18.5 1.2 %collective-permute-done.3.swap_a = bf16[36,4,128]{2,1,0:T(4,128)(2,1)S(1)} collective-permute-done((bf16[36,4,128]{2,1,0:T(4,128)(2,1)S(1)}, bf16[36,4,128]{2,1,0:T(4,128)(2,1)S(1)}, u32[]{:S(2)}, u32[]{:S(2)}) %collective-permute-start.3) | collective-permute-done | bytes 36896 | tf_op jit(solution)/shard_map/ppermute | solution.py:462
  19.7 3.3 %shard_map.113 = (bf16[32,16,128]{2,1,0:T(8,128)(2,1)S(1)}, bf16[8,192,128]{2,1,0:T(8,128)(2,1)S(1)}, f32[8,192,128]{2,1,0:T(8,128)S(1)}, bf16[6,192,128]{2,1,0:...) custom-call(s32[2]{0:T(128)S(1)} %pad_add_fusion.pos, ...), custom_call_target="tpu_custom_call" | custom-call | tf_op jit(solution)/shard_map/pallas_call | solution.py:447
  23.0 9.4 %all-to-all-start = ((bf16[32,24,128]{2,1,0:T(8,128)(2,1)}), bf16[32,24,128]{2,1,0:T(8,128)(2,1)S(1)}, u32[]{:S(2)}, u32[]{:S(2)}) async-start(bf16[32,24,128]{2,1,0:T(8,128)(2,1)} %get-tuple-element.27), calls=%async_computation | async-start | bytes 393216 | tf_op jit(solution)/shard_map/all_to_all | solution.py:466
  32.4 0.0 copy-start.7
  32.4 0.6 copy-done.7
  33.0 0.6 dynamic_slice.6
  35.6 0.0 copy-done
  35.6 6.9 %all-to-all-done.rays = bf16[32,24,128]{2,1,0:T(8,128)(2,1)S(1)} async-done(((bf16[32,24,128]{2,1,0:T(8,128)(2,1)}), bf16[32,24,128]{2,1,0:T(8,128)(2,1)S(1)}, u32[]{:S(2)}, u32[]{:S(2)}) %all-to-all-start) | async-done | bytes 196640 | tf_op jit(solution)/shard_map/all_to_all | solution.py:466
  42.5 0.1 shard_map.114
  42.5 12.7 %all_to_all.25.rays = bf16[32,8,128]{2,1,0:T(8,128)(2,1)S(1)} all-to-all(bf16[32,8,128]{2,1,0:T(8,128)(2,1)S(1)} %shard_map.114), channel_id=1, replica_groups=mesh['depth'=16,'plane'=32] {'plane'}, dimensions={0} | all-to-all | bytes 131072 | tf_op jit(solution)/shard_map/all_to_all | solution.py:466
  55.2 1.1 %shard_map.115 = (bf16[12,4,128]{2,1,0:T(4,128)(2,1)S(1)}, f32[4,4,128]{2,1,0:T(4,128)S(1)}) custom-call(s32[2]{0:T(128)S(1)} %pad_add_fusion.pos, bf16[32,8,128]{2,1,0:T(8,128)(2,1)S(1)} %all_to_all.25.rays, bf16[36,4,128]{2,1,0:T(4,128)(2,1)S(1)} %collective-permute-done.2.swap_b, bf16[36,4,128]{2,1,0:T(4,128)(2,1)S(1)} %collective-permute-done.3.swap_a, ...), custom_call_target="tpu_custom_call" | custom-call | tf_op jit(solution)/shard_map/pallas_call | solution.py:447
  56.3 3.2 %shard_map.116 = (f32[4,4,128]{2,1,0:T(4,128)S(1)}, bf16[16,32,128]{2,1,0:T(8,128)(2,1)S(1)}) custom-call(s32[2]{0:T(128)S(1)} %pad_add_fusion.pos, bf16[12,4,128]{2,1,0:T(4,128)(2,1)S(1)} %get-tuple-element.28.slab, f32[4,4,128]{2,1,0:T(4,128)S(1)} %get-tuple-element.29.own, bf16[24,576]{1,0:T(8,128)(2,1)S(1)} %get-tuple-element.30.first, ...), custom_call_target="tpu_custom_call" | custom-call | tf_op jit(solution)/shard_map/pallas_call | solution.py:447
  59.6 22.6 %all_to_all.26.slots = bf16[16,32,128]{2,1,0:T(8,128)(2,1)S(1)} all-to-all(bf16[16,32,128]{2,1,0:T(8,128)(2,1)S(1)} %get-tuple-element.38), channel_id=1, replica_groups=mesh['depth'=16,'plane'=32] {'depth'}, dimensions={0} | all-to-all | bytes 262144 | tf_op jit(solution)/shard_map/all_to_all | solution.py:466
  82.2 14.2 %all_to_all.27 = bf16[32,16,128]{2,1,0:T(8,128)(2,1)S(1)} all-to-all(bf16[32,16,128]{2,1,0:T(8,128)(2,1)S(1)} %broadcast_in_dim.4), channel_id=1, replica_groups=mesh['depth'=16,'plane'=32] {'plane'}, dimensions={0} | all-to-all | bytes 262144 | tf_op jit(solution)/shard_map/all_to_all | solution.py:466
  96.5 11.7 %all_to_all.28.sums = bf16[16,16,128]{2,1,0:T(8,128)(2,1)S(1)} all-to-all(bf16[16,16,128]{2,1,0:T(8,128)(2,1)S(1)} %broadcast_in_dim.5), channel_id=1, replica_groups=mesh['depth'=16,'plane'=32] {'depth'}, dimensions={0} | all-to-all | bytes 131072 | tf_op jit(solution)/shard_map/all_to_all | solution.py:466
  108.2 1.5 %shard_map.117 = (f32[4,4,128]{2,1,0:T(4,128)}, f32[27,32]{1,0:T(8,128)}, f32[27,32,32]{2,1,0:T(8,128)}, f32[27,32]{1,0:T(8,128)}) custom-call(s32[2]{0:T(128)S(1)} %pad_add_fusion.pos, bf16[16,16,128]{2,1,0:T(8,128)(2,1)S(1)} %all_to_all.28.sums, bf16[16,32,128]{2,1,0:T(8,128)(2,1)S(1)} %all_to_all.26.slots, f32[4,4,128]{2,1,0:T(4,128)S(1)} %get-tuple-element.39.volume), custom_call_target="tpu_custom_call" | custom-call | tf_op jit(solution)/shard_map/pallas_call | solution.py:447
  (5 shorter events, 0.1 us)
Async XLA Ops:
  0.6 35.0 %copy-start = (f32[4,32,1024]{2,1,0:T(8,128)S(1)}, f32[4,32,1024]{2,1,0:T(8,128)}, u32[]{:S(2)}) copy-start(f32[4,32,1024]{2,1,0:T(8,128)} %param.13) | copy-start | bytes 1572868
  0.6 11.3 %collective-permute-start = (bf16[4,4,128]{2,1,0:T(4,128)(2,1)}, bf16[4,4,128]{2,1,0:T(4,128)(2,1)S(1)}, u32[]{:S(2)}, u32[]{:S(2)}) collective-permute-start(bf16[4,4,128]{2,1,0:T(4,128)(2,1)} %own.1), channel_id=1, source_target_pairs={{0,32},{32,0},{64,96},{96,64},{128,160},{160,128},{192,224},{224,1... | collective-permute-start | bytes 12296 | tf_op jit(solution)/shard_map/ppermute | solution.py:462
  7.4 4.5 %collective-permute-start.1 = (bf16[4,4,128]{2,1,0:T(4,128)(2,1)}, bf16[4,4,128]{2,1,0:T(4,128)(2,1)S(1)}, u32[]{:S(2)}, u32[]{:S(2)}) collective-permute-start(bf16[4,4,128]{2,1,0:T(4,128)(2,1)} %own.1), channel_id=1, source_target_pairs={{32,64},{64,32},{96,128},{128,96},{160,192},{192,160},{224,256},{2... | collective-permute-start | bytes 12296 | tf_op jit(solution)/shard_map/ppermute | solution.py:461
  8.1 0.7 copy-start.4
  8.1 0.7 copy-start.2
  8.8 0.9 copy-start.1
  9.7 0.7 copy-start.3
  10.5 0.7 copy-start.5
  11.2 0.8 copy-start.6
  12.5 6.0 %collective-permute-start.2 = (bf16[36,4,128]{2,1,0:T(4,128)(2,1)S(1)}, bf16[36,4,128]{2,1,0:T(4,128)(2,1)S(1)}, u32[]{:S(2)}, u32[]{:S(2)}) collective-permute-start(bf16[36,4,128]{2,1,0:T(4,128)(2,1)S(1)} %shard_map.112.mid), channel_id=1, source_target_pairs={{1,2},{2,1},{3,4},{4,3},{5,6},{6,5},{7,8},{8,7},{9,10},{10,9},{11,... | collective-permute-start | bytes 110600 | tf_op jit(solution)/shard_map/ppermute | solution.py:461
  16.6 3.1 %collective-permute-start.3 = (bf16[36,4,128]{2,1,0:T(4,128)(2,1)S(1)}, bf16[36,4,128]{2,1,0:T(4,128)(2,1)S(1)}, u32[]{:S(2)}, u32[]{:S(2)}) collective-permute-start(bf16[36,4,128]{2,1,0:T(4,128)(2,1)S(1)} %shard_map.112.mid), channel_id=1, source_target_pairs={{0,1},{1,0},{2,3},{3,2},{4,5},{5,4},{6,7},{7,6},{8,9},{9,8},{10,11... | collective-permute-start | bytes 110600 | tf_op jit(solution)/shard_map/ppermute | solution.py:462
  23.0 19.5 %all-to-all-start = ((bf16[32,24,128]{2,1,0:T(8,128)(2,1)}), bf16[32,24,128]{2,1,0:T(8,128)(2,1)S(1)}, u32[]{:S(2)}, u32[]{:S(2)}) async-start(bf16[32,24,128]{2,1,0:T(8,128)(2,1)} %get-tuple-element.27), calls=%async_computation | async-start | bytes 393216 | tf_op jit(solution)/shard_map/all_to_all | solution.py:466
  32.4 0.7 copy-start.7
